TPU v7x, 128 devices: a whole 4x4x4 slice. The times are simulated.
128 devices in a mesh: dp: 16 (over x, y), expert: 8 (over z, core).
Axes of the slice: x: 4, y: 4, z: 4, core: 2. Of those that a mesh axis runs over, the one named last changes fastest.
Arguments:
- context: bfloat16 [8192, 4096], P('dp'), may hold values from -6 to 6
- out_weight: bfloat16 [4096, 4096], P('dp', 'expert'), may hold values from -0.09375 to 0.09375
- residual: bfloat16 [8192, 4096], P('dp', 'expert'), may hold values from -6 to 6
- gate_weight: bfloat16 [8, 4096, 8192], P('expert', None, 'dp'), may hold values from -0.09375 to 0.09375
- up_weight: bfloat16 [8, 4096, 8192], P('expert', None, 'dp'), may hold values from -0.09375 to 0.09375
- down_weight: bfloat16 [8, 8192, 4096], P('expert', 'dp'), may hold values from -0.0625 to 0.0625
- gate_values: float32 [8, 512], P('expert'), may hold values from 0.2 to 1
- chosen_blocks: int32 [8, 4], replicated, may hold values from 0 to 63, as said below
- block_counts: int32 [8], replicated, may hold values from 1 to 4, as said below
Outputs:
- mixed: bfloat16 [8192, 4096], P('dp', 'expert')
Inputs may be any that keep to these rules, and one draw needn't show every extreme that they name: `chosen_blocks`: within one expert the 4 block numbers are distinct; slots from block_counts on are unused but hold valid block numbers. `block_counts`: some expert uses all 4 slots.
All inputs are finite; a program needn't handle non-finite values.
Results may differ from a plain program's by a relative error of at most 0.008.
Values may be sent and summed in bfloat16 or wider, within the bound.
A program may use at most 128 MiB of HBM per device.

v0:
```python
import jax
import jax.numpy as jnp
from jax import lax
from jax.sharding import PartitionSpec as P

BLK = 128
CAP = 4


def spread_2(value, axis, source):
    kept = jnp.where(lax.axis_index(axis) == source, value, 0).astype(value.dtype)
    return lax.psum(kept, axis)


def spread(selected, owners):
    return jnp.stack(
        [spread_2(selected[slot], "dp", owners[slot]) for slot in range(selected.shape[0])]
    )


def expert_block(inputs, w_gate, w_up, down_split, scale):
    gate = jnp.dot(inputs, w_gate, preferred_element_type=jnp.float32)
    upper = jnp.dot(inputs, w_up, preferred_element_type=jnp.float32)
    hidden = (jax.nn.silu(gate) * upper).astype(jnp.bfloat16)
    part = jnp.einsum("rf,fcd->crd", hidden, down_split, preferred_element_type=jnp.float32)
    return (part * scale[None, :, None]).astype(jnp.bfloat16)


def body(
    context,
    out_weight,
    residual,
    gate_weight,
    up_weight,
    down_weight,
    gate_values,
    chosen_blocks,
    block_counts,
):
    n_expert = lax.axis_size("expert")
    local_tokens = context.shape[0]
    local_width = residual.shape[1]
    model_width = context.shape[1]
    local_blocks = local_tokens // BLK
    my_expert = lax.axis_index("expert")
    my_data = lax.axis_index("dp")
    projected = jnp.dot(
        context,
        lax.all_gather(out_weight, "dp", axis=0, tiled=True),
        preferred_element_type=jnp.float32,
    )
    attended = (residual.astype(jnp.float32) + projected).astype(jnp.bfloat16)
    owners = chosen_blocks // local_blocks
    offsets = chosen_blocks % local_blocks
    my_owners = lax.dynamic_index_in_dim(owners, my_expert, 0, keepdims=False)
    my_offsets = lax.dynamic_index_in_dim(offsets, my_expert, 0, keepdims=False)
    whole = lax.all_gather(attended, "expert", axis=1, tiled=True)
    selected = whole.reshape(local_blocks, BLK, model_width)[my_offsets]
    picked = spread(selected, my_owners).reshape(CAP * BLK, model_width)
    w_gate = gate_weight[0]
    w_up = up_weight[0]
    down_split = down_weight[0].reshape(down_weight.shape[1], n_expert, local_width)
    gate_row = gate_values[0]
    my_count = lax.dynamic_index_in_dim(block_counts, my_expert, 0, keepdims=False)
    live = jnp.arange(CAP * BLK) // BLK < my_count
    scale = jnp.where(live, gate_row, jnp.zeros_like(gate_row))
    partial_value = expert_block(picked, w_gate, w_up, down_split, scale)
    received = lax.all_to_all(partial_value, "expert", split_axis=0, concat_axis=0, tiled=True)
    terms = received.reshape(n_expert * CAP * BLK, local_width).astype(jnp.float32)
    expert_out = lax.psum(terms.astype(jnp.bfloat16), "dp")
    expert_out = expert_out.reshape(n_expert * CAP, BLK, local_width)
    flat_owners = owners.reshape(-1)
    flat_offsets = offsets.reshape(-1)
    selector = (flat_owners[None, :] == my_data) & (
        flat_offsets[None, :] == jnp.arange(local_blocks)[:, None]
    )
    added = jnp.einsum(
        "bs,srd->brd", selector.astype(jnp.bfloat16), expert_out, preferred_element_type=jnp.float32
    )
    total = attended.astype(jnp.float32).reshape(local_blocks, BLK, local_width) + added
    return total.reshape(local_tokens, local_width).astype(jnp.bfloat16)


def solution(mesh):
    in_specs = (
        P("dp", None),
        P("dp", "expert"),
        P("dp", "expert"),
        P("expert", None, "dp"),
        P("expert", None, "dp"),
        P("expert", "dp", None),
        P("expert", None),
        P(),
        P(),
    )
    out_specs = P("dp", "expert")
    return jax.shard_map(body, mesh=mesh, in_specs=in_specs, out_specs=out_specs, check_vma=False)
```

profile of v0, /device:TPU:24, one launch (start us, length us, event | category | flops | bytes accessed | tf_op | source)
XLA Modules:
  0.0 397.0 jit_solution(8035669221233366851)
XLA Ops:
  6.5 0.7 all-gather.3.cloned.1.call-update
  7.3 55.7 %all-gather.3.cloned.1.call-done = bf16[4096,512]{1,0:T(8,128)(2,1)} async-done(((bf16[256,512]{1,0:T(8,128)(2,1)}), bf16[4096,512]{1,0:T(8,128)(2,1)}) %all-gather.3.cloned.1.call-update) | async-done | bytes 4194320 | tf_op jit(solution)/shard_map/all_gather | solution.py:49
  63.0 6.6 %fusion.12 = bf16[512,512]{1,0:T(8,128)(2,1)} fusion(bf16[512,4096]{1,0:T(8,128)(2,1)} %param.9, bf16[4096,512]{1,0:T(8,128)(2,1)} %all-gather.3.cloned.1.call-done, bf16[512,512]{1,0:T(8,128)(2,1)} %param.11), kind=kOutput, calls=%fused_computation.12 | convolution fusion | flops 2148270080 | bytes 9437184 | tf_op jit(solution)/shard_map/dot_general | solution.py:47
  69.7 0.2 dynamic-slice_reduce_fusion
  69.9 0.6 fusion.33
  73.1 28.8 %all-gather.5.cloned.1.call-done = bf16[512,4096]{1,0:T(8,128)(2,1)} async-done(((bf16[512,512]{1,0:T(8,128)(2,1)}), bf16[512,4096]{1,0:T(8,128)(2,1)}) %all-gather.5.cloned.1.call-update) | async-done | bytes 4194320 | tf_op jit(solution)/shard_map/all_gather | solution.py:57
  101.9 5.0 %gather_fusion = bf16[4,128,4096]{2,1,0:T(8,128)(2,1)} fusion(bf16[4,128,4096]{2,1,0:T(8,128)(2,1)} %bitcast.46, s32[1024]{0:T(1024)S(1)} %pad_clamp_fusion), kind=kCustom, calls=%fused_computation | custom fusion | bytes 8388624 | tf_op jit(solution)/shard_map/gather | solution.py:58
  106.9 4.2 %slice_select_fusion.3 = (bf16[1,128,4096]{2,1,0:T(8,128)(2,1)}, bf16[1,128,4096]{2,1,0:T(8,128)(2,1)}, bf16[1,128,4096]{2,1,0:T(8,128)(2,1)}, bf16[1,128,4096]{2,1,0:T(8,128)(2,1)}) fusion(bf16[4,128,4096]{2,1,0:T(8,128)(2,1)} %gather_fusion, pred[]{:T(512)S(6)} %eq.50, pred[]{:T(512)S(6)} %eq.52, pred[]{:T(512)S(6)} %eq.51, pred[]{:T(512)S(6)} %eq.53), kind=kLoop, calls=%fused_computation.18 | loop fusion | flops 2097152 | bytes 8388612 | tf_op jit(solution)/shard_map/jit(_where)/select_n | solution.py:11
  111.2 0.6 copy-done.6
  111.7 0.6 dynamic_slice.13
  112.4 6.4 %copy.26 = bf16[64,8,8,512]{3,2,1,0:T(8,128)(2,1)} copy(bf16[64,8,8,512]{3,1,2,0:T(8,128)(2,1)} %bitcast.45) | data formatting | bytes 8388608
  118.8 0.6 fusion.23
  119.4 95.3 %all-reduce.6.cloned.1.call-done = (bf16[1,128,4096]{2,1,0:T(8,128)(2,1)}, bf16[1,128,4096]{2,1,0:T(8,128)(2,1)}, bf16[1,128,4096]{2,1,0:T(8,128)(2,1)}, bf16[1,128,4096]{2,1,0:T(8,128)(2,1)}) async-done(((bf16[1,128,4096]{2,1,0:T(8,128)(2,1)}, bf16[1,128,4096]{2,1,0:T(8,128)(2,1)}, bf16[1,128,4096]{2,1,0:T(8,128)(2,1)}, bf16[1,128,4096]{2,1,0:T(8,128)(2,1)}), (bf16[1,128,4096]{2,1,0:T(8,128)(2,1)}, ...) | async-done | bytes 4194320 | tf_op jit(solution)/shard_map/psum | solution.py:12
  214.7 2.6 pad_maximum_fusion
  217.3 0.9 copy-done.4
  218.2 2.3 fusion.3
  220.5 2.4 fusion.16
  223.0 3.4 fusion
  226.3 54.6 %all_to_all.5 = bf16[8,512,512]{2,1,0:T(8,128)(2,1)S(1)} all-to-all(bf16[8,512,512]{2,1,0:T(8,128)(2,1)S(1)} %fusion), channel_id=1, replica_groups=mesh['dp'=16,'expert'=8] {'expert'}, dimensions={0} | all-to-all | bytes 8388608 | tf_op jit(solution)/shard_map/all_to_all | solution.py:68
  280.9 4.4 %copy.24 = bf16[32,128,512]{2,0,1:T(8,128)(2,1)} copy(bf16[32,128,512]{2,1,0:T(8,128)(2,1)S(1)} %bitcast.44) | data formatting | bytes 8388608 | tf_op jit(solution)/shard_map/reshape | solution.py:71
  285.4 0.1 copy.21
  285.7 100.9 %all-reduce.4.cloned.1.call-done = bf16[32,128,512]{2,0,1:T(8,128)(2,1)} async-done(((bf16[32,128,512]{2,0,1:T(8,128)(2,1)}), bf16[32,128,512]{2,0,1:T(8,128)(2,1)}) %all-reduce.4.cloned.1.call-update) | async-done | bytes 4194320 | tf_op jit(solution)/shard_map/psum | solution.py:70
  386.5 2.8 fusion.28
  389.4 1.1 fusion.19
  (26 shorter events, 0.5 us)
Async XLA Ops:
  6.5 56.4 %all-gather.3.cloned.1.call-start = ((), (), s32[]{:S(2)}) async-start(), calls=%async_computation.1 | async-start | bytes 4456448 | tf_op jit(solution)/shard_map/all_gather | solution.py:49
  7.3 62.4 %copy-start.2 = (s32[8,4]{0,1:T(4,128)S(1)}, s32[8,4]{0,1:T(4,128)}, u32[]{:S(2)}) copy-start(s32[8,4]{0,1:T(4,128)} %param.16) | copy-start | bytes 388
  7.3 94.6 %all-gather.5.cloned.1.call-start = ((), (), s32[]{:S(2)}) async-start(), calls=%async_computation.2 | async-start | bytes 4718592 | tf_op jit(solution)/shard_map/all_gather | solution.py:57
  69.6 145.1 %all-reduce.6.cloned.1.call-start = ((), (), s32[]{:S(2)}) async-start(), calls=%async_computation.4 | async-start | bytes 8388608 | tf_op jit(solution)/shard_map/psum | solution.py:12
  111.1 0.7 copy-start.6
  111.1 275.4 %all-reduce.4.cloned.1.call-start = ((), (), s32[]{:S(2)}) async-start(), calls=%async_computation.3 | async-start | bytes 8388608 | tf_op jit(solution)/shard_map/psum | solution.py:70
  112.4 6.4 %copy-start.3 = (f32[1,512]{1,0:T(1,128)S(1)}, f32[1,512]{1,0:T(1,128)}, u32[]{:S(2)}) copy-start(f32[1,512]{1,0:T(1,128)} %param.15) | copy-start | bytes 6148
  214.7 3.4 copy-start.4
  218.2 2.3 copy-start.5
  220.5 2.4 copy-start
  285.3 104.1 %copy-start.1 = (bf16[512,512]{1,0:T(8,128)(2,1)S(1)}, bf16[512,512]{1,0:T(8,128)(2,1)}, u32[]{:S(2)}) copy-start(bf16[512,512]{1,0:T(8,128)(2,1)} %fusion.12) | copy-start | bytes 1572868
Sparse Core Ops, SparseCore 0:
  9.5 53.4 all-gather.2
  69.7 32.0 all-gather.4
  111.2 103.4 all-reduce.5
  285.4 101.0 all-reduce.3
where the time goes:
time: 398 us; the launch traced here: 397 us
  waiting for transfers between devices  281 us (71%)
  blocking collectives  54.6 us (14%)
  local copies, waits for them, and re-layouts  19 us (5%)
  matrix products  17.6 us (4%)
  between operations  15.8 us (4%)
  other arithmetic  8.58 us (2%)
    psum x1, waiting for transfers between devices, body(): expert_out = lax.psum(terms.astype(jnp.bfloat16), 'dp')  101 us
    psum x1, waiting for transfers between devices, spread_2(): return lax.psum(kept, axis)  95.3 us
    all_gather x1, waiting for transfers between devices, body(): lax.all_gather(out_weight, 'dp', axis=0, tiled=True)  55.7 us
    all_to_all x1, blocking collectives, body(): lax.all_to_all(partial_value, 'expert', split_axis=0, concat_axis=0, tile...  54.6 us
    all_gather x1, waiting for transfers between devices, body(): whole = lax.all_gather(attended, 'expert', axis=1, tiled=True)  28.8 us
  transfers between devices with their start and end apart: 4, of which 4 were waited for; matrix products, arithmetic and copies ran while one was open for 2% of the time, Pallas kernels for 0%

commit v1 on v0

v1 whole, which is shorter than its diff:
```python
import jax
import jax.numpy as jnp
from jax import lax
from jax.sharding import PartitionSpec as P

BLK = 128
CAP = 4


def body(
    context,
    out_weight,
    residual,
    gate_weight,
    up_weight,
    down_weight,
    gate_values,
    chosen_blocks,
    block_counts,
):
    n_dp = lax.axis_size("dp")
    n_expert = lax.axis_size("expert")
    local_tokens = context.shape[0]
    local_width = residual.shape[1]
    model_width = context.shape[1]
    local_blocks = local_tokens // BLK
    n_blocks = local_blocks * n_dp
    piece = BLK // n_dp
    my_expert = lax.axis_index("expert")

    projected = jnp.dot(
        context,
        lax.all_gather(out_weight, "dp", axis=0, tiled=True),
        preferred_element_type=jnp.float32,
    )
    attended = (residual.astype(jnp.float32) + projected).astype(jnp.bfloat16)

    split = attended.reshape(local_blocks, n_dp, piece, local_width).transpose(1, 0, 2, 3)
    pieces = lax.all_to_all(split, "dp", 0, 0, tiled=True)
    pieces = pieces.reshape(n_blocks, piece, local_width)

    slots = jnp.take(pieces, chosen_blocks.reshape(-1), axis=0)
    slots = slots.reshape(n_expert, CAP, piece, local_width)
    mine = lax.all_to_all(slots, "expert", 0, 3, tiled=True)
    mine = mine.reshape(CAP * piece, model_width)
    picked = lax.all_gather(mine, "dp", axis=0, tiled=True)

    w_gate = gate_weight[0]
    w_up = up_weight[0]
    w_down = down_weight[0]
    gate_row = gate_values[0]
    my_count = lax.dynamic_index_in_dim(block_counts, my_expert, 0, keepdims=False)
    live = jnp.arange(CAP * BLK) // BLK < my_count
    scale = jnp.where(live, gate_row, jnp.zeros_like(gate_row))
    scale = scale.reshape(CAP, n_dp, piece).transpose(1, 0, 2).reshape(-1)

    gate = jnp.dot(picked, w_gate, preferred_element_type=jnp.float32)
    upper = jnp.dot(picked, w_up, preferred_element_type=jnp.float32)
    hidden = (jax.nn.silu(gate) * upper).astype(jnp.bfloat16)
    part = jnp.dot(hidden, w_down, preferred_element_type=jnp.float32)
    part = (part * scale[:, None]).astype(jnp.bfloat16)

    summed = lax.psum_scatter(
        part.reshape(n_dp, CAP * piece, model_width), "dp", scatter_dimension=0, tiled=True
    )
    summed = summed.reshape(CAP * piece, n_expert, local_width).transpose(1, 0, 2)
    outs = lax.all_to_all(summed, "expert", 0, 0, tiled=True)
    outs = outs.reshape(n_expert * CAP, piece * local_width)

    selector = chosen_blocks.reshape(-1)[None, :] == jnp.arange(n_blocks)[:, None]
    added = jnp.dot(selector.astype(jnp.bfloat16), outs, preferred_element_type=jnp.float32)
    added = added.reshape(n_dp, local_blocks, piece, local_width)
    back = lax.all_to_all(added, "dp", 0, 0, tiled=True)
    back = back.transpose(1, 0, 2, 3).reshape(local_tokens, local_width)

    total = attended.astype(jnp.float32) + back
    return total.astype(jnp.bfloat16)


def solution(mesh):
    in_specs = (
        P("dp", None),
        P("dp", "expert"),
        P("dp", "expert"),
        P("expert", None, "dp"),
        P("expert", None, "dp"),
        P("expert", "dp", None),
        P("expert", None),
        P(),
        P(),
    )
    out_specs = P("dp", "expert")
    return jax.shard_map(body, mesh=mesh, in_specs=in_specs, out_specs=out_specs, check_vma=False)
```

time: 398 us -> 282 us (0.71)
  waiting for transfers between devices: 281 us -> 196 us
  blocking collectives: 54.6 us -> 31.4 us
  local copies, waits for them, and re-layouts: 19 us -> 7.45 us
  starting transfers between devices: 0.12 us -> 10.2 us
  other arithmetic: 8.58 us -> 2.51 us
    psum x2 -> x0, waiting for transfers between devices: 196 us -> none  [the longest x1 101 us: body(): expert_out = lax.psum(terms.astype(jnp.bfloat16), 'dp')]
    unnamed x4, waiting for transfers between devices: 0.76 us -> 77.8 us
    all_to_all x1 -> x2, blocking collectives: 54.6 us -> 31.4 us  [the longest x1 19.6 us: body(): back = lax.all_to_all(added, 'dp', 0, 0, tiled=True)]
    all_gather x1, waiting for transfers between devices: 28.8 us -> 46.7 us  [body(): picked = lax.all_gather(mine, 'dp', axis=0, tiled=True)]
    all_to_all x0 -> x2, waiting for transfers between devices: none -> 16.2 us  [the longest x1 8.78 us: body(): pieces = lax.all_to_all(split, 'dp', 0, 0, tiled=True)]
    all_to_all x0 -> x2, starting transfers between devices: none -> 10.1 us  [the longest x1 5.71 us: body(): pieces = lax.all_to_all(split, 'dp', 0, 0, tiled=True)]
    select_n x4 -> x2, other arithmetic: 4.87 us -> 0.11 us  [body(): slots = jnp.take(pieces, chosen_blocks.reshape(-1), axis=0)]
    unnamed x15 -> x16, local copies, waits for them, and re-layouts: 7.86 us -> 3.18 us
  transfers between devices with their start and end apart: 4 -> 5, of which waited for: 4 -> 5; matrix products, arithmetic and copies ran while one was open for 2% -> 1% of each run, Pallas kernels for 0% -> 0%
where the time goes in v1:
time: 282 us; the launch traced here: 279 us
  waiting for transfers between devices  196 us (70%)
  blocking collectives  31.4 us (11%)
  matrix products  18.9 us (7%)
  between operations  13.3 us (5%)
  starting transfers between devices  10.2 us (4%)
  local copies, waits for them, and re-layouts  7.45 us (3%)
    unnamed x4, waiting for transfers between devices  77.8 us
    all_gather x1, waiting for transfers between devices, body(): lax.all_gather(out_weight, 'dp', axis=0, tiled=True)  54.9 us
    all_gather x1, waiting for transfers between devices, body(): picked = lax.all_gather(mine, 'dp', axis=0, tiled=True)  46.7 us
    all_to_all x1, blocking collectives, body(): back = lax.all_to_all(added, 'dp', 0, 0, tiled=True)  19.6 us
    all_to_all x1, blocking collectives, body(): mine = lax.all_to_all(slots, 'expert', 0, 3, tiled=True)  11.8 us
    all_to_all x1, waiting for transfers between devices, body(): pieces = lax.all_to_all(split, 'dp', 0, 0, tiled=True)  8.78 us
    all_to_all x1, waiting for transfers between devices, body(): outs = lax.all_to_all(summed, 'expert', 0, 0, tiled=True)  7.45 us
    dot_general x1, matrix products, body(): gate = jnp.dot(picked, w_gate, preferred_element_type=jnp.float32)  5.92 us
  transfers between devices with their start and end apart: 5, of which 5 were waited for; matrix products, arithmetic and copies ran while one was open for 1% of the time, Pallas kernels for 0%

profile of v1, /device:TPU:24, one launch (start us, length us, event | category | flops | bytes accessed | tf_op | source)
XLA Modules:
  0.0 279.3 jit_solution(4458407969886781237)
XLA Ops:
  6.5 0.7 all-gather.3.cloned.1.call-update
  7.3 0.8 copy.29
  8.1 54.9 %all-gather.3.cloned.1.call-done = bf16[4096,512]{1,0:T(8,128)(2,1)} async-done(((bf16[256,512]{1,0:T(8,128)(2,1)}), bf16[4096,512]{1,0:T(8,128)(2,1)}) %all-gather.3.cloned.1.call-update) | async-done | bytes 4194320 | tf_op jit(solution)/shard_map/all_gather | solution.py:33
  63.0 5.8 %fusion.8 = bf16[512,512]{1,0:T(8,128)(2,1)S(1)} fusion(bf16[512,4096]{1,0:T(8,128)(2,1)} %param.9, bf16[4096,512]{1,0:T(8,128)(2,1)} %all-gather.3.cloned.1.call-done, bf16[512,512]{1,0:T(8,128)(2,1)} %param.11), kind=kOutput, calls=%fused_computation.9 | convolution fusion | flops 2148270080 | bytes 9437184 | tf_op jit(solution)/shard_map/dot_general | solution.py:31
  68.9 0.8 copy.49
  69.7 5.7 %all-to-all-start = ((bf16[16,4,8,512]{3,2,1,0:T(8,128)(2,1)}), bf16[16,4,8,512]{3,2,1,0:T(8,128)(2,1)S(1)}, u32[]{:S(2)}, u32[]{:S(2)}) async-start(bf16[16,4,8,512]{3,2,1,0:T(8,128)(2,1)} %bitcast.60), calls=%async_computation | async-start | bytes 1048576 | tf_op jit(solution)/shard_map/all_to_all | solution.py:39
  75.6 8.8 %all-to-all-done = bf16[16,4,8,512]{3,2,1,0:T(8,128)(2,1)S(1)} async-done(((bf16[16,4,8,512]{3,2,1,0:T(8,128)(2,1)}), bf16[16,4,8,512]{3,2,1,0:T(8,128)(2,1)S(1)}, u32[]{:S(2)}, u32[]{:S(2)}) %all-to-all-start) | async-done | bytes 524320 | tf_op jit(solution)/shard_map/all_to_all | solution.py:39
  85.1 11.8 %all_to_all.30 = bf16[8,4,8,512]{3,2,1,0:T(8,128)(2,1)S(1)} all-to-all(bf16[8,4,8,512]{3,2,1,0:T(8,128)(2,1)S(1)} %broadcast_select_fusion), channel_id=1, replica_groups=mesh['dp'=16,'expert'=8] {'expert'}, dimensions={0} | all-to-all | bytes 524288 | tf_op jit(solution)/shard_map/all_to_all | solution.py:44
  97.0 0.8 copy.41
  98.4 0.7 reduce.3
  99.2 0.7 dynamic_slice.4
  99.9 0.7 select_bitcast_fusion
  100.7 46.7 %all-gather.5.cloned.1.call-done = bf16[512,4096]{1,0:T(8,128)(2,1)} async-done(((bf16[32,4096]{1,0:T(8,128)(2,1)}), bf16[512,4096]{1,0:T(8,128)(2,1)}) %all-gather.5.cloned.1.call-update) | async-done | bytes 4194320 | tf_op jit(solution)/shard_map/all_gather | solution.py:46
  147.4 5.9 %fusion.3 = f32[512,512]{1,0:T(8,128)S(1)} fusion(bf16[512,4096]{1,0:T(8,128)(2,1)} %all-gather.5.cloned.1.call-done, bf16[1,4096,512]{2,1,0:T(8,128)(2,1)} %param.12), kind=kOutput, calls=%fused_computation.5 | convolution fusion | flops 2147483648 | bytes 9437184 | tf_op jit(solution)/shard_map/dot_general | solution.py:57
  153.4 2.4 fusion.9
  155.8 4.3 %multiply_convert_fusion = bf16[512,4096]{1,0:T(8,128)(2,1)} fusion(bf16[512,512]{1,0:T(8,128)(2,1)S(1)} %fusion.9, bf16[1,512,4096]{2,1,0:T(8,128)(2,1)S(1)} %copy-done.3, f32[512]{0:T(512)S(1)} %mul.19), kind=kOutput, calls=%fused_computation.1 | convolution fusion | flops 2151677952 | bytes 8914944 | tf_op jit(solution)/shard_map/dot_general | solution.py:60
  160.1 77.1 %reduce-scatter.4.cloned.1.call-done = bf16[1,32,4096]{2,1,0:T(8,128)(2,1)} async-done(((bf16[16,32,4096]{2,1,0:T(8,128)(2,1)}), bf16[1,32,4096]{2,1,0:T(8,128)(2,1)}) %reduce-scatter.4.cloned.1.call-update) | async-done | bytes 262160
  237.2 1.0 copy.42
  238.3 0.8 copy.35
  239.0 4.4 %all-to-all-start.2 = ((bf16[8,32,512]{2,1,0:T(8,128)(2,1)}), bf16[8,32,512]{2,1,0:T(8,128)(2,1)S(1)}, u32[]{:S(2)}, u32[]{:S(2)}) async-start(bf16[8,32,512]{2,1,0:T(8,128)(2,1)} %copy.35), calls=%async_computation.2 | async-start | bytes 524288 | tf_op jit(solution)/shard_map/all_to_all | solution.py:67
  243.6 7.5 %all-to-all-done.2 = bf16[8,32,512]{2,1,0:T(8,128)(2,1)S(1)} async-done(((bf16[8,32,512]{2,1,0:T(8,128)(2,1)}), bf16[8,32,512]{2,1,0:T(8,128)(2,1)S(1)}, u32[]{:S(2)}, u32[]{:S(2)}) %all-to-all-start.2) | async-done | bytes 262176 | tf_op jit(solution)/shard_map/all_to_all | solution.py:67
  251.5 0.6 copy.37
  252.1 19.6 %all_to_all.31 = f32[16,4,8,512]{3,2,1,0:T(8,128)S(1)} all-to-all(f32[16,4,8,512]{3,2,1,0:T(8,128)S(1)} %copy.37), channel_id=1, replica_groups=mesh['dp'=16,'expert'=8] {'dp'}, dimensions={0} | all-to-all | bytes 2097152 | tf_op jit(solution)/shard_map/all_to_all | solution.py:73
  271.8 1.0 fusion.12
  (34 shorter events, 2.6 us)
Async XLA Ops:
  6.5 56.4 %all-gather.3.cloned.1.call-start = ((), (), s32[]{:S(2)}) async-start(), calls=%async_computation.5 | async-start | bytes 4456448 | tf_op jit(solution)/shard_map/all_gather | solution.py:33
  8.1 67.4 %copy-start = (s32[8,4]{0,1:T(4,128)S(1)}, s32[8,4]{0,1:T(4,128)}, u32[]{:S(2)}) copy-start(s32[8,4]{0,1:T(4,128)} %param.16) | copy-start | bytes 388
  68.8 29.6 %copy-start.1 = (f32[1,512]{1,0:T(1,128)S(1)}, f32[1,512]{1,0:T(1,128)}, u32[]{:S(2)}) copy-start(f32[1,512]{1,0:T(1,128)} %param.15) | copy-start | bytes 6148
  68.8 30.4 %copy-start.5 = (s32[8]{0:T(128)S(1)}, s32[8]{0:T(128)}, u32[]{:S(2)}) copy-start(s32[8]{0:T(128)} %param.17) | copy-start | bytes 100
  69.7 14.7 %all-to-all-start = ((bf16[16,4,8,512]{3,2,1,0:T(8,128)(2,1)}), bf16[16,4,8,512]{3,2,1,0:T(8,128)(2,1)S(1)}, u32[]{:S(2)}, u32[]{:S(2)}) async-start(bf16[16,4,8,512]{3,2,1,0:T(8,128)(2,1)} %bitcast.60), calls=%async_computation | async-start | bytes 1048576 | tf_op jit(solution)/shard_map/all_to_all | solution.py:39
  75.4 72.0 %all-gather.5.cloned.1.call-start = ((), (), s32[]{:S(2)}) async-start(), calls=%async_computation.6 | async-start | bytes 4456448 | tf_op jit(solution)/shard_map/all_gather | solution.py:46
  97.8 139.4 %reduce-scatter.4.cloned.1.call-start = ((), (), s32[]{:S(2)}) async-start(), calls=%async_computation.7 | async-start | bytes 4456448
  147.4 5.9 %copy-start.2 = (bf16[1,4096,512]{2,1,0:T(8,128)(2,1)S(1)}, bf16[1,4096,512]{2,1,0:T(8,128)(2,1)}, u32[]{:S(2)}) copy-start(bf16[1,4096,512]{2,1,0:T(8,128)(2,1)} %param.13) | copy-start | bytes 12582916
  147.4 5.9 %copy-start.4 = (bf16[512,4096]{1,0:T(8,128)(2,1)S(1)}, bf16[512,4096]{1,0:T(8,128)(2,1)}, u32[]{:S(2)}) copy-start(bf16[512,4096]{1,0:T(8,128)(2,1)} %all-gather.5.cloned.1.call-done) | copy-start | bytes 12582916
  153.3 2.5 copy-start.3
  239.0 12.0 %all-to-all-start.2 = ((bf16[8,32,512]{2,1,0:T(8,128)(2,1)}), bf16[8,32,512]{2,1,0:T(8,128)(2,1)S(1)}, u32[]{:S(2)}, u32[]{:S(2)}) async-start(bf16[8,32,512]{2,1,0:T(8,128)(2,1)} %copy.35), calls=%async_computation.2 | async-start | bytes 524288 | tf_op jit(solution)/shard_map/all_to_all | solution.py:67
Sparse Core Ops, SparseCore 0:
  9.5 53.4 all-gather.2
  97.9 49.4 all-gather.4
  160.3 76.9 reduce-scatter.3

commit v2 on v1

--- a/solution.py
+++ b/solution.py
@@ -1,10 +1,58 @@
+import functools
+
 import jax
 import jax.numpy as jnp
 from jax import lax
 from jax.sharding import PartitionSpec as P
+from jax.experimental import pallas as pl
+from jax.experimental.pallas import tpu as pltpu
 
 BLK = 128
 CAP = 4
+
+
+def _exchange_kernel(n, gather, x_ref, o_ref, local_sem, send_sems, recv_sems):
+    me = lax.axis_index("dp")
+    mesh_id = pl.DeviceIdType.MESH
+    barrier = pltpu.get_barrier_semaphore()
+    for k in range(1, n):
+        pl.semaphore_signal(barrier, 1, device_id={"dp": lax.rem(me + k, n)}, device_id_type=mesh_id)
+    pl.semaphore_wait(barrier, n - 1)
+    local = pltpu.make_async_copy(x_ref if gather else x_ref.at[me], o_ref.at[me], local_sem)
+    local.start()
+    copies = []
+    for k in range(1, n):
+        target = lax.rem(me + k, n)
+        copy = pltpu.make_async_remote_copy(
+            src_ref=x_ref if gather else x_ref.at[target],
+            dst_ref=o_ref.at[me],
+            send_sem=send_sems.at[k - 1],
+            recv_sem=recv_sems.at[k - 1],
+            device_id={"dp": target},
+            device_id_type=mesh_id,
+        )
+        copy.start()
+        copies.append(copy)
+    local.wait()
+    for copy in copies:
+        copy.wait()
+
+
+def dp_exchange(x, gather, cid):
+    n = lax.axis_size("dp")
+    shape = (n,) + x.shape if gather else x.shape
+    return pl.pallas_call(
+        functools.partial(_exchange_kernel, n, gather),
+        out_shape=jax.ShapeDtypeStruct(shape, x.dtype),
+        in_specs=[pl.BlockSpec(memory_space=pl.ANY)],
+        out_specs=pl.BlockSpec(memory_space=pl.ANY),
+        scratch_shapes=[
+            pltpu.SemaphoreType.DMA(()),
+            pltpu.SemaphoreType.DMA((n - 1,)),
+            pltpu.SemaphoreType.DMA((n - 1,)),
+        ],
+        compiler_params=pltpu.CompilerParams(collective_id=cid, has_side_effects=True),
+    )(x)
 
 
 def body(
@@ -36,7 +84,7 @@
     attended = (residual.astype(jnp.float32) + projected).astype(jnp.bfloat16)
 
     split = attended.reshape(local_blocks, n_dp, piece, local_width).transpose(1, 0, 2, 3)
-    pieces = lax.all_to_all(split, "dp", 0, 0, tiled=True)
+    pieces = dp_exchange(split, gather=False, cid=0)
     pieces = pieces.reshape(n_blocks, piece, local_width)
 
     slots = jnp.take(pieces, chosen_blocks.reshape(-1), axis=0)
@@ -60,9 +108,8 @@
     part = jnp.dot(hidden, w_down, preferred_element_type=jnp.float32)
     part = (part * scale[:, None]).astype(jnp.bfloat16)
 
-    summed = lax.psum_scatter(
-        part.reshape(n_dp, CAP * piece, model_width), "dp", scatter_dimension=0, tiled=True
-    )
+    terms = dp_exchange(part.reshape(n_dp, CAP * piece, model_width), gather=False, cid=1)
+    summed = terms.astype(jnp.float32).sum(axis=0).astype(jnp.bfloat16)
     summed = summed.reshape(CAP * piece, n_expert, local_width).transpose(1, 0, 2)
     outs = lax.all_to_all(summed, "expert", 0, 0, tiled=True)
     outs = outs.reshape(n_expert * CAP, piece * local_width)
@@ -70,7 +117,7 @@
     selector = chosen_blocks.reshape(-1)[None, :] == jnp.arange(n_blocks)[:, None]
     added = jnp.dot(selector.astype(jnp.bfloat16), outs, preferred_element_type=jnp.float32)
     added = added.reshape(n_dp, local_blocks, piece, local_width)
-    back = lax.all_to_all(added, "dp", 0, 0, tiled=True)
+    back = dp_exchange(added, gather=False, cid=2)
     back = back.transpose(1, 0, 2, 3).reshape(local_tokens, local_width)
 
     total = attended.astype(jnp.float32) + back

time: 282 us -> 300 us (1.064)
  Pallas kernels: 0 us -> 126 us
  waiting for transfers between devices: 196 us -> 109 us
  blocking collectives: 31.4 us -> 11.8 us
  starting transfers between devices: 10.2 us -> 4.56 us
  other arithmetic: 2.51 us -> 6.04 us
    pallas_call x0 -> x3, Pallas kernels: none -> 126 us  [dp_exchange(): pl.pallas_call(functools.partial(_exchange_kernel, n, gather), out_shape=...]
    unnamed x4 -> x2, waiting for transfers between devices: 77.8 us -> 0.73 us
    all_to_all x1 -> x0, blocking collectives: 19.6 us -> none  [body(): back = lax.all_to_all(added, 'dp', 0, 0, tiled=True)]
    all_to_all x1 -> x0, waiting for transfers between devices: 8.78 us -> none  [body(): pieces = lax.all_to_all(split, 'dp', 0, 0, tiled=True)]
    all_to_all x1 -> x0, starting transfers between devices: 5.71 us -> none  [body(): pieces = lax.all_to_all(split, 'dp', 0, 0, tiled=True)]
  transfers between devices with their start and end apart: 5 -> 3, of which waited for: 5 -> 3; matrix products, arithmetic and copies ran while one was open for 1% -> 1% of each run, Pallas kernels for 0% -> 0%
where the time goes in v2:
time: 300 us
  Pallas kernels  126 us (42%)
  waiting for transfers between devices  109 us (36%)
  matrix products  18.8 us (6%)
  between operations  13.6 us (5%)
  blocking collectives  11.8 us (4%)
  local copies, waits for them, and re-layouts  9.66 us (3%)
  other arithmetic  6.04 us (2%)
  starting transfers between devices  4.56 us (2%)
    pallas_call x3, Pallas kernels, dp_exchange(): pl.pallas_call(functools.partial(_exchange_kernel, n, gather), out_shape=...  126 us
    all_gather x1, waiting for transfers between devices, body(): lax.all_gather(out_weight, 'dp', axis=0, tiled=True)  54 us
    all_gather x1, waiting for transfers between devices, body(): picked = lax.all_gather(mine, 'dp', axis=0, tiled=True)  46.8 us
    all_to_all x1, blocking collectives, body(): mine = lax.all_to_all(slots, 'expert', 0, 3, tiled=True)  11.8 us
    all_to_all x1, waiting for transfers between devices, body(): outs = lax.all_to_all(summed, 'expert', 0, 0, tiled=True)  7.45 us
  transfers between devices with their start and end apart: 3, of which 3 were waited for; matrix products, arithmetic and copies ran while one was open for 1% of the time, Pallas kernels for 0%

profile of v2, /device:TPU:24, one launch (start us, length us, event | category | flops | bytes accessed | tf_op | source)
XLA Modules:
  0.0 299.8 jit_solution(6843805478152524687)
XLA Ops:
  6.5 0.7 all-gather.3.cloned.1.call-update
  7.3 0.8 copy.31
  8.1 0.7 compare_and_fusion
  8.9 54.0 %all-gather.3.cloned.1.call-done = bf16[4096,512]{1,0:T(8,128)(2,1)} async-done(((bf16[256,512]{1,0:T(8,128)(2,1)}), bf16[4096,512]{1,0:T(8,128)(2,1)}) %all-gather.3.cloned.1.call-update) | async-done | bytes 4194320 | tf_op jit(solution)/shard_map/all_gather | solution.py:81
  63.0 5.8 %fusion.8 = bf16[512,512]{1,0:T(8,128)(2,1)S(1)} fusion(bf16[512,4096]{1,0:T(8,128)(2,1)} %param.9, bf16[4096,512]{1,0:T(8,128)(2,1)} %all-gather.3.cloned.1.call-done, bf16[512,512]{1,0:T(8,128)(2,1)} %param.11), kind=kOutput, calls=%fused_computation.9 | convolution fusion | flops 2148270080 | bytes 9437184 | tf_op jit(solution)/shard_map/dot_general | solution.py:79
  68.8 0.8 copy.51
  69.7 12.9 %shard_map.91 = bf16[16,4,8,512]{3,2,1,0:T(8,128)(2,1)} custom-call(bf16[16,4,8,512]{3,2,1,0:T(8,128)(2,1)} %bitcast.62), custom_call_target="tpu_custom_call" | custom-call | tf_op jit(solution)/shard_map/pallas_call | solution.py:44
  82.6 1.6 gather_fusion
  84.3 11.8 %all_to_all.20 = bf16[8,4,8,512]{3,2,1,0:T(8,128)(2,1)S(1)} all-to-all(bf16[8,4,8,512]{3,2,1,0:T(8,128)(2,1)S(1)} %broadcast_select_fusion), channel_id=1, replica_groups=mesh['dp'=16,'expert'=8] {'expert'}, dimensions={0} | all-to-all | bytes 524288 | tf_op jit(solution)/shard_map/all_to_all | solution.py:92
  96.2 0.8 copy.43
  98.9 0.6 select_bitcast_fusion
  99.7 46.8 %all-gather.5.cloned.1.call-done = bf16[512,4096]{1,0:T(8,128)(2,1)} async-done(((bf16[32,4096]{1,0:T(8,128)(2,1)}), bf16[512,4096]{1,0:T(8,128)(2,1)}) %all-gather.5.cloned.1.call-update) | async-done | bytes 4194320 | tf_op jit(solution)/shard_map/all_gather | solution.py:94
  146.5 5.9 %fusion.3 = f32[512,512]{1,0:T(8,128)S(1)} fusion(bf16[512,4096]{1,0:T(8,128)(2,1)} %all-gather.5.cloned.1.call-done, bf16[1,4096,512]{2,1,0:T(8,128)(2,1)} %param.12), kind=kOutput, calls=%fused_computation.5 | convolution fusion | flops 2147483648 | bytes 9437184 | tf_op jit(solution)/shard_map/dot_general | solution.py:105
  152.5 2.4 fusion.9
  154.9 4.3 %multiply_convert_fusion = bf16[512,4096]{1,0:T(8,128)(2,1)} fusion(bf16[512,512]{1,0:T(8,128)(2,1)S(1)} %fusion.9, bf16[1,512,4096]{2,1,0:T(8,128)(2,1)S(1)} %copy-done.2, f32[512]{0:T(512)S(1)} %mul.19), kind=kOutput, calls=%fused_computation.1 | convolution fusion | flops 2151677952 | bytes 8914944 | tf_op jit(solution)/shard_map/dot_general | solution.py:108
  159.2 92.5 %shard_map.92 = bf16[16,32,4096]{2,1,0:T(8,128)(2,1)} custom-call(bf16[16,32,4096]{2,1,0:T(8,128)(2,1)} %bitcast.60), custom_call_target="tpu_custom_call" | custom-call | tf_op jit(solution)/shard_map/pallas_call | solution.py:44
  251.8 3.0 reduce_sum.12
  254.8 0.8 copy.37
  255.6 4.5 %all-to-all-start.1 = ((bf16[8,32,512]{2,1,0:T(8,128)(2,1)}), bf16[8,32,512]{2,1,0:T(8,128)(2,1)S(1)}, u32[]{:S(2)}, u32[]{:S(2)}) async-start(bf16[8,32,512]{2,1,0:T(8,128)(2,1)} %copy.37), calls=%async_computation.1 | async-start | bytes 524288 | tf_op jit(solution)/shard_map/all_to_all | solution.py:114
  260.2 7.5 %all-to-all-done.1 = bf16[8,32,512]{2,1,0:T(8,128)(2,1)S(1)} async-done(((bf16[8,32,512]{2,1,0:T(8,128)(2,1)}), bf16[8,32,512]{2,1,0:T(8,128)(2,1)S(1)}, u32[]{:S(2)}, u32[]{:S(2)}) %all-to-all-start.1) | async-done | bytes 262176 | tf_op jit(solution)/shard_map/all_to_all | solution.py:114
  268.2 1.6 copy.39.x_ref
  269.7 20.9 %shard_map.93 = f32[16,4,8,512]{3,2,1,0:T(8,128)} custom-call(f32[16,4,8,512]{3,2,1,0:T(8,128)} %copy.39.x_ref), custom_call_target="tpu_custom_call" | custom-call | tf_op jit(solution)/shard_map/pallas_call | solution.py:44
  290.6 1.3 copy.40
  291.9 1.0 fusion.12
  (30 shorter events, 3.1 us)
Async XLA Ops:
  6.5 56.4 %all-gather.3.cloned.1.call-start = ((), (), s32[]{:S(2)}) async-start(), calls=%async_computation.2 | async-start | bytes 4456448 | tf_op jit(solution)/shard_map/all_gather | solution.py:81
  7.3 139.2 %all-gather.5.cloned.1.call-start = ((), (), s32[]{:S(2)}) async-start(), calls=%async_computation.3 | async-start | bytes 4456448 | tf_op jit(solution)/shard_map/all_gather | solution.py:94
  68.8 28.8 %copy-start = (f32[1,512]{1,0:T(1,128)S(1)}, f32[1,512]{1,0:T(1,128)}, u32[]{:S(2)}) copy-start(f32[1,512]{1,0:T(1,128)} %param.15) | copy-start | bytes 6148
  68.8 29.5 %copy-start.4 = (s32[8]{0:T(128)S(1)}, s32[8]{0:T(128)}, u32[]{:S(2)}) copy-start(s32[8]{0:T(128)} %param.17) | copy-start | bytes 100
  146.5 5.9 %copy-start.1 = (bf16[1,4096,512]{2,1,0:T(8,128)(2,1)S(1)}, bf16[1,4096,512]{2,1,0:T(8,128)(2,1)}, u32[]{:S(2)}) copy-start(bf16[1,4096,512]{2,1,0:T(8,128)(2,1)} %param.13) | copy-start | bytes 12582916
  146.5 5.9 %copy-start.3 = (bf16[512,4096]{1,0:T(8,128)(2,1)S(1)}, bf16[512,4096]{1,0:T(8,128)(2,1)}, u32[]{:S(2)}) copy-start(bf16[512,4096]{1,0:T(8,128)(2,1)} %all-gather.5.cloned.1.call-done) | copy-start | bytes 12582916
  152.4 2.5 copy-start.2
  255.6 12.1 %all-to-all-start.1 = ((bf16[8,32,512]{2,1,0:T(8,128)(2,1)}), bf16[8,32,512]{2,1,0:T(8,128)(2,1)S(1)}, u32[]{:S(2)}, u32[]{:S(2)}) async-start(bf16[8,32,512]{2,1,0:T(8,128)(2,1)} %copy.37), calls=%async_computation.1 | async-start | bytes 524288 | tf_op jit(solution)/shard_map/all_to_all | solution.py:114
Sparse Core Ops, SparseCore 0:
  9.5 53.4 all-gather.2
  97.2 49.2 all-gather.4

commit v3 on v2

--- a/solution.py
+++ b/solution.py
@@ -55,6 +55,79 @@
     )(x)
 
 
+def _route_kernel(strides, side, *refs):
+    n_in = len(strides)
+    ins, outs = refs[:n_in], refs[n_in:2 * n_in]
+    local_sems, send_sems, recv_sems = refs[2 * n_in:]
+    me = lax.axis_index("dp")
+    mesh_id = pl.DeviceIdType.MESH
+    routes = []
+    for r, stride in enumerate(strides):
+        coord = lax.rem(me // stride, side)
+        base = me - coord * stride
+        for k in range(1, side):
+            to = lax.rem(coord + k, side)
+            routes.append((r, coord, to, base + to * stride))
+    barrier = pltpu.get_barrier_semaphore()
+    for _, _, _, target in routes:
+        pl.semaphore_signal(barrier, 1, device_id={"dp": target}, device_id_type=mesh_id)
+    pl.semaphore_wait(barrier, len(routes))
+    locals_ = []
+    for r in range(n_in):
+        coord = lax.rem(me // strides[r], side)
+        local = pltpu.make_async_copy(ins[r].at[coord], outs[r].at[coord], local_sems.at[r])
+        local.start()
+        locals_.append(local)
+    copies = []
+    for i, (r, coord, to, target) in enumerate(routes):
+        copy = pltpu.make_async_remote_copy(
+            src_ref=ins[r].at[to],
+            dst_ref=outs[r].at[coord],
+            send_sem=send_sems.at[i],
+            recv_sem=recv_sems.at[i],
+            device_id={"dp": target},
+            device_id_type=mesh_id,
+        )
+        copy.start()
+        copies.append(copy)
+    for local in locals_:
+        local.wait()
+    for copy in copies:
+        copy.wait()
+
+
+def dp_route(xs, strides, cid, side=4):
+    n_routes = len(strides) * (side - 1)
+    return pl.pallas_call(
+        functools.partial(_route_kernel, tuple(strides), side),
+        out_shape=[jax.ShapeDtypeStruct(x.shape, x.dtype) for x in xs],
+        in_specs=[pl.BlockSpec(memory_space=pl.ANY)] * len(xs),
+        out_specs=[pl.BlockSpec(memory_space=pl.ANY)] * len(xs),
+        scratch_shapes=[
+            pltpu.SemaphoreType.DMA((len(xs),)),
+            pltpu.SemaphoreType.DMA((n_routes,)),
+            pltpu.SemaphoreType.DMA((n_routes,)),
+        ],
+        compiler_params=pltpu.CompilerParams(collective_id=cid, has_side_effects=True),
+    )(*xs)
+
+
+def reduce_scatter_2d(part, cid):
+    side = 4
+    n_dp, rows, cols = part.shape
+    half = cols // 2
+    grid = part.reshape(side, side, rows, cols)
+    first_a = grid[..., :half].transpose(1, 0, 2, 3)
+    first_b = grid[..., half:]
+    got_a, got_b = dp_route([first_a, first_b], (1, side), cid)
+    second_a = got_a.astype(jnp.float32).sum(axis=0).astype(jnp.bfloat16)
+    second_b = got_b.astype(jnp.float32).sum(axis=0).astype(jnp.bfloat16)
+    got_a, got_b = dp_route([second_a, second_b], (side, 1), cid + 1)
+    total_a = got_a.astype(jnp.float32).sum(axis=0)
+    total_b = got_b.astype(jnp.float32).sum(axis=0)
+    return jnp.concatenate([total_a, total_b], axis=-1)
+
+
 def body(
     context,
     out_weight,
@@ -108,8 +181,8 @@
     part = jnp.dot(hidden, w_down, preferred_element_type=jnp.float32)
     part = (part * scale[:, None]).astype(jnp.bfloat16)
 
-    terms = dp_exchange(part.reshape(n_dp, CAP * piece, model_width), gather=False, cid=1)
-    summed = terms.astype(jnp.float32).sum(axis=0).astype(jnp.bfloat16)
+    summed = reduce_scatter_2d(part.reshape(n_dp, CAP * piece, model_width), cid=1)
+    summed = summed.astype(jnp.bfloat16)
     summed = summed.reshape(CAP * piece, n_expert, local_width).transpose(1, 0, 2)
     outs = lax.all_to_all(summed, "expert", 0, 0, tiled=True)
     outs = outs.reshape(n_expert * CAP, piece * local_width)
@@ -117,7 +190,7 @@
     selector = chosen_blocks.reshape(-1)[None, :] == jnp.arange(n_blocks)[:, None]
     added = jnp.dot(selector.astype(jnp.bfloat16), outs, preferred_element_type=jnp.float32)
     added = added.reshape(n_dp, local_blocks, piece, local_width)
-    back = dp_exchange(added, gather=False, cid=2)
+    back = lax.all_to_all(added, "dp", 0, 0, tiled=True)
     back = back.transpose(1, 0, 2, 3).reshape(local_tokens, local_width)
 
     total = attended.astype(jnp.float32) + back

time: 300 us -> 259 us (0.86)
  Pallas kernels: 126 us -> 58.6 us
  blocking collectives: 11.8 us -> 31.4 us
  other arithmetic: 6.04 us -> 11.4 us
    pallas_call x3 -> x1, Pallas kernels: 126 us -> 12.9 us  [dp_exchange(): pl.pallas_call(functools.partial(_exchange_kernel, n, gather), out_shape=...]
    pallas_call x0 -> x2, Pallas kernels: none -> 45.7 us  [dp_route(): pl.pallas_call(functools.partial(_route_kernel, tuple(strides), side), ou...]
    all_to_all x0 -> x1, blocking collectives: none -> 19.7 us  [body(): back = lax.all_to_all(added, 'dp', 0, 0, tiled=True)]
    reduce_sum x1 -> x4, other arithmetic: 2.99 us -> 8.09 us  [the longest x1 2.92 us: reduce_scatter_2d(): second_a = got_a.astype(jnp.float32).sum(axis=0).astype(jnp.bfloat16)]
  transfers between devices with their start and end apart: 3 -> 3, of which waited for: 3 -> 3; matrix products, arithmetic and copies ran while one was open for 1% -> 2% of each run, Pallas kernels for 0% -> 0%
where the time goes in v3:
time: 259 us; the launch traced here: 256 us
  waiting for transfers between devices  109 us (42%)
  Pallas kernels  58.6 us (23%)
  blocking collectives  31.4 us (12%)
  matrix products  16.8 us (6%)
  between operations  13.6 us (5%)
  other arithmetic  11.4 us (4%)
  local copies, waits for them, and re-layouts  11.1 us (4%)
  starting transfers between devices  4.47 us (2%)
    all_gather x1, waiting for transfers between devices, body(): lax.all_gather(out_weight, 'dp', axis=0, tiled=True)  54 us
    all_gather x1, waiting for transfers between devices, body(): picked = lax.all_gather(mine, 'dp', axis=0, tiled=True)  46.5 us
    pallas_call x2, Pallas kernels, dp_route(): pl.pallas_call(functools.partial(_route_kernel, tuple(strides), side), ou...  45.7 us
    all_to_all x1, blocking collectives, body(): back = lax.all_to_all(added, 'dp', 0, 0, tiled=True)  19.7 us
    pallas_call x1, Pallas kernels, dp_exchange(): pl.pallas_call(functools.partial(_exchange_kernel, n, gather), out_shape=...  12.9 us
    all_to_all x1, blocking collectives, body(): mine = lax.all_to_all(slots, 'expert', 0, 3, tiled=True)  11.8 us
    all_to_all x1, waiting for transfers between devices, body(): outs = lax.all_to_all(summed, 'expert', 0, 0, tiled=True)  7.45 us
    dot_general x1, matrix products, body(): gate = jnp.dot(picked, w_gate, preferred_element_type=jnp.float32)  5.92 us
  transfers between devices with their start and end apart: 3, of which 3 were waited for; matrix products, arithmetic and copies ran while one was open for 2% of the time, Pallas kernels for 0%

profile of v3, /device:TPU:24, one launch (start us, length us, event | category | flops | bytes accessed | tf_op | source)
XLA Modules:
  0.0 256.2 jit_solution(17836771045501327961)
XLA Ops:
  8.9 54.0 %all-gather.3.cloned.1.call-done = bf16[4096,512]{1,0:T(8,128)(2,1)} async-done(((bf16[256,512]{1,0:T(8,128)(2,1)}), bf16[4096,512]{1,0:T(8,128)(2,1)}) %all-gather.3.cloned.1.call-update) | async-done | bytes 4194320 | tf_op jit(solution)/shard_map/all_gather | solution.py:154
  63.0 5.8 %fusion.8 = bf16[512,512]{1,0:T(8,128)(2,1)S(1)} fusion(bf16[512,4096]{1,0:T(8,128)(2,1)} %param.9, bf16[4096,512]{1,0:T(8,128)(2,1)} %all-gather.3.cloned.1.call-done, bf16[512,512]{1,0:T(8,128)(2,1)} %param.11), kind=kOutput, calls=%fused_computation.10 | convolution fusion | flops 2148270080 | bytes 9437184 | tf_op jit(solution)/shard_map/dot_general | solution.py:152
  68.8 0.8 copy.52
  69.7 12.9 %shard_map.91 = bf16[16,4,8,512]{3,2,1,0:T(8,128)(2,1)} custom-call(bf16[16,4,8,512]{3,2,1,0:T(8,128)(2,1)} %bitcast.62), custom_call_target="tpu_custom_call" | custom-call | tf_op jit(solution)/shard_map/pallas_call | solution.py:44
  82.6 1.6 gather_fusion
  84.3 11.8 %all_to_all.25 = bf16[8,4,8,512]{3,2,1,0:T(8,128)(2,1)S(1)} all-to-all(bf16[8,4,8,512]{3,2,1,0:T(8,128)(2,1)S(1)} %broadcast_select_fusion), channel_id=1, replica_groups=mesh['dp'=16,'expert'=8] {'expert'}, dimensions={0} | all-to-all | bytes 524288 | tf_op jit(solution)/shard_map/all_to_all | solution.py:165
  96.2 0.8 copy.45
  100.0 46.5 %all-gather.5.cloned.1.call-done = bf16[512,4096]{1,0:T(8,128)(2,1)} async-done(((bf16[32,4096]{1,0:T(8,128)(2,1)}), bf16[512,4096]{1,0:T(8,128)(2,1)}) %all-gather.5.cloned.1.call-update) | async-done | bytes 4194320 | tf_op jit(solution)/shard_map/all_gather | solution.py:167
  146.5 5.9 %fusion.3 = f32[512,512]{1,0:T(8,128)S(1)} fusion(bf16[512,4096]{1,0:T(8,128)(2,1)} %all-gather.5.cloned.1.call-done, bf16[1,4096,512]{2,1,0:T(8,128)(2,1)} %param.12), kind=kOutput, calls=%fused_computation.5 | convolution fusion | flops 2147483648 | bytes 9437184 | tf_op jit(solution)/shard_map/dot_general | solution.py:178
  152.4 2.4 fusion.9
  154.9 2.4 multiply_convert_fusion
  157.2 1.8 fusion.24
  159.1 1.6 copy.38.refs_0_
  160.7 34.5 %shard_map.92 = (bf16[4,4,32,2048]{3,2,1,0:T(8,128)(2,1)}, bf16[4,4,32,2048]{3,2,1,0:T(8,128)(2,1)}) custom-call(bf16[4,4,32,2048]{3,2,1,0:T(8,128)(2,1)} %copy.38.refs_0_, bf16[4,4,32,2048]{3,2,1,0:T(8,128)(2,1)} %get-tuple-element.13.refs_1_), custom_call_target="tpu_custom_call" | custom-call | tf_op jit(solution)/shard_map/pallas_call | solution.py:101
  195.1 2.9 %reduce_sum.42.refs_0_ = bf16[4,32,2048]{2,1,0:T(8,128)(2,1)} reduce(bf16[4,4,32,2048]{3,2,1,0:T(8,128)(2,1)} %get-tuple-element.9, bf16[]{:T(256)} %constant.65.clone.1), dimensions={0}, to_apply=%region_0.1 | reduce | flops 786432 | bytes 2621442 | tf_op jit(solution)/shard_map/reduce_sum | solution.py:123
  198.1 2.9 %reduce_sum.43.refs_1_ = bf16[4,32,2048]{2,1,0:T(8,128)(2,1)} reduce(bf16[4,4,32,2048]{3,2,1,0:T(8,128)(2,1)} %get-tuple-element.10, bf16[]{:T(256)} %constant.65.clone.1), dimensions={0}, to_apply=%region_1.2 | reduce | flops 786432 | bytes 2621442 | tf_op jit(solution)/shard_map/reduce_sum | solution.py:124
  201.0 11.3 %shard_map.93 = (bf16[4,32,2048]{2,1,0:T(8,128)(2,1)}, bf16[4,32,2048]{2,1,0:T(8,128)(2,1)}) custom-call(bf16[4,32,2048]{2,1,0:T(8,128)(2,1)} %reduce_sum.42.refs_0_, bf16[4,32,2048]{2,1,0:T(8,128)(2,1)} %reduce_sum.43.refs_1_), custom_call_target="tpu_custom_call" | custom-call | tf_op jit(solution)/shard_map/pallas_call | solution.py:101
  212.2 1.1 reduce.2
  213.4 1.1 reduce.3
  214.8 0.8 copy.39
  215.6 4.4 %all-to-all-start.1 = ((bf16[8,32,512]{2,1,0:T(8,128)(2,1)}), bf16[8,32,512]{2,1,0:T(8,128)(2,1)S(1)}, u32[]{:S(2)}, u32[]{:S(2)}) async-start(bf16[8,32,512]{2,1,0:T(8,128)(2,1)} %copy.39), calls=%async_computation.1 | async-start | bytes 524288 | tf_op jit(solution)/shard_map/all_to_all | solution.py:187
  220.1 7.5 %all-to-all-done.1 = bf16[8,32,512]{2,1,0:T(8,128)(2,1)S(1)} async-done(((bf16[8,32,512]{2,1,0:T(8,128)(2,1)}), bf16[8,32,512]{2,1,0:T(8,128)(2,1)S(1)}, u32[]{:S(2)}, u32[]{:S(2)}) %all-to-all-start.1) | async-done | bytes 262176 | tf_op jit(solution)/shard_map/all_to_all | solution.py:187
  228.6 19.7 %all_to_all.26 = f32[16,4,8,512]{3,2,1,0:T(8,128)S(1)} all-to-all(f32[16,4,8,512]{3,2,1,0:T(8,128)S(1)} %copy.41), channel_id=1, replica_groups=mesh['dp'=16,'expert'=8] {'dp'}, dimensions={0} | all-to-all | bytes 2097152 | tf_op jit(solution)/shard_map/all_to_all | solution.py:193
  248.4 1.0 fusion.12
  (38 shorter events, 7.1 us)
Async XLA Ops:
  6.5 56.4 %all-gather.3.cloned.1.call-start = ((), (), s32[]{:S(2)}) async-start(), calls=%async_computation.3 | async-start | bytes 4456448 | tf_op jit(solution)/shard_map/all_gather | solution.py:154
  7.3 139.2 %all-gather.5.cloned.1.call-start = ((), (), s32[]{:S(2)}) async-start(), calls=%async_computation.4 | async-start | bytes 4456448 | tf_op jit(solution)/shard_map/all_gather | solution.py:167
  68.8 28.8 %copy-start = (f32[1,512]{1,0:T(1,128)S(1)}, f32[1,512]{1,0:T(1,128)}, u32[]{:S(2)}) copy-start(f32[1,512]{1,0:T(1,128)} %param.15) | copy-start | bytes 6148
  68.8 29.6 %copy-start.4 = (s32[8]{0:T(128)S(1)}, s32[8]{0:T(128)}, u32[]{:S(2)}) copy-start(s32[8]{0:T(128)} %param.17) | copy-start | bytes 100
  146.5 5.9 %copy-start.1 = (bf16[1,4096,512]{2,1,0:T(8,128)(2,1)S(1)}, bf16[1,4096,512]{2,1,0:T(8,128)(2,1)}, u32[]{:S(2)}) copy-start(bf16[1,4096,512]{2,1,0:T(8,128)(2,1)} %param.13) | copy-start | bytes 12582916
  146.5 5.9 %copy-start.3 = (bf16[512,4096]{1,0:T(8,128)(2,1)S(1)}, bf16[512,4096]{1,0:T(8,128)(2,1)}, u32[]{:S(2)}) copy-start(bf16[512,4096]{1,0:T(8,128)(2,1)} %all-gather.5.cloned.1.call-done) | copy-start | bytes 12582916
  152.4 2.4 copy-start.2
  215.6 12.0 %all-to-all-start.1 = ((bf16[8,32,512]{2,1,0:T(8,128)(2,1)}), bf16[8,32,512]{2,1,0:T(8,128)(2,1)S(1)}, u32[]{:S(2)}, u32[]{:S(2)}) async-start(bf16[8,32,512]{2,1,0:T(8,128)(2,1)} %copy.39), calls=%async_computation.1 | async-start | bytes 524288 | tf_op jit(solution)/shard_map/all_to_all | solution.py:187
Sparse Core Ops, SparseCore 0:
  9.5 53.4 all-gather.2
  97.2 49.2 all-gather.4

commit v4 on v3

--- a/solution.py
+++ b/solution.py
@@ -55,7 +55,7 @@
     )(x)
 
 
-def _route_kernel(strides, side, *refs):
+def _route_kernel(strides, side, gather, *refs):
     n_in = len(strides)
     ins, outs = refs[:n_in], refs[n_in:2 * n_in]
     local_sems, send_sems, recv_sems = refs[2 * n_in:]
@@ -75,13 +75,14 @@
     locals_ = []
     for r in range(n_in):
         coord = lax.rem(me // strides[r], side)
-        local = pltpu.make_async_copy(ins[r].at[coord], outs[r].at[coord], local_sems.at[r])
+        source = ins[r] if gather else ins[r].at[coord]
+        local = pltpu.make_async_copy(source, outs[r].at[coord], local_sems.at[r])
         local.start()
         locals_.append(local)
     copies = []
     for i, (r, coord, to, target) in enumerate(routes):
         copy = pltpu.make_async_remote_copy(
-            src_ref=ins[r].at[to],
+            src_ref=ins[r] if gather else ins[r].at[to],
             dst_ref=outs[r].at[coord],
             send_sem=send_sems.at[i],
             recv_sem=recv_sems.at[i],
@@ -96,11 +97,12 @@
         copy.wait()
 
 
-def dp_route(xs, strides, cid, side=4):
+def dp_route(xs, strides, cid, side=4, gather=False):
     n_routes = len(strides) * (side - 1)
+    shapes = [((side,) + x.shape) if gather else x.shape for x in xs]
     return pl.pallas_call(
-        functools.partial(_route_kernel, tuple(strides), side),
-        out_shape=[jax.ShapeDtypeStruct(x.shape, x.dtype) for x in xs],
+        functools.partial(_route_kernel, tuple(strides), side, gather),
+        out_shape=[jax.ShapeDtypeStruct(s, x.dtype) for s, x in zip(shapes, xs)],
         in_specs=[pl.BlockSpec(memory_space=pl.ANY)] * len(xs),
         out_specs=[pl.BlockSpec(memory_space=pl.ANY)] * len(xs),
         scratch_shapes=[
@@ -126,6 +128,18 @@
     total_a = got_a.astype(jnp.float32).sum(axis=0)
     total_b = got_b.astype(jnp.float32).sum(axis=0)
     return jnp.concatenate([total_a, total_b], axis=-1)
+
+
+def all_gather_2d(x, cid):
+    side = 4
+    half = x.shape[-1] // 2
+    got_a, got_b = dp_route([x[..., :half], x[..., half:]], (1, side), cid, gather=True)
+    got_a, got_b = dp_route([got_a, got_b], (side, 1), cid + 1, gather=True)
+    n = side * side
+    got_a = got_a.reshape((n,) + got_a.shape[2:])
+    perm = (1, 0) + tuple(range(2, got_b.ndim))
+    got_b = got_b.transpose(perm).reshape((n,) + got_b.shape[2:])
+    return got_a, got_b
 
 
 def body(
@@ -149,10 +163,15 @@
     piece = BLK // n_dp
     my_expert = lax.axis_index("expert")
 
-    projected = jnp.dot(
-        context,
-        lax.all_gather(out_weight, "dp", axis=0, tiled=True),
-        preferred_element_type=jnp.float32,
+    w_a, w_b = all_gather_2d(out_weight, cid=10)
+    w_a = w_a.reshape(model_width, -1)
+    w_b = w_b.reshape(model_width, -1)
+    projected = jnp.concatenate(
+        [
+            jnp.dot(context, w_a, preferred_element_type=jnp.float32),
+            jnp.dot(context, w_b, preferred_element_type=jnp.float32),
+        ],
+        axis=1,
     )
     attended = (residual.astype(jnp.float32) + projected).astype(jnp.bfloat16)
 
@@ -164,7 +183,10 @@
     slots = slots.reshape(n_expert, CAP, piece, local_width)
     mine = lax.all_to_all(slots, "expert", 0, 3, tiled=True)
     mine = mine.reshape(CAP * piece, model_width)
-    picked = lax.all_gather(mine, "dp", axis=0, tiled=True)
+    picked_a, picked_b = all_gather_2d(mine, cid=20)
+    picked_a = picked_a.reshape(n_dp * CAP * piece, -1)
+    picked_b = picked_b.reshape(n_dp * CAP * piece, -1)
+    half = picked_a.shape[1]
 
     w_gate = gate_weight[0]
     w_up = up_weight[0]
@@ -175,8 +197,12 @@
     scale = jnp.where(live, gate_row, jnp.zeros_like(gate_row))
     scale = scale.reshape(CAP, n_dp, piece).transpose(1, 0, 2).reshape(-1)
 
-    gate = jnp.dot(picked, w_gate, preferred_element_type=jnp.float32)
-    upper = jnp.dot(picked, w_up, preferred_element_type=jnp.float32)
+    gate = jnp.dot(picked_a, w_gate[:half], preferred_element_type=jnp.float32) + jnp.dot(
+        picked_b, w_gate[half:], preferred_element_type=jnp.float32
+    )
+    upper = jnp.dot(picked_a, w_up[:half], preferred_element_type=jnp.float32) + jnp.dot(
+        picked_b, w_up[half:], preferred_element_type=jnp.float32
+    )
     hidden = (jax.nn.silu(gate) * upper).astype(jnp.bfloat16)
     part = jnp.dot(hidden, w_down, preferred_element_type=jnp.float32)
     part = (part * scale[:, None]).astype(jnp.bfloat16)
@@ -189,12 +215,10 @@
 
     selector = chosen_blocks.reshape(-1)[None, :] == jnp.arange(n_blocks)[:, None]
     added = jnp.dot(selector.astype(jnp.bfloat16), outs, preferred_element_type=jnp.float32)
-    added = added.reshape(n_dp, local_blocks, piece, local_width)
-    back = lax.all_to_all(added, "dp", 0, 0, tiled=True)
-    back = back.transpose(1, 0, 2, 3).reshape(local_tokens, local_width)
-
-    total = attended.astype(jnp.float32) + back
-    return total.astype(jnp.bfloat16)
+    mixed = pieces.reshape(n_blocks, piece * local_width).astype(jnp.float32) + added
+    mixed = mixed.astype(jnp.bfloat16).reshape(n_dp, local_blocks, piece, local_width)
+    back = dp_exchange(mixed, gather=False, cid=3)
+    return back.transpose(1, 0, 2, 3).reshape(local_tokens, local_width)
 
 
 def solution(mesh):

time: 259 us -> 236 us (0.911)
  Pallas kernels: 58.6 us -> 163 us
  waiting for transfers between devices: 109 us -> 11.8 us
  blocking collectives: 31.4 us -> 0 us
  between operations: 13.6 us -> 0.27 us
  local copies, waits for them, and re-layouts: 11.1 us -> 24.4 us
  starting transfers between devices: 4.47 us -> 8.72 us
    all_gather x2 -> x0, waiting for transfers between devices: 101 us -> none  [the longest x1 54 us: body(): lax.all_gather(out_weight, 'dp', axis=0, tiled=True)]
    pallas_call x2 -> x6, Pallas kernels: 45.7 us -> 138 us  [dp_route(): pl.pallas_call(functools.partial(_route_kernel, tuple(strides), side, gat...]
    all_to_all x2 -> x0, blocking collectives: 31.4 us -> none  [the longest x1 19.7 us: body(): back = lax.all_to_all(added, 'dp', 0, 0, tiled=True)]
    pallas_call x1 -> x2, Pallas kernels: 12.9 us -> 25.1 us  [dp_exchange(): pl.pallas_call(functools.partial(_exchange_kernel, n, gather), out_shape=...]
    dot_general x3 -> x5, matrix products: 14.1 us -> 7.33 us  [the longest x1 2.23 us: body(): jnp.dot(picked_b, w_up[half:], preferred_element_type=jnp.float32)]
    dot_general x1, matrix products: 2.36 us -> 8.68 us  [body(): part = jnp.dot(hidden, w_down, preferred_element_type=jnp.float32)]
    transpose x1 -> x3, local copies, waits for them, and re-layouts: 0.08 us -> 5.68 us  [the longest x2 3.8 us: all_gather_2d(): got_b = got_b.transpose(perm).reshape((n,) + got_b.shape[2:])]
    all_to_all x0 -> x1, starting transfers between devices: none -> 5.31 us  [body(): mine = lax.all_to_all(slots, 'expert', 0, 3, tiled=True)]
  transfers between devices with their start and end apart: 3 -> 2, of which waited for: 3 -> 2; matrix products, arithmetic and copies ran while one was open for 2% -> 1% of each run, Pallas kernels for 0% -> 0%
where the time goes in v4:
time: 236 us; the launch traced here: 235 us
  Pallas kernels  163 us (69%)
  local copies, waits for them, and re-layouts  24.4 us (10%)
  matrix products  16.3 us (7%)
  waiting for transfers between devices  11.8 us (5%)
  other arithmetic  9.85 us (4%)
  starting transfers between devices  8.72 us (4%)
    pallas_call x6, Pallas kernels, dp_route(): pl.pallas_call(functools.partial(_route_kernel, tuple(strides), side, gat...  138 us
    pallas_call x2, Pallas kernels, dp_exchange(): pl.pallas_call(functools.partial(_exchange_kernel, n, gather), out_shape=...  25.1 us
    dot_general x1, matrix products, body(): part = jnp.dot(hidden, w_down, preferred_element_type=jnp.float32)  8.68 us
    all_to_all x1, waiting for transfers between devices, body(): outs = lax.all_to_all(summed, 'expert', 0, 0, tiled=True)  7.18 us
    unnamed x25, local copies, waits for them, and re-layouts  5.77 us
    all_to_all x1, starting transfers between devices, body(): mine = lax.all_to_all(slots, 'expert', 0, 3, tiled=True)  5.31 us
  transfers between devices with their start and end apart: 2, of which 2 were waited for; matrix products, arithmetic and copies ran while one was open for 1% of the time, Pallas kernels for 0%

profile of v4, /device:TPU:24, one launch (start us, length us, event | category | flops | bytes accessed | tf_op | source)
XLA Modules:
  0.0 234.6 jit_solution(13320285464512704392)
XLA Ops:
  1.4 1.7 fusion.39
  3.1 12.2 %shard_map.91 = (bf16[4,256,256]{2,1,0:T(8,128)(2,1)}, bf16[4,256,256]{2,1,0:T(8,128)(2,1)}) custom-call(bf16[256,256]{1,0:T(8,128)(2,1)} %get-tuple-element.34.refs_0_, bf16[256,256]{1,0:T(8,128)(2,1)} %get-tuple-element.33.refs_1_), custom_call_target="tpu_custom_call" | custom-call | tf_op jit(solution)/shard_map/pallas_call | solution.py:103
  15.3 34.4 %shard_map.92 = (bf16[4,4,256,256]{3,2,1,0:T(8,128)(2,1)}, bf16[4,4,256,256]{3,2,1,0:T(8,128)(2,1)}) custom-call(bf16[4,256,256]{2,1,0:T(8,128)(2,1)} %get-tuple-element.17.refs_0_, bf16[4,256,256]{2,1,0:T(8,128)(2,1)} %get-tuple-element.18.refs_1_), custom_call_target="tpu_custom_call" | custom-call | tf_op jit(solution)/shard_map/pallas_call | solution.py:103
  49.7 1.9 copy.40
  52.5 1.3 convolution_bitcast_fusion
  56.9 12.4 %shard_map.93 = bf16[16,4,8,512]{3,2,1,0:T(8,128)(2,1)} custom-call(bf16[16,4,8,512]{3,2,1,0:T(8,128)(2,1)} %bitcast.83), custom_call_target="tpu_custom_call" | custom-call | tf_op jit(solution)/shard_map/pallas_call | solution.py:44
  69.6 1.6 gather_fusion
  72.0 5.3 %all-to-all-start = ((bf16[8,4,8,512]{3,2,1,0:T(8,128)(2,1)}), bf16[8,4,8,512]{3,2,1,0:T(8,128)(2,1)S(1)}, u32[]{:S(2)}, u32[]{:S(2)}) async-start(bf16[8,4,8,512]{3,2,1,0:T(8,128)(2,1)} %broadcast_select_fusion), calls=%async_computation | async-start | bytes 524288 | tf_op jit(solution)/shard_map/all_to_all | solution.py:184
  80.2 4.7 %all-to-all-done = bf16[8,4,8,512]{3,2,1,0:T(8,128)(2,1)S(1)} async-done(((bf16[8,4,8,512]{3,2,1,0:T(8,128)(2,1)}), bf16[8,4,8,512]{3,2,1,0:T(8,128)(2,1)S(1)}, u32[]{:S(2)}, u32[]{:S(2)}) %all-to-all-start) | async-done | bytes 262176 | tf_op jit(solution)/shard_map/all_to_all | solution.py:184
  85.6 11.3 %shard_map.94 = (bf16[4,32,2048]{2,1,0:T(8,128)(2,1)}, bf16[4,32,2048]{2,1,0:T(8,128)(2,1)}) custom-call(bf16[32,2048]{1,0:T(8,128)(2,1)} %get-tuple-element.32.refs_0_, bf16[32,2048]{1,0:T(8,128)(2,1)} %get-tuple-element.31.refs_1_), custom_call_target="tpu_custom_call" | custom-call | tf_op jit(solution)/shard_map/pallas_call | solution.py:103
  96.9 34.6 %shard_map.95 = (bf16[4,4,32,2048]{3,2,1,0:T(8,128)(2,1)}, bf16[4,4,32,2048]{3,2,1,0:T(8,128)(2,1)}) custom-call(bf16[4,32,2048]{2,1,0:T(8,128)(2,1)} %get-tuple-element.21.refs_0_, bf16[4,32,2048]{2,1,0:T(8,128)(2,1)} %get-tuple-element.22.refs_1_), custom_call_target="tpu_custom_call" | custom-call | tf_op jit(solution)/shard_map/pallas_call | solution.py:103
  131.5 1.9 copy.47
  136.5 2.2 fusion.2
  140.0 8.7 %multiply_convert_fusion = bf16[512,4096]{1,0:T(8,128)(2,1)} fusion(bf16[1,512,4096]{2,1,0:T(8,128)(2,1)} %param.14, f32[512]{0:T(512)S(1)} %mul.19, f32[512,512]{1,0:T(8,128)} %fusion.2, bf16[512,2048]{1,0:T(8,128)(2,1)S(1)} %bitcast.91, bf16[1,4096,512]{2,1,0:T(8,128)(2,1)} %param.13, f32[512,512]{1,0:T(8,128)S(1)} %fusion.14), kind=kOutput, calls=%fused_computation.1 | convolution fusion | flops 3227254784 | bytes 14682112 | tf_op jit(solution)/shard_map/dot_general | solution.py:207
  148.7 4.1 %fusion.37 = (bf16[4,4,32,2048]{3,2,1,0:T(8,128)(2,1)}, bf16[4,4,32,2048]{3,2,0,1:T(8,128)(2,1)S(1)}) fusion(bf16[4,4,32,4096]{3,2,1,0:T(8,128)(2,1)} %bitcast.73), kind=kLoop, calls=%fused_computation.49 | loop fusion | bytes 8388608 | tf_op jit(solution)/shard_map/slice | solution.py:123
  152.7 1.6 copy.49.refs_0_
  154.3 35.1 %shard_map.96 = (bf16[4,4,32,2048]{3,2,1,0:T(8,128)(2,1)}, bf16[4,4,32,2048]{3,2,1,0:T(8,128)(2,1)}) custom-call(bf16[4,4,32,2048]{3,2,1,0:T(8,128)(2,1)} %copy.49.refs_0_, bf16[4,4,32,2048]{3,2,1,0:T(8,128)(2,1)} %get-tuple-element.29.refs_1_), custom_call_target="tpu_custom_call" | custom-call | tf_op jit(solution)/shard_map/pallas_call | solution.py:103
  189.5 3.1 %reduce_sum.42.refs_0_ = bf16[4,32,2048]{2,1,0:T(8,128)(2,1)} reduce(bf16[4,4,32,2048]{3,2,1,0:T(8,128)(2,1)} %get-tuple-element.25, bf16[]{:T(256)} %constant.63.clone.1), dimensions={0}, to_apply=%region_0.1 | reduce | flops 786432 | bytes 2621442 | tf_op jit(solution)/shard_map/reduce_sum | solution.py:125
  192.5 1.3 reduce_sum.43.refs_1_
  193.8 10.6 %shard_map.97 = (bf16[4,32,2048]{2,1,0:T(8,128)(2,1)}, bf16[4,32,2048]{2,1,0:T(8,128)(2,1)}) custom-call(bf16[4,32,2048]{2,1,0:T(8,128)(2,1)} %reduce_sum.42.refs_0_, bf16[4,32,2048]{2,1,0:T(8,128)(2,1)} %reduce_sum.43.refs_1_), custom_call_target="tpu_custom_call" | custom-call | tf_op jit(solution)/shard_map/pallas_call | solution.py:103
  207.8 3.4 %all-to-all-start.1 = ((bf16[8,32,512]{2,1,0:T(8,128)(2,1)}), bf16[8,32,512]{2,1,0:T(8,128)(2,1)S(1)}, u32[]{:S(2)}, u32[]{:S(2)}) async-start(bf16[8,32,512]{2,1,0:T(8,128)(2,1)} %copy.50), calls=%async_computation.1 | async-start | bytes 524288 | tf_op jit(solution)/shard_map/all_to_all | solution.py:213
  211.5 7.2 %all-to-all-done.1 = bf16[8,32,512]{2,1,0:T(8,128)(2,1)S(1)} async-done(((bf16[8,32,512]{2,1,0:T(8,128)(2,1)}), bf16[8,32,512]{2,1,0:T(8,128)(2,1)S(1)}, u32[]{:S(2)}, u32[]{:S(2)}) %all-to-all-start.1) | async-done | bytes 262176 | tf_op jit(solution)/shard_map/all_to_all | solution.py:213
  220.1 12.6 %shard_map.98 = bf16[16,4,8,512]{3,2,1,0:T(8,128)(2,1)} custom-call(bf16[16,4,8,512]{3,2,1,0:T(8,128)(2,1)} %bitcast.84), custom_call_target="tpu_custom_call" | custom-call | tf_op jit(solution)/shard_map/pallas_call | solution.py:44
  232.7 1.9 copy.51
  (54 shorter events, 19.3 us)
Async XLA Ops:
  49.7 2.8 %copy-start.4 = (bf16[512,4096]{1,0:T(8,128)(2,1)S(1)}, bf16[512,4096]{1,0:T(8,128)(2,1)}, u32[]{:S(2)}) copy-start(bf16[512,4096]{1,0:T(8,128)(2,1)} %param.9) | copy-start | bytes 12582916
  52.5 1.6 copy-start.8
  54.1 1.3 copy-start.2
  56.1 21.8 %copy-start.3 = (f32[1,512]{1,0:T(1,128)S(1)}, f32[1,512]{1,0:T(1,128)}, u32[]{:S(2)}) copy-start(f32[1,512]{1,0:T(1,128)} %param.15) | copy-start | bytes 6148
  56.1 22.6 %copy-start.9 = (s32[8]{0:T(128)S(1)}, s32[8]{0:T(128)}, u32[]{:S(2)}) copy-start(s32[8]{0:T(128)} %param.17) | copy-start | bytes 100
  72.0 12.8 %all-to-all-start = ((bf16[8,4,8,512]{3,2,1,0:T(8,128)(2,1)}), bf16[8,4,8,512]{3,2,1,0:T(8,128)(2,1)S(1)}, u32[]{:S(2)}, u32[]{:S(2)}) async-start(bf16[8,4,8,512]{3,2,1,0:T(8,128)(2,1)} %broadcast_select_fusion), calls=%async_computation | async-start | bytes 524288 | tf_op jit(solution)/shard_map/all_to_all | solution.py:184
  131.5 2.8 %copy-start.5 = (bf16[1,4096,512]{2,1,0:T(8,128)(2,1)S(1)}, bf16[1,4096,512]{2,1,0:T(8,128)(2,1)}, u32[]{:S(2)}) copy-start(bf16[1,4096,512]{2,1,0:T(8,128)(2,1)} %param.12) | copy-start | bytes 12582916
  134.3 2.2 copy-start.6
  136.5 2.2 copy-start.7
  189.5 3.1 %copy-start.1 = (bf16[4,4,32,2048]{3,2,1,0:T(8,128)(2,1)S(1)}, bf16[4,4,32,2048]{3,2,1,0:T(8,128)(2,1)}, u32[]{:S(2)}) copy-start(bf16[4,4,32,2048]{3,2,1,0:T(8,128)(2,1)} %get-tuple-element.26) | copy-start | bytes 6291460
  193.8 17.5 %copy-start = (bf16[16,4,8,512]{3,2,1,0:T(8,128)(2,1)S(1)}, bf16[16,4,8,512]{3,2,1,0:T(8,128)(2,1)}, u32[]{:S(2)}) copy-start(bf16[16,4,8,512]{3,2,1,0:T(8,128)(2,1)} %shard_map.93) | copy-start | bytes 1572868
  207.8 10.9 %all-to-all-start.1 = ((bf16[8,32,512]{2,1,0:T(8,128)(2,1)}), bf16[8,32,512]{2,1,0:T(8,128)(2,1)S(1)}, u32[]{:S(2)}, u32[]{:S(2)}) async-start(bf16[8,32,512]{2,1,0:T(8,128)(2,1)} %copy.50), calls=%async_computation.1 | async-start | bytes 524288 | tf_op jit(solution)/shard_map/all_to_all | solution.py:213

commit v5 on v4

--- a/solution.py
+++ b/solution.py
@@ -163,11 +163,14 @@
     piece = BLK // n_dp
     my_expert = lax.axis_index("expert")
 
-    w_a, w_b = all_gather_2d(out_weight, cid=10)
+    split_w = local_width // 2
+    w_s = lax.all_gather(out_weight[:, :split_w], "dp", axis=0, tiled=True)
+    w_a, w_b = all_gather_2d(out_weight[:, split_w:], cid=10)
     w_a = w_a.reshape(model_width, -1)
     w_b = w_b.reshape(model_width, -1)
     projected = jnp.concatenate(
         [
+            jnp.dot(context, w_s, preferred_element_type=jnp.float32),
             jnp.dot(context, w_a, preferred_element_type=jnp.float32),
             jnp.dot(context, w_b, preferred_element_type=jnp.float32),
         ],
@@ -183,10 +186,12 @@
     slots = slots.reshape(n_expert, CAP, piece, local_width)
     mine = lax.all_to_all(slots, "expert", 0, 3, tiled=True)
     mine = mine.reshape(CAP * piece, model_width)
-    picked_a, picked_b = all_gather_2d(mine, cid=20)
+    split_m = model_width // 2
+    picked_s = lax.all_gather(mine[:, :split_m], "dp", axis=0, tiled=True)
+    picked_a, picked_b = all_gather_2d(mine[:, split_m:], cid=20)
     picked_a = picked_a.reshape(n_dp * CAP * piece, -1)
     picked_b = picked_b.reshape(n_dp * CAP * piece, -1)
-    half = picked_a.shape[1]
+    quarter = picked_a.shape[1]
 
     w_gate = gate_weight[0]
     w_up = up_weight[0]
@@ -197,18 +202,23 @@
     scale = jnp.where(live, gate_row, jnp.zeros_like(gate_row))
     scale = scale.reshape(CAP, n_dp, piece).transpose(1, 0, 2).reshape(-1)
 
-    gate = jnp.dot(picked_a, w_gate[:half], preferred_element_type=jnp.float32) + jnp.dot(
-        picked_b, w_gate[half:], preferred_element_type=jnp.float32
-    )
-    upper = jnp.dot(picked_a, w_up[:half], preferred_element_type=jnp.float32) + jnp.dot(
-        picked_b, w_up[half:], preferred_element_type=jnp.float32
-    )
+    def contract(w):
+        return (
+            jnp.dot(picked_s, w[:split_m], preferred_element_type=jnp.float32)
+            + jnp.dot(picked_a, w[split_m:split_m + quarter], preferred_element_type=jnp.float32)
+            + jnp.dot(picked_b, w[split_m + quarter:], preferred_element_type=jnp.float32)
+        )
+
+    gate = contract(w_gate)
+    upper = contract(w_up)
     hidden = (jax.nn.silu(gate) * upper).astype(jnp.bfloat16)
     part = jnp.dot(hidden, w_down, preferred_element_type=jnp.float32)
     part = (part * scale[:, None]).astype(jnp.bfloat16)
 
-    summed = reduce_scatter_2d(part.reshape(n_dp, CAP * piece, model_width), cid=1)
-    summed = summed.astype(jnp.bfloat16)
+    part = part.reshape(n_dp, CAP * piece, model_width)
+    summed_s = lax.psum_scatter(part[..., :split_m], "dp", scatter_dimension=0, tiled=True)
+    summed_k = reduce_scatter_2d(part[..., split_m:], cid=1).astype(jnp.bfloat16)
+    summed = jnp.concatenate([summed_s[0], summed_k], axis=-1)
     summed = summed.reshape(CAP * piece, n_expert, local_width).transpose(1, 0, 2)
     outs = lax.all_to_all(summed, "expert", 0, 0, tiled=True)
     outs = outs.reshape(n_expert * CAP, piece * local_width)

time: 236 us -> 273 us (1.16)
  waiting for transfers between devices: 11.8 us -> 80.9 us
  Pallas kernels: 163 us -> 104 us
  between operations: 0.27 us -> 13.5 us
  blocking collectives: 0 us -> 11.8 us
  matrix products: 16.3 us -> 24.3 us
  starting transfers between devices: 8.72 us -> 4.7 us
    pallas_call x6, Pallas kernels: 138 us -> 79.5 us  [dp_route(): pl.pallas_call(functools.partial(_route_kernel, tuple(strides), side, gat...]
    unnamed x0 -> x4, waiting for transfers between devices: none -> 40.9 us
    all_gather x0 -> x2, waiting for transfers between devices: none -> 32.8 us  [the longest x1 16.8 us: body(): picked_s = lax.all_gather(mine[:, :split_m], 'dp', axis=0, tiled=True)]
    all_to_all x0 -> x1, blocking collectives: none -> 11.8 us  [body(): mine = lax.all_to_all(slots, 'expert', 0, 3, tiled=True)]
    dot_general x3 -> x6, matrix products: 4.74 us -> 11.2 us  [the longest x2 4.86 us: contract(): jnp.dot(picked_s, w[:split_m], preferred_element_type=jnp.float32)]
    slice x0 -> x3, local copies, waits for them, and re-layouts: none -> 6.25 us  [the longest x1 4.01 us: body(): part[..., :split_m]]
    all_to_all x1 -> x0, starting transfers between devices: 5.31 us -> none  [body(): mine = lax.all_to_all(slots, 'expert', 0, 3, tiled=True)]
    all_to_all x1 -> x0, waiting for transfers between devices: 4.66 us -> none  [body(): mine = lax.all_to_all(slots, 'expert', 0, 3, tiled=True)]
  transfers between devices with their start and end apart: 2 -> 4, of which waited for: 2 -> 4; matrix products, arithmetic and copies ran while one was open for 1% -> 9% of each run, Pallas kernels for 0% -> 29%
where the time goes in v5:
time: 273 us; the launch traced here: 272 us
  Pallas kernels  104 us (38%)
  waiting for transfers between devices  80.9 us (30%)
  local copies, waits for them, and re-layouts  25 us (9%)
  matrix products  24.3 us (9%)
  between operations  13.5 us (5%)
  blocking collectives  11.8 us (4%)
  other arithmetic  8.23 us (3%)
  starting transfers between devices  4.7 us (2%)
    pallas_call x6, Pallas kernels, dp_route(): pl.pallas_call(functools.partial(_route_kernel, tuple(strides), side, gat...  79.5 us
    unnamed x4, waiting for transfers between devices  40.9 us
    pallas_call x2, Pallas kernels, dp_exchange(): pl.pallas_call(functools.partial(_exchange_kernel, n, gather), out_shape=...  24.4 us
    all_gather x1, waiting for transfers between devices, body(): picked_s = lax.all_gather(mine[:, :split_m], 'dp', axis=0, tiled=True)  16.8 us
    all_gather x1, waiting for transfers between devices, body(): w_s = lax.all_gather(out_weight[:, :split_w], 'dp', axis=0, tiled=True)  16 us
    all_to_all x1, blocking collectives, body(): mine = lax.all_to_all(slots, 'expert', 0, 3, tiled=True)  11.8 us
    dot_general x1, matrix products, body(): part = jnp.dot(hidden, w_down, preferred_element_type=jnp.float32)  7.48 us
    all_to_all x1, waiting for transfers between devices, body(): outs = lax.all_to_all(summed, 'expert', 0, 0, tiled=True)  7.26 us
  transfers between devices with their start and end apart: 4, of which 4 were waited for; matrix products, arithmetic and copies ran while one was open for 9% of the time, Pallas kernels for 29%

profile of v5, /device:TPU:24, one launch (start us, length us, event | category | flops | bytes accessed | tf_op | source)
XLA Modules:
  0.0 272.3 jit_solution(17508658382162239798)
XLA Ops:
  6.5 1.6 slice.72
  9.7 8.2 %shard_map.91 = (bf16[4,256,128]{2,1,0:T(8,128)(2,1)}, bf16[4,256,128]{2,1,0:T(8,128)(2,1)}) custom-call(bf16[256,128]{1,0:T(8,128)(2,1)} %get-tuple-element.36.refs_0_, bf16[256,128]{1,0:T(8,128)(2,1)} %get-tuple-element.35.refs_1_), custom_call_target="tpu_custom_call" | custom-call | tf_op jit(solution)/shard_map/pallas_call | solution.py:103
  18.0 19.2 %shard_map.92 = (bf16[4,4,256,128]{3,2,1,0:T(8,128)(2,1)}, bf16[4,4,256,128]{3,2,1,0:T(8,128)(2,1)}) custom-call(bf16[4,256,128]{2,1,0:T(8,128)(2,1)} %get-tuple-element.17.refs_0_, bf16[4,256,128]{2,1,0:T(8,128)(2,1)} %get-tuple-element.18.refs_1_), custom_call_target="tpu_custom_call" | custom-call | tf_op jit(solution)/shard_map/pallas_call | solution.py:103
  40.2 3.8 %convolution_bitcast_fusion = f32[512,128]{0,1:T(8,128)S(1)} fusion(bf16[4096,128]{1,0:T(8,128)(2,1)S(1)} %bitcast.82, bf16[512,4096]{1,0:T(8,128)(2,1)} %param.9), kind=kOutput, calls=%fused_computation.17 | convolution fusion | flops 536870912 | bytes 5505024 | tf_op jit(solution)/shard_map/dot_general | solution.py:175
  45.6 16.0 %all-gather.3.cloned.1.call-done = bf16[4096,256]{1,0:T(8,128)(2,1)} async-done(((bf16[256,256]{1,0:T(8,128)(2,1)}), bf16[4096,256]{1,0:T(8,128)(2,1)}) %all-gather.3.cloned.1.call-update) | async-done | bytes 2097168 | tf_op jit(solution)/shard_map/all_gather | solution.py:167
  61.6 4.2 %fusion.33 = f32[512,256]{0,1:T(8,128)S(1)} fusion(bf16[512,4096]{1,0:T(8,128)(2,1)} %param.9, bf16[4096,256]{1,0:T(8,128)(2,1)} %all-gather.3.cloned.1.call-done), kind=kOutput, calls=%fused_computation.57 | convolution fusion | flops 1073741824 | bytes 6815744 | tf_op jit(solution)/shard_map/dot_general | solution.py:173
  67.0 11.8 %shard_map.93 = bf16[16,4,8,512]{3,2,1,0:T(8,128)(2,1)} custom-call(bf16[16,4,8,512]{3,2,1,0:T(8,128)(2,1)} %bitcast.88), custom_call_target="tpu_custom_call" | custom-call | tf_op jit(solution)/shard_map/pallas_call | solution.py:44
  78.8 1.6 gather_fusion
  80.6 11.8 %all_to_all.20 = bf16[8,4,8,512]{3,2,1,0:T(8,128)(2,1)S(1)} all-to-all(bf16[8,4,8,512]{3,2,1,0:T(8,128)(2,1)S(1)} %broadcast_select_fusion), channel_id=1, replica_groups=mesh['dp'=16,'expert'=8] {'expert'}, dimensions={0} | all-to-all | bytes 524288 | tf_op jit(solution)/shard_map/all_to_all | solution.py:187
  96.6 7.4 %shard_map.94 = (bf16[4,32,1024]{2,1,0:T(8,128)(2,1)}, bf16[4,32,1024]{2,1,0:T(8,128)(2,1)}) custom-call(bf16[32,1024]{1,0:T(8,128)(2,1)} %get-tuple-element.34.refs_0_, bf16[32,1024]{1,0:T(8,128)(2,1)} %get-tuple-element.33.refs_1_), custom_call_target="tpu_custom_call" | custom-call | tf_op jit(solution)/shard_map/pallas_call | solution.py:103
  104.0 18.7 %shard_map.95 = (bf16[4,4,32,1024]{3,2,1,0:T(8,128)(2,1)}, bf16[4,4,32,1024]{3,2,1,0:T(8,128)(2,1)}) custom-call(bf16[4,32,1024]{2,1,0:T(8,128)(2,1)} %get-tuple-element.21.refs_0_, bf16[4,32,1024]{2,1,0:T(8,128)(2,1)} %get-tuple-element.22.refs_1_), custom_call_target="tpu_custom_call" | custom-call | tf_op jit(solution)/shard_map/pallas_call | solution.py:103
  124.1 16.8 %all-gather.5.cloned.1.call-done = bf16[512,2048]{1,0:T(8,128)(2,1)} async-done(((bf16[32,2048]{1,0:T(8,128)(2,1)}), bf16[512,2048]{1,0:T(8,128)(2,1)}) %all-gather.5.cloned.1.call-update) | async-done | bytes 2097168 | tf_op jit(solution)/shard_map/all_gather | solution.py:190
  140.8 3.6 %fusion.4 = f32[512,512]{1,0:T(8,128)S(1)} fusion(bf16[512,2048]{1,0:T(8,128)(2,1)} %all-gather.5.cloned.1.call-done, bf16[1,4096,512]{2,1,0:T(8,128)(2,1)} %param.12), kind=kOutput, calls=%fused_computation.7 | convolution fusion | flops 1073741824 | bytes 5242880 | tf_op jit(solution)/shard_map/dot_general | solution.py:207
  148.8 7.5 %multiply_convert_fusion = bf16[512,4096]{1,0:T(8,128)(2,1)} fusion(bf16[1,512,4096]{2,1,0:T(8,128)(2,1)} %param.14, f32[512]{0:T(512)S(1)} %mul.19, f32[512,512]{1,0:T(8,128)S(1)} %convolution_add_fusion.2, bf16[512,1024]{1,0:T(8,128)(2,1)S(1)} %bitcast.81, bf16[1,4096,512]{2,1,0:T(8,128)(2,1)} %param.13, f32[512,512]{1,0:T(8,128)S(1)} %convolution_add_fusion.3), kind=kOutput, calls=%fused_computation.1 | convolution fusion | flops 2690383872 | bytes 12584960 | tf_op jit(solution)/shard_map/dot_general | solution.py:215
  156.3 4.0 %fusion.29 = (bf16[16,32,2048]{2,1,0:T(8,128)(2,1)}, bf16[16,32,2048]{2,1,0:T(8,128)(2,1)S(1)}) fusion(bf16[16,32,4096]{2,1,0:T(8,128)(2,1)} %bitcast.78), kind=kLoop, calls=%fused_computation.53 | loop fusion | bytes 8388608 | tf_op jit(solution)/shard_map/slice | solution.py:219
  162.6 18.6 %shard_map.96 = (bf16[4,4,32,1024]{3,2,1,0:T(8,128)(2,1)}, bf16[4,4,32,1024]{3,2,1,0:T(8,128)(2,1)}) custom-call(bf16[4,4,32,1024]{3,2,1,0:T(8,128)(2,1)} %copy.49.refs_0_, bf16[4,4,32,1024]{3,2,1,0:T(8,128)(2,1)} %get-tuple-element.31.refs_1_), custom_call_target="tpu_custom_call" | custom-call | tf_op jit(solution)/shard_map/pallas_call | solution.py:103
  181.2 2.2 reduce_sum.42.refs_0_
  183.4 2.2 reduce_sum.43.refs_1_
  185.6 7.4 %shard_map.97 = (bf16[4,32,1024]{2,1,0:T(8,128)(2,1)}, bf16[4,32,1024]{2,1,0:T(8,128)(2,1)}) custom-call(bf16[4,32,1024]{2,1,0:T(8,128)(2,1)} %reduce_sum.42.refs_0_, bf16[4,32,1024]{2,1,0:T(8,128)(2,1)} %reduce_sum.43.refs_1_), custom_call_target="tpu_custom_call" | custom-call | tf_op jit(solution)/shard_map/pallas_call | solution.py:103
  195.1 40.8 %reduce-scatter.4.cloned.1.call-done = bf16[1,32,2048]{2,1,0:T(8,128)(2,1)} async-done(((bf16[16,32,2048]{2,1,0:T(8,128)(2,1)}), bf16[1,32,2048]{2,1,0:T(8,128)(2,1)}) %reduce-scatter.4.cloned.1.call-update) | async-done | bytes 131088
  237.9 4.4 %all-to-all-start.1 = ((bf16[8,32,512]{2,1,0:T(8,128)(2,1)}), bf16[8,32,512]{2,1,0:T(8,128)(2,1)S(1)}, u32[]{:S(2)}, u32[]{:S(2)}) async-start(bf16[8,32,512]{2,1,0:T(8,128)(2,1)} %copy.50), calls=%async_computation.1 | async-start | bytes 524288 | tf_op jit(solution)/shard_map/all_to_all | solution.py:223
  242.6 7.3 %all-to-all-done.1 = bf16[8,32,512]{2,1,0:T(8,128)(2,1)S(1)} async-done(((bf16[8,32,512]{2,1,0:T(8,128)(2,1)}), bf16[8,32,512]{2,1,0:T(8,128)(2,1)S(1)}, u32[]{:S(2)}, u32[]{:S(2)}) %all-to-all-start.1) | async-done | bytes 262176 | tf_op jit(solution)/shard_map/all_to_all | solution.py:223
  251.3 12.6 %shard_map.98 = bf16[16,4,8,512]{3,2,1,0:T(8,128)(2,1)} custom-call(bf16[16,4,8,512]{3,2,1,0:T(8,128)(2,1)} %bitcast.89), custom_call_target="tpu_custom_call" | custom-call | tf_op jit(solution)/shard_map/pallas_call | solution.py:44
  263.9 1.9 copy.51
  (69 shorter events, 25.2 us)
Async XLA Ops:
  6.5 33.3 %copy-start.6 = (s32[8,4]{0,1:T(4,128)S(1)}, s32[8,4]{0,1:T(4,128)}, u32[]{:S(2)}) copy-start(s32[8,4]{0,1:T(4,128)} %param.16) | copy-start | bytes 388
  6.5 55.1 %all-gather.3.cloned.1.call-start = ((), (), s32[]{:S(2)}) async-start(), calls=%async_computation.3 | async-start | bytes 2228224 | tf_op jit(solution)/shard_map/all_gather | solution.py:167
  8.1 132.7 %all-gather.5.cloned.1.call-start = ((), (), s32[]{:S(2)}) async-start(), calls=%async_computation.4 | async-start | bytes 2228224 | tf_op jit(solution)/shard_map/all_gather | solution.py:190
  37.2 6.8 %copy-start.4 = (bf16[4,4,256,128]{3,2,1,0:T(8,128)(2,1)S(1)}, bf16[4,4,256,128]{3,2,1,0:T(8,128)(2,1)}, u32[]{:S(2)}) copy-start(bf16[4,4,256,128]{3,2,1,0:T(8,128)(2,1)} %get-tuple-element.19) | copy-start | bytes 3145732
  40.1 3.9 %copy-start = (bf16[512,4096]{1,0:T(8,128)(2,1)S(1)}, bf16[512,4096]{1,0:T(8,128)(2,1)}, u32[]{:S(2)}) copy-start(bf16[512,4096]{1,0:T(8,128)(2,1)} %param.9) | copy-start | bytes 12582916
  65.8 28.1 %copy-start.7 = (f32[1,512]{1,0:T(1,128)S(1)}, f32[1,512]{1,0:T(1,128)}, u32[]{:S(2)}) copy-start(f32[1,512]{1,0:T(1,128)} %param.15) | copy-start | bytes 6148
  65.8 28.8 %copy-start.9 = (s32[8]{0:T(128)S(1)}, s32[8]{0:T(128)}, u32[]{:S(2)}) copy-start(s32[8]{0:T(128)} %param.17) | copy-start | bytes 100
  93.0 142.9 %reduce-scatter.4.cloned.1.call-start = ((), (), s32[]{:S(2)}) async-start(), calls=%async_computation.5 | async-start | bytes 2228224
  124.1 20.4 %copy-start.1 = (bf16[4,4,32,1024]{3,2,1,0:T(8,128)(2,1)S(1)}, bf16[4,4,32,1024]{3,2,1,0:T(8,128)(2,1)}, u32[]{:S(2)}) copy-start(bf16[4,4,32,1024]{3,2,1,0:T(8,128)(2,1)} %get-tuple-element.23) | copy-start | bytes 3145732
  140.8 3.6 %copy-start.3 = (bf16[1,4096,512]{2,1,0:T(8,128)(2,1)S(1)}, bf16[1,4096,512]{2,1,0:T(8,128)(2,1)}, u32[]{:S(2)}) copy-start(bf16[1,4096,512]{2,1,0:T(8,128)(2,1)} %param.12) | copy-start | bytes 12582916
  140.8 4.7 %copy-start.5 = (bf16[1,4096,512]{2,1,0:T(8,128)(2,1)S(1)}, bf16[1,4096,512]{2,1,0:T(8,128)(2,1)}, u32[]{:S(2)}) copy-start(bf16[1,4096,512]{2,1,0:T(8,128)(2,1)} %param.13) | copy-start | bytes 12582916
  140.8 5.3 %copy-start.8 = (bf16[512,2048]{1,0:T(8,128)(2,1)S(1)}, bf16[512,2048]{1,0:T(8,128)(2,1)}, u32[]{:S(2)}) copy-start(bf16[512,2048]{1,0:T(8,128)(2,1)} %all-gather.5.cloned.1.call-done) | copy-start | bytes 6291460
  162.6 79.9 %copy-start.2 = (bf16[16,4,8,512]{3,2,1,0:T(8,128)(2,1)S(1)}, bf16[16,4,8,512]{3,2,1,0:T(8,128)(2,1)}, u32[]{:S(2)}) copy-start(bf16[16,4,8,512]{3,2,1,0:T(8,128)(2,1)} %shard_map.93) | copy-start | bytes 1572868
  237.9 12.0 %all-to-all-start.1 = ((bf16[8,32,512]{2,1,0:T(8,128)(2,1)}), bf16[8,32,512]{2,1,0:T(8,128)(2,1)S(1)}, u32[]{:S(2)}, u32[]{:S(2)}) async-start(bf16[8,32,512]{2,1,0:T(8,128)(2,1)} %copy.50), calls=%async_computation.1 | async-start | bytes 524288 | tf_op jit(solution)/shard_map/all_to_all | solution.py:223
Sparse Core Ops, SparseCore 0:
  9.5 52.0 all-gather.2
  93.2 47.6 all-gather.4
  160.5 75.3 reduce-scatter.3

commit v6 on v4

--- a/solution.py
+++ b/solution.py
@@ -11,12 +11,12 @@
 CAP = 4
 
 
-def _exchange_kernel(n, gather, x_ref, o_ref, local_sem, send_sems, recv_sems):
-    me = lax.axis_index("dp")
+def _exchange_kernel(n, gather, axis, x_ref, o_ref, local_sem, send_sems, recv_sems):
+    me = lax.axis_index(axis)
     mesh_id = pl.DeviceIdType.MESH
     barrier = pltpu.get_barrier_semaphore()
     for k in range(1, n):
-        pl.semaphore_signal(barrier, 1, device_id={"dp": lax.rem(me + k, n)}, device_id_type=mesh_id)
+        pl.semaphore_signal(barrier, 1, device_id={axis: lax.rem(me + k, n)}, device_id_type=mesh_id)
     pl.semaphore_wait(barrier, n - 1)
     local = pltpu.make_async_copy(x_ref if gather else x_ref.at[me], o_ref.at[me], local_sem)
     local.start()
@@ -28,7 +28,7 @@
             dst_ref=o_ref.at[me],
             send_sem=send_sems.at[k - 1],
             recv_sem=recv_sems.at[k - 1],
-            device_id={"dp": target},
+            device_id={axis: target},
             device_id_type=mesh_id,
         )
         copy.start()
@@ -38,11 +38,11 @@
         copy.wait()
 
 
-def dp_exchange(x, gather, cid):
-    n = lax.axis_size("dp")
+def dp_exchange(x, gather, cid, axis="dp"):
+    n = lax.axis_size(axis)
     shape = (n,) + x.shape if gather else x.shape
     return pl.pallas_call(
-        functools.partial(_exchange_kernel, n, gather),
+        functools.partial(_exchange_kernel, n, gather, axis),
         out_shape=jax.ShapeDtypeStruct(shape, x.dtype),
         in_specs=[pl.BlockSpec(memory_space=pl.ANY)],
         out_specs=pl.BlockSpec(memory_space=pl.ANY),
@@ -181,8 +181,8 @@
 
     slots = jnp.take(pieces, chosen_blocks.reshape(-1), axis=0)
     slots = slots.reshape(n_expert, CAP, piece, local_width)
-    mine = lax.all_to_all(slots, "expert", 0, 3, tiled=True)
-    mine = mine.reshape(CAP * piece, model_width)
+    mine = dp_exchange(slots, gather=False, cid=4, axis="expert")
+    mine = mine.transpose(1, 2, 0, 3).reshape(CAP * piece, model_width)
     picked_a, picked_b = all_gather_2d(mine, cid=20)
     picked_a = picked_a.reshape(n_dp * CAP * piece, -1)
     picked_b = picked_b.reshape(n_dp * CAP * piece, -1)
@@ -210,7 +210,7 @@
     summed = reduce_scatter_2d(part.reshape(n_dp, CAP * piece, model_width), cid=1)
     summed = summed.astype(jnp.bfloat16)
     summed = summed.reshape(CAP * piece, n_expert, local_width).transpose(1, 0, 2)
-    outs = lax.all_to_all(summed, "expert", 0, 0, tiled=True)
+    outs = dp_exchange(summed, gather=False, cid=5, axis="expert")
     outs = outs.reshape(n_expert * CAP, piece * local_width)
 
     selector = chosen_blocks.reshape(-1)[None, :] == jnp.arange(n_blocks)[:, None]

time: 236 us -> 233 us (0.987)
  Pallas kernels: 163 us -> 181 us
  waiting for transfers between devices: 11.8 us -> 0 us
  starting transfers between devices: 8.72 us -> 0 us
    pallas_call x2 -> x4, Pallas kernels: 25.1 us -> 42.7 us  [dp_exchange(): pl.pallas_call(functools.partial(_exchange_kernel, n, gather, axis), out_...]
    all_to_all x2 -> x0, waiting for transfers between devices: 11.8 us -> none  [the longest x1 7.18 us: body(): outs = lax.all_to_all(summed, 'expert', 0, 0, tiled=True)]
    all_to_all x2 -> x0, starting transfers between devices: 8.72 us -> none  [the longest x1 5.31 us: body(): mine = lax.all_to_all(slots, 'expert', 0, 3, tiled=True)]
    unnamed x25 -> x27, local copies, waits for them, and re-layouts: 5.77 us -> 5.36 us
  transfers between devices with their start and end apart: 2 -> 0, of which waited for: 2 -> 0; matrix products, arithmetic and copies ran while one was open for 1% -> 0% of each run, Pallas kernels for 0% -> 0%
where the time goes in v6:
time: 233 us; the launch traced here: 232 us
  Pallas kernels  181 us (78%)
  local copies, waits for them, and re-layouts  25 us (11%)
  matrix products  16.3 us (7%)
  other arithmetic  9.72 us (4%)
    pallas_call x6, Pallas kernels, dp_route(): pl.pallas_call(functools.partial(_route_kernel, tuple(strides), side, gat...  138 us
    pallas_call x4, Pallas kernels, dp_exchange(): pl.pallas_call(functools.partial(_exchange_kernel, n, gather, axis), out_...  42.7 us
    dot_general x1, matrix products, body(): part = jnp.dot(hidden, w_down, preferred_element_type=jnp.float32)  8.69 us
    unnamed x27, local copies, waits for them, and re-layouts  5.36 us

profile of v6, /device:TPU:24, one launch (start us, length us, event | category | flops | bytes accessed | tf_op | source)
XLA Modules:
  0.0 232.1 jit_solution(7987787514408580872)
XLA Ops:
  0.0 1.7 fusion.39
  1.7 12.2 %shard_map.91 = (bf16[4,256,256]{2,1,0:T(8,128)(2,1)}, bf16[4,256,256]{2,1,0:T(8,128)(2,1)}) custom-call(bf16[256,256]{1,0:T(8,128)(2,1)} %get-tuple-element.34.refs_0_, bf16[256,256]{1,0:T(8,128)(2,1)} %get-tuple-element.33.refs_1_), custom_call_target="tpu_custom_call" | custom-call | tf_op jit(solution)/shard_map/pallas_call | solution.py:103
  13.9 34.4 %shard_map.92 = (bf16[4,4,256,256]{3,2,1,0:T(8,128)(2,1)}, bf16[4,4,256,256]{3,2,1,0:T(8,128)(2,1)}) custom-call(bf16[4,256,256]{2,1,0:T(8,128)(2,1)} %get-tuple-element.17.refs_0_, bf16[4,256,256]{2,1,0:T(8,128)(2,1)} %get-tuple-element.18.refs_1_), custom_call_target="tpu_custom_call" | custom-call | tf_op jit(solution)/shard_map/pallas_call | solution.py:103
  48.3 1.9 copy.17
  51.1 1.3 convolution_bitcast_fusion
  52.7 1.3 convolution_bitcast_fusion.1
  55.5 12.4 %shard_map.93 = bf16[16,4,8,512]{3,2,1,0:T(8,128)(2,1)} custom-call(bf16[16,4,8,512]{3,2,1,0:T(8,128)(2,1)} %bitcast.87), custom_call_target="tpu_custom_call" | custom-call | tf_op jit(solution)/shard_map/pallas_call | solution.py:44
  68.1 1.6 gather_fusion
  70.7 9.4 %shard_map.94 = bf16[8,4,8,512]{3,2,1,0:T(8,128)(2,1)} custom-call(bf16[8,4,8,512]{3,2,1,0:T(8,128)(2,1)} %broadcast_select_fusion.x_ref), custom_call_target="tpu_custom_call" | custom-call | tf_op jit(solution)/shard_map/pallas_call | solution.py:44
  81.8 11.3 %shard_map.95 = (bf16[4,32,2048]{2,1,0:T(8,128)(2,1)}, bf16[4,32,2048]{2,1,0:T(8,128)(2,1)}) custom-call(bf16[32,2048]{1,0:T(8,128)(2,1)} %get-tuple-element.32.refs_0_, bf16[32,2048]{1,0:T(8,128)(2,1)} %get-tuple-element.31.refs_1_), custom_call_target="tpu_custom_call" | custom-call | tf_op jit(solution)/shard_map/pallas_call | solution.py:103
  93.0 34.6 %shard_map.96 = (bf16[4,4,32,2048]{3,2,1,0:T(8,128)(2,1)}, bf16[4,4,32,2048]{3,2,1,0:T(8,128)(2,1)}) custom-call(bf16[4,32,2048]{2,1,0:T(8,128)(2,1)} %get-tuple-element.21.refs_0_, bf16[4,32,2048]{2,1,0:T(8,128)(2,1)} %get-tuple-element.22.refs_1_), custom_call_target="tpu_custom_call" | custom-call | tf_op jit(solution)/shard_map/pallas_call | solution.py:103
  127.6 1.9 copy.24
  132.0 1.3 fusion.14
  134.2 2.2 fusion.2
  139.2 8.7 %multiply_convert_fusion = bf16[512,4096]{1,0:T(8,128)(2,1)} fusion(bf16[1,512,4096]{2,1,0:T(8,128)(2,1)} %param.14, f32[512]{0:T(512)S(1)} %mul.19, f32[512,512]{1,0:T(8,128)} %fusion.2, bf16[512,2048]{1,0:T(8,128)(2,1)S(1)} %bitcast.97, bf16[1,4096,512]{2,1,0:T(8,128)(2,1)} %param.13, f32[512,512]{1,0:T(8,128)S(1)} %fusion.14), kind=kOutput, calls=%fused_computation.1 | convolution fusion | flops 3227254784 | bytes 14682112 | tf_op jit(solution)/shard_map/dot_general | solution.py:207
  147.9 4.1 %fusion.37 = (bf16[4,4,32,2048]{3,2,1,0:T(8,128)(2,1)}, bf16[4,4,32,2048]{3,2,0,1:T(8,128)(2,1)S(1)}) fusion(bf16[4,4,32,4096]{3,2,1,0:T(8,128)(2,1)} %bitcast.77), kind=kLoop, calls=%fused_computation.51 | loop fusion | bytes 8388608 | tf_op jit(solution)/shard_map/slice | solution.py:123
  152.0 1.6 copy.26.refs_0_
  153.6 35.1 %shard_map.97 = (bf16[4,4,32,2048]{3,2,1,0:T(8,128)(2,1)}, bf16[4,4,32,2048]{3,2,1,0:T(8,128)(2,1)}) custom-call(bf16[4,4,32,2048]{3,2,1,0:T(8,128)(2,1)} %copy.26.refs_0_, bf16[4,4,32,2048]{3,2,1,0:T(8,128)(2,1)} %get-tuple-element.29.refs_1_), custom_call_target="tpu_custom_call" | custom-call | tf_op jit(solution)/shard_map/pallas_call | solution.py:103
  188.7 3.1 %reduce_sum.42.refs_0_ = bf16[4,32,2048]{2,1,0:T(8,128)(2,1)} reduce(bf16[4,4,32,2048]{3,2,1,0:T(8,128)(2,1)} %get-tuple-element.25, bf16[]{:T(256)} %constant.63.clone.1), dimensions={0}, to_apply=%region_0.1 | reduce | flops 786432 | bytes 2621442 | tf_op jit(solution)/shard_map/reduce_sum | solution.py:125
  191.8 1.3 reduce_sum.43.refs_1_
  193.1 10.6 %shard_map.98 = (bf16[4,32,2048]{2,1,0:T(8,128)(2,1)}, bf16[4,32,2048]{2,1,0:T(8,128)(2,1)}) custom-call(bf16[4,32,2048]{2,1,0:T(8,128)(2,1)} %reduce_sum.42.refs_0_, bf16[4,32,2048]{2,1,0:T(8,128)(2,1)} %reduce_sum.43.refs_1_), custom_call_target="tpu_custom_call" | custom-call | tf_op jit(solution)/shard_map/pallas_call | solution.py:103
  206.7 7.4 %shard_map.99 = bf16[8,32,512]{2,1,0:T(8,128)(2,1)} custom-call(bf16[8,32,512]{2,1,0:T(8,128)(2,1)} %maximum_bitcast_fusion.x_ref), custom_call_target="tpu_custom_call" | custom-call | tf_op jit(solution)/shard_map/pallas_call | solution.py:44
  216.8 13.4 %shard_map.100 = bf16[16,4,8,512]{3,2,1,0:T(8,128)(2,1)} custom-call(bf16[16,4,8,512]{3,2,1,0:T(8,128)(2,1)} %bitcast.88), custom_call_target="tpu_custom_call" | custom-call | tf_op jit(solution)/shard_map/pallas_call | solution.py:44
  230.2 1.9 copy.29
  (52 shorter events, 17.2 us)
Async XLA Ops:
  48.3 2.8 %copy-start.5 = (bf16[512,4096]{1,0:T(8,128)(2,1)S(1)}, bf16[512,4096]{1,0:T(8,128)(2,1)}, u32[]{:S(2)}) copy-start(bf16[512,4096]{1,0:T(8,128)(2,1)} %param.9) | copy-start | bytes 12582916
  51.1 1.6 copy-start.9
  52.7 1.3 copy-start.2
  54.4 13.5 %copy-start.3 = (s32[8,4]{0,1:T(4,128)S(1)}, s32[8,4]{0,1:T(4,128)}, u32[]{:S(2)}) copy-start(s32[8,4]{0,1:T(4,128)} %param.16) | copy-start | bytes 388
  127.6 2.8 %copy-start.6 = (bf16[1,4096,512]{2,1,0:T(8,128)(2,1)S(1)}, bf16[1,4096,512]{2,1,0:T(8,128)(2,1)}, u32[]{:S(2)}) copy-start(bf16[1,4096,512]{2,1,0:T(8,128)(2,1)} %param.12) | copy-start | bytes 12582916
  130.4 1.6 copy-start.8
  132.0 2.2 copy-start.7
  134.2 2.2 copy-start.10
  134.2 3.4 %copy-start.4 = (f32[1,512]{1,0:T(1,128)S(1)}, f32[1,512]{1,0:T(1,128)}, u32[]{:S(2)}) copy-start(f32[1,512]{1,0:T(1,128)} %param.15) | copy-start | bytes 6148
  188.7 3.1 %copy-start.1 = (bf16[4,4,32,2048]{3,2,1,0:T(8,128)(2,1)S(1)}, bf16[4,4,32,2048]{3,2,1,0:T(8,128)(2,1)}, u32[]{:S(2)}) copy-start(bf16[4,4,32,2048]{3,2,1,0:T(8,128)(2,1)} %get-tuple-element.26) | copy-start | bytes 6291460
  193.1 22.2 %copy-start = (bf16[16,4,8,512]{3,2,1,0:T(8,128)(2,1)S(1)}, bf16[16,4,8,512]{3,2,1,0:T(8,128)(2,1)}, u32[]{:S(2)}) copy-start(bf16[16,4,8,512]{3,2,1,0:T(8,128)(2,1)} %shard_map.93) | copy-start | bytes 1572868

commit v7 on v6

--- a/solution.py
+++ b/solution.py
@@ -130,11 +130,89 @@
     return jnp.concatenate([total_a, total_b], axis=-1)
 
 
+def _ring_gather_kernel(strides, side, *refs):
+    n_in = len(strides)
+    ins, outs = refs[:n_in], refs[n_in:2 * n_in]
+    local_sems, send_sems, recv_sems = refs[2 * n_in:]
+    me = lax.axis_index("dp")
+    mesh_id = pl.DeviceIdType.MESH
+    geo = []
+    for r, stride in enumerate(strides):
+        coord = lax.rem(me // stride, side)
+        base = me - coord * stride
+        plus = lax.rem(coord + 1, side)
+        minus = lax.rem(coord + side - 1, side)
+        far = lax.rem(coord + 2, side)
+        geo.append((coord, plus, minus, far, base + plus * stride, base + minus * stride))
+    barrier = pltpu.get_barrier_semaphore()
+    for _, _, _, _, to_plus, to_minus in geo:
+        pl.semaphore_signal(barrier, 1, device_id={"dp": to_plus}, device_id_type=mesh_id)
+        pl.semaphore_signal(barrier, 1, device_id={"dp": to_minus}, device_id_type=mesh_id)
+    pl.semaphore_wait(barrier, 2 * n_in)
+
+    def remote(r, src, dst, slot, target):
+        return pltpu.make_async_remote_copy(
+            src_ref=src,
+            dst_ref=dst,
+            send_sem=send_sems.at[r, slot],
+            recv_sem=recv_sems.at[r, slot],
+            device_id={"dp": target},
+            device_id_type=mesh_id,
+        )
+
+    started, locals_ = [], []
+    for r, (coord, plus, minus, far, to_plus, to_minus) in enumerate(geo):
+        local = pltpu.make_async_copy(ins[r], outs[r].at[coord], local_sems.at[r])
+        local.start()
+        locals_.append(local)
+        for slot, target in ((0, to_plus), (1, to_minus)):
+            copy = remote(r, ins[r], outs[r].at[coord], slot, target)
+            copy.start()
+            started.append(copy)
+    finals = []
+    for r, (coord, plus, minus, far, to_plus, to_minus) in enumerate(geo):
+        half = outs[r].shape[1] // 2
+        rest = outs[r].shape[1] - half
+        first = pl.ds(0, half)
+        second = pl.ds(half, rest)
+        remote(r, ins[r], outs[r].at[minus], 0, to_minus).wait_recv()
+        onward = remote(r, outs[r].at[minus, first], outs[r].at[minus, first], 2, to_plus)
+        onward.start()
+        started.append(onward)
+        remote(r, ins[r], outs[r].at[plus], 1, to_plus).wait_recv()
+        onward = remote(r, outs[r].at[plus, second], outs[r].at[plus, second], 3, to_minus)
+        onward.start()
+        started.append(onward)
+        finals.append(remote(r, outs[r].at[far, first], outs[r].at[far, first], 2, to_minus))
+        finals.append(remote(r, outs[r].at[far, second], outs[r].at[far, second], 3, to_plus))
+    for copy in finals:
+        copy.wait_recv()
+    for local in locals_:
+        local.wait()
+    for copy in started:
+        copy.wait_send()
+
+
+def ring_gather(xs, strides, cid, side=4):
+    return pl.pallas_call(
+        functools.partial(_ring_gather_kernel, tuple(strides), side),
+        out_shape=[jax.ShapeDtypeStruct((side,) + x.shape, x.dtype) for x in xs],
+        in_specs=[pl.BlockSpec(memory_space=pl.ANY)] * len(xs),
+        out_specs=[pl.BlockSpec(memory_space=pl.ANY)] * len(xs),
+        scratch_shapes=[
+            pltpu.SemaphoreType.DMA((len(xs),)),
+            pltpu.SemaphoreType.DMA((len(xs), 4)),
+            pltpu.SemaphoreType.DMA((len(xs), 4)),
+        ],
+        compiler_params=pltpu.CompilerParams(collective_id=cid, has_side_effects=True),
+    )(*xs)
+
+
 def all_gather_2d(x, cid):
     side = 4
     half = x.shape[-1] // 2
-    got_a, got_b = dp_route([x[..., :half], x[..., half:]], (1, side), cid, gather=True)
-    got_a, got_b = dp_route([got_a, got_b], (side, 1), cid + 1, gather=True)
+    got_a, got_b = ring_gather([x[..., :half], x[..., half:]], (1, side), cid)
+    got_a, got_b = ring_gather([got_a, got_b], (side, 1), cid + 1)
     n = side * side
     got_a = got_a.reshape((n,) + got_a.shape[2:])
     perm = (1, 0) + tuple(range(2, got_b.ndim))

time: 233 us -> 233 us (level)
    pallas_call x0 -> x4, Pallas kernels: none -> 92.5 us  [ring_gather(): pl.pallas_call(functools.partial(_ring_gather_kernel, tuple(strides), sid...]
    pallas_call x6 -> x2, Pallas kernels: 138 us -> 45.7 us  [dp_route(): pl.pallas_call(functools.partial(_route_kernel, tuple(strides), side, gat...]
where the time goes in v7:
time: 233 us; the launch traced here: 232 us
  Pallas kernels  181 us (78%)
  local copies, waits for them, and re-layouts  25 us (11%)
  matrix products  16.3 us (7%)
  other arithmetic  9.72 us (4%)
    pallas_call x4, Pallas kernels, ring_gather(): pl.pallas_call(functools.partial(_ring_gather_kernel, tuple(strides), sid...  92.5 us
    pallas_call x2, Pallas kernels, dp_route(): pl.pallas_call(functools.partial(_route_kernel, tuple(strides), side, gat...  45.7 us
    pallas_call x4, Pallas kernels, dp_exchange(): pl.pallas_call(functools.partial(_exchange_kernel, n, gather, axis), out_...  42.8 us
    dot_general x1, matrix products, body(): part = jnp.dot(hidden, w_down, preferred_element_type=jnp.float32)  8.69 us
    unnamed x27, local copies, waits for them, and re-layouts  5.37 us

profile of v7, /device:TPU:24, one launch (start us, length us, event | category | flops | bytes accessed | tf_op | source)
XLA Modules:
  0.0 232.2 jit_solution(11501566166273434704)
XLA Ops:
  0.0 1.7 fusion.39
  1.7 12.3 %shard_map.91 = (bf16[4,256,256]{2,1,0:T(8,128)(2,1)}, bf16[4,256,256]{2,1,0:T(8,128)(2,1)}) custom-call(bf16[256,256]{1,0:T(8,128)(2,1)} %get-tuple-element.34.refs_0_, bf16[256,256]{1,0:T(8,128)(2,1)} %get-tuple-element.33.refs_1_), custom_call_target="tpu_custom_call" | custom-call | tf_op jit(solution)/shard_map/pallas_call | solution.py:197
  14.0 34.0 %shard_map.92 = (bf16[4,4,256,256]{3,2,1,0:T(8,128)(2,1)}, bf16[4,4,256,256]{3,2,1,0:T(8,128)(2,1)}) custom-call(bf16[4,256,256]{2,1,0:T(8,128)(2,1)} %get-tuple-element.17.refs_0_, bf16[4,256,256]{2,1,0:T(8,128)(2,1)} %get-tuple-element.18.refs_1_), custom_call_target="tpu_custom_call" | custom-call | tf_op jit(solution)/shard_map/pallas_call | solution.py:197
  48.0 1.9 copy.17
  50.8 1.3 convolution_bitcast_fusion
  52.4 1.3 convolution_bitcast_fusion.1
  55.1 12.4 %shard_map.93 = bf16[16,4,8,512]{3,2,1,0:T(8,128)(2,1)} custom-call(bf16[16,4,8,512]{3,2,1,0:T(8,128)(2,1)} %bitcast.87), custom_call_target="tpu_custom_call" | custom-call | tf_op jit(solution)/shard_map/pallas_call | solution.py:44
  67.7 1.6 gather_fusion
  70.3 9.4 %shard_map.94 = bf16[8,4,8,512]{3,2,1,0:T(8,128)(2,1)} custom-call(bf16[8,4,8,512]{3,2,1,0:T(8,128)(2,1)} %broadcast_select_fusion.x_ref), custom_call_target="tpu_custom_call" | custom-call | tf_op jit(solution)/shard_map/pallas_call | solution.py:44
  81.4 11.8 %shard_map.95 = (bf16[4,32,2048]{2,1,0:T(8,128)(2,1)}, bf16[4,32,2048]{2,1,0:T(8,128)(2,1)}) custom-call(bf16[32,2048]{1,0:T(8,128)(2,1)} %get-tuple-element.32.refs_0_, bf16[32,2048]{1,0:T(8,128)(2,1)} %get-tuple-element.31.refs_1_), custom_call_target="tpu_custom_call" | custom-call | tf_op jit(solution)/shard_map/pallas_call | solution.py:197
  93.2 34.4 %shard_map.96 = (bf16[4,4,32,2048]{3,2,1,0:T(8,128)(2,1)}, bf16[4,4,32,2048]{3,2,1,0:T(8,128)(2,1)}) custom-call(bf16[4,32,2048]{2,1,0:T(8,128)(2,1)} %get-tuple-element.21.refs_0_, bf16[4,32,2048]{2,1,0:T(8,128)(2,1)} %get-tuple-element.22.refs_1_), custom_call_target="tpu_custom_call" | custom-call | tf_op jit(solution)/shard_map/pallas_call | solution.py:197
  127.7 1.9 copy.24
  132.1 1.2 fusion.14
  134.3 2.2 fusion.2
  139.3 8.7 %multiply_convert_fusion = bf16[512,4096]{1,0:T(8,128)(2,1)} fusion(bf16[1,512,4096]{2,1,0:T(8,128)(2,1)} %param.14, f32[512]{0:T(512)S(1)} %mul.19, f32[512,512]{1,0:T(8,128)} %fusion.2, bf16[512,2048]{1,0:T(8,128)(2,1)S(1)} %bitcast.97, bf16[1,4096,512]{2,1,0:T(8,128)(2,1)} %param.13, f32[512,512]{1,0:T(8,128)S(1)} %fusion.14), kind=kOutput, calls=%fused_computation.1 | convolution fusion | flops 3227254784 | bytes 14682112 | tf_op jit(solution)/shard_map/dot_general | solution.py:285
  148.0 4.1 %fusion.37 = (bf16[4,4,32,2048]{3,2,1,0:T(8,128)(2,1)}, bf16[4,4,32,2048]{3,2,0,1:T(8,128)(2,1)S(1)}) fusion(bf16[4,4,32,4096]{3,2,1,0:T(8,128)(2,1)} %bitcast.77), kind=kLoop, calls=%fused_computation.51 | loop fusion | bytes 8388608 | tf_op jit(solution)/shard_map/slice | solution.py:123
  152.0 1.6 copy.26.refs_0_
  153.6 35.0 %shard_map.97 = (bf16[4,4,32,2048]{3,2,1,0:T(8,128)(2,1)}, bf16[4,4,32,2048]{3,2,1,0:T(8,128)(2,1)}) custom-call(bf16[4,4,32,2048]{3,2,1,0:T(8,128)(2,1)} %copy.26.refs_0_, bf16[4,4,32,2048]{3,2,1,0:T(8,128)(2,1)} %get-tuple-element.29.refs_1_), custom_call_target="tpu_custom_call" | custom-call | tf_op jit(solution)/shard_map/pallas_call | solution.py:103
  188.6 3.1 %reduce_sum.42.refs_0_ = bf16[4,32,2048]{2,1,0:T(8,128)(2,1)} reduce(bf16[4,4,32,2048]{3,2,1,0:T(8,128)(2,1)} %get-tuple-element.25, bf16[]{:T(256)} %constant.63.clone.1), dimensions={0}, to_apply=%region_0.1 | reduce | flops 786432 | bytes 2621442 | tf_op jit(solution)/shard_map/reduce_sum | solution.py:125
  191.7 1.3 reduce_sum.43.refs_1_
  193.0 10.7 %shard_map.98 = (bf16[4,32,2048]{2,1,0:T(8,128)(2,1)}, bf16[4,32,2048]{2,1,0:T(8,128)(2,1)}) custom-call(bf16[4,32,2048]{2,1,0:T(8,128)(2,1)} %reduce_sum.42.refs_0_, bf16[4,32,2048]{2,1,0:T(8,128)(2,1)} %reduce_sum.43.refs_1_), custom_call_target="tpu_custom_call" | custom-call | tf_op jit(solution)/shard_map/pallas_call | solution.py:103
  206.8 7.4 %shard_map.99 = bf16[8,32,512]{2,1,0:T(8,128)(2,1)} custom-call(bf16[8,32,512]{2,1,0:T(8,128)(2,1)} %maximum_bitcast_fusion.x_ref), custom_call_target="tpu_custom_call" | custom-call | tf_op jit(solution)/shard_map/pallas_call | solution.py:44
  216.8 13.5 %shard_map.100 = bf16[16,4,8,512]{3,2,1,0:T(8,128)(2,1)} custom-call(bf16[16,4,8,512]{3,2,1,0:T(8,128)(2,1)} %bitcast.88), custom_call_target="tpu_custom_call" | custom-call | tf_op jit(solution)/shard_map/pallas_call | solution.py:44
  230.3 1.9 copy.29
  (52 shorter events, 17.2 us)
Async XLA Ops:
  47.9 2.8 %copy-start.5 = (bf16[512,4096]{1,0:T(8,128)(2,1)S(1)}, bf16[512,4096]{1,0:T(8,128)(2,1)}, u32[]{:S(2)}) copy-start(bf16[512,4096]{1,0:T(8,128)(2,1)} %param.9) | copy-start | bytes 12582916
  50.8 1.6 copy-start.9
  52.4 1.3 copy-start.2
  54.1 13.5 %copy-start.3 = (s32[8,4]{0,1:T(4,128)S(1)}, s32[8,4]{0,1:T(4,128)}, u32[]{:S(2)}) copy-start(s32[8,4]{0,1:T(4,128)} %param.16) | copy-start | bytes 388
  127.7 2.8 %copy-start.6 = (bf16[1,4096,512]{2,1,0:T(8,128)(2,1)S(1)}, bf16[1,4096,512]{2,1,0:T(8,128)(2,1)}, u32[]{:S(2)}) copy-start(bf16[1,4096,512]{2,1,0:T(8,128)(2,1)} %param.12) | copy-start | bytes 12582916
  130.5 1.6 copy-start.8
  132.1 2.2 copy-start.7
  134.3 2.2 copy-start.10
  134.3 3.4 %copy-start.4 = (f32[1,512]{1,0:T(1,128)S(1)}, f32[1,512]{1,0:T(1,128)}, u32[]{:S(2)}) copy-start(f32[1,512]{1,0:T(1,128)} %param.15) | copy-start | bytes 6148
  188.6 3.1 %copy-start.1 = (bf16[4,4,32,2048]{3,2,1,0:T(8,128)(2,1)S(1)}, bf16[4,4,32,2048]{3,2,1,0:T(8,128)(2,1)}, u32[]{:S(2)}) copy-start(bf16[4,4,32,2048]{3,2,1,0:T(8,128)(2,1)} %get-tuple-element.26) | copy-start | bytes 6291460
  193.0 22.3 %copy-start = (bf16[16,4,8,512]{3,2,1,0:T(8,128)(2,1)S(1)}, bf16[16,4,8,512]{3,2,1,0:T(8,128)(2,1)}, u32[]{:S(2)}) copy-start(bf16[16,4,8,512]{3,2,1,0:T(8,128)(2,1)} %shard_map.93) | copy-start | bytes 1572868

commit v8 on v7

--- a/solution.py
+++ b/solution.py
@@ -208,11 +208,93 @@
     )(*xs)
 
 
+def _gather_2d_kernel(side, *refs):
+    routes = ((1, side), (side, 1))
+    ins, outs = refs[:2], refs[2:4]
+    local_sems, send_sems, recv_sems = refs[4:]
+    me = lax.axis_index("dp")
+    mesh_id = pl.DeviceIdType.MESH
+
+    def coords(stride):
+        coord = lax.rem(me // stride, side)
+        return coord, me - coord * stride
+
+    barrier = pltpu.get_barrier_semaphore()
+    for stride in (1, side):
+        coord, base = coords(stride)
+        for k in range(1, side):
+            peer = base + lax.rem(coord + k, side) * stride
+            pl.semaphore_signal(barrier, 1, device_id={"dp": peer}, device_id_type=mesh_id)
+    pl.semaphore_wait(barrier, 2 * (side - 1))
+
+    def remote(r, src, dst, slot, target):
+        return pltpu.make_async_remote_copy(
+            src_ref=src,
+            dst_ref=dst,
+            send_sem=send_sems.at[r, slot],
+            recv_sem=recv_sems.at[r, slot],
+            device_id={"dp": target},
+            device_id_type=mesh_id,
+        )
+
+    started, locals_, waits = [], [], []
+    for r, (first, second) in enumerate(routes):
+        c1, base1 = coords(first)
+        c2, base2 = coords(second)
+        out = outs[r]
+        local = pltpu.make_async_copy(ins[r], out.at[c2, c1], local_sems.at[r])
+        local.start()
+        locals_.append(local)
+        for k in range(1, side):
+            copy = remote(r, ins[r], out.at[c2, c1], k - 1, base1 + lax.rem(c1 + k, side) * first)
+            copy.start()
+            started.append(copy)
+        for k in range(1, side):
+            slot = (side - 1) + (k - 1) * side
+            target = base2 + lax.rem(c2 + k, side) * second
+            copy = remote(r, ins[r], out.at[c2, c1], slot + 0, target)
+            copy.start()
+            started.append(copy)
+        for j in range(1, side):
+            held = lax.rem(c1 + side - j, side)
+            remote(r, ins[r], out.at[c2, held], j - 1, base1 + held * first).wait_recv()
+            for k in range(1, side):
+                slot = (side - 1) + (k - 1) * side + j
+                target = base2 + lax.rem(c2 + k, side) * second
+                copy = remote(r, out.at[c2, held], out.at[c2, held], slot, target)
+                copy.start()
+                started.append(copy)
+        for k in range(1, side):
+            source = lax.rem(c2 + side - k, side)
+            for j in range(side):
+                slot = (side - 1) + (k - 1) * side + j
+                held = lax.rem(c1 + side - j, side)
+                waits.append(remote(r, out.at[source, held], out.at[source, held], slot, base2 + source * second))
+    for copy in waits:
+        copy.wait_recv()
+    for local in locals_:
+        local.wait()
+    for copy in started:
+        copy.wait_send()
+
+
 def all_gather_2d(x, cid):
     side = 4
     half = x.shape[-1] // 2
-    got_a, got_b = ring_gather([x[..., :half], x[..., half:]], (1, side), cid)
-    got_a, got_b = ring_gather([got_a, got_b], (side, 1), cid + 1)
+    parts = [x[..., :half], x[..., half:]]
+    n_slots = (side - 1) * (side + 1)
+    got_a, got_b = pl.pallas_call(
+        functools.partial(_gather_2d_kernel, side),
+        out_shape=[jax.ShapeDtypeStruct((side, side) + p.shape, p.dtype) for p in parts],
+        in_specs=[pl.BlockSpec(memory_space=pl.ANY)] * 2,
+        out_specs=[pl.BlockSpec(memory_space=pl.ANY)] * 2,
+        scratch_shapes=[
+            pltpu.SemaphoreType.DMA((2,)),
+            pltpu.SemaphoreType.DMA((2, n_slots)),
+            pltpu.SemaphoreType.DMA((2, n_slots)),
+        ],
+        compiler_params=pltpu.CompilerParams(collective_id=cid, has_side_effects=True),
+    )(*parts)
     n = side * side
     got_a = got_a.reshape((n,) + got_a.shape[2:])
     perm = (1, 0) + tuple(range(2, got_b.ndim))

time: 233 us -> 239 us (1.026)
  Pallas kernels: 181 us -> 187 us
    pallas_call x4 -> x2, Pallas kernels: 92.5 us -> 98.9 us  [all_gather_2d(): pl.pallas_call(functools.partial(_gather_2d_kernel, side), out_shape=[jax...]
where the time goes in v8:
time: 239 us; the launch traced here: 238 us
  Pallas kernels  187 us (78%)
  local copies, waits for them, and re-layouts  24.9 us (10%)
  matrix products  16.3 us (7%)
  other arithmetic  9.66 us (4%)
    pallas_call x2, Pallas kernels, all_gather_2d(): pl.pallas_call(functools.partial(_gather_2d_kernel, side), out_shape=[jax...  98.9 us
    pallas_call x2, Pallas kernels, dp_route(): pl.pallas_call(functools.partial(_route_kernel, tuple(strides), side, gat...  46.6 us
    pallas_call x4, Pallas kernels, dp_exchange(): pl.pallas_call(functools.partial(_exchange_kernel, n, gather, axis), out_...  41.5 us
    dot_general x1, matrix products, body(): part = jnp.dot(hidden, w_down, preferred_element_type=jnp.float32)  8.68 us
    unnamed x27, local copies, waits for them, and re-layouts  5.35 us

profile of v8, /device:TPU:24, one launch (start us, length us, event | category | flops | bytes accessed | tf_op | source)
XLA Modules:
  0.0 238.1 jit_solution(8784484199680866330)
XLA Ops:
  0.0 1.7 fusion.39
  1.7 50.1 %shard_map.91 = (bf16[4,4,256,256]{3,2,1,0:T(8,128)(2,1)}, bf16[4,4,256,256]{3,2,1,0:T(8,128)(2,1)}) custom-call(bf16[256,256]{1,0:T(8,128)(2,1)} %get-tuple-element.26.refs_0_, bf16[256,256]{1,0:T(8,128)(2,1)} %get-tuple-element.25.refs_1_), custom_call_target="tpu_custom_call" | custom-call | tf_op jit(solution)/shard_map/pallas_call | solution.py:286
  51.8 1.9 copy.17
  54.6 1.3 convolution_bitcast_fusion
  56.2 1.3 convolution_bitcast_fusion.1
  59.0 11.2 %shard_map.92 = bf16[16,4,8,512]{3,2,1,0:T(8,128)(2,1)} custom-call(bf16[16,4,8,512]{3,2,1,0:T(8,128)(2,1)} %bitcast.87), custom_call_target="tpu_custom_call" | custom-call | tf_op jit(solution)/shard_map/pallas_call | solution.py:44
  70.4 1.6 gather_fusion
  73.0 9.4 %shard_map.93 = bf16[8,4,8,512]{3,2,1,0:T(8,128)(2,1)} custom-call(bf16[8,4,8,512]{3,2,1,0:T(8,128)(2,1)} %broadcast_select_fusion.x_ref), custom_call_target="tpu_custom_call" | custom-call | tf_op jit(solution)/shard_map/pallas_call | solution.py:44
  84.1 48.8 %shard_map.94 = (bf16[4,4,32,2048]{3,2,1,0:T(8,128)(2,1)}, bf16[4,4,32,2048]{3,2,1,0:T(8,128)(2,1)}) custom-call(bf16[32,2048]{1,0:T(8,128)(2,1)} %get-tuple-element.24.refs_0_, bf16[32,2048]{1,0:T(8,128)(2,1)} %get-tuple-element.23.refs_1_), custom_call_target="tpu_custom_call" | custom-call | tf_op jit(solution)/shard_map/pallas_call | solution.py:286
  132.9 1.9 copy.24
  135.7 1.2 fusion.6
  137.3 1.3 fusion.14
  139.5 2.2 fusion.2
  144.4 8.7 %multiply_convert_fusion = bf16[512,4096]{1,0:T(8,128)(2,1)} fusion(bf16[1,512,4096]{2,1,0:T(8,128)(2,1)} %param.14, f32[512]{0:T(512)S(1)} %mul.19, f32[512,512]{1,0:T(8,128)} %fusion.2, bf16[512,2048]{1,0:T(8,128)(2,1)S(1)} %bitcast.97, bf16[1,4096,512]{2,1,0:T(8,128)(2,1)} %param.13, f32[512,512]{1,0:T(8,128)S(1)} %fusion.14), kind=kOutput, calls=%fused_computation.1 | convolution fusion | flops 3227254784 | bytes 14682112 | tf_op jit(solution)/shard_map/dot_general | solution.py:367
  153.1 4.1 %fusion.37 = (bf16[4,4,32,2048]{3,2,1,0:T(8,128)(2,1)}, bf16[4,4,32,2048]{3,2,0,1:T(8,128)(2,1)S(1)}) fusion(bf16[4,4,32,4096]{3,2,1,0:T(8,128)(2,1)} %bitcast.77), kind=kLoop, calls=%fused_computation.51 | loop fusion | bytes 8388608 | tf_op jit(solution)/shard_map/slice | solution.py:123
  157.1 1.6 copy.26.refs_0_
  158.7 36.0 %shard_map.95 = (bf16[4,4,32,2048]{3,2,1,0:T(8,128)(2,1)}, bf16[4,4,32,2048]{3,2,1,0:T(8,128)(2,1)}) custom-call(bf16[4,4,32,2048]{3,2,1,0:T(8,128)(2,1)} %copy.26.refs_0_, bf16[4,4,32,2048]{3,2,1,0:T(8,128)(2,1)} %get-tuple-element.21.refs_1_), custom_call_target="tpu_custom_call" | custom-call | tf_op jit(solution)/shard_map/pallas_call | solution.py:103
  194.7 3.1 %reduce_sum.42.refs_0_ = bf16[4,32,2048]{2,1,0:T(8,128)(2,1)} reduce(bf16[4,4,32,2048]{3,2,1,0:T(8,128)(2,1)} %get-tuple-element.17, bf16[]{:T(256)} %constant.63.clone.1), dimensions={0}, to_apply=%region_0.1 | reduce | flops 786432 | bytes 2621442 | tf_op jit(solution)/shard_map/reduce_sum | solution.py:125
  197.8 1.3 reduce_sum.43.refs_1_
  199.1 10.6 %shard_map.96 = (bf16[4,32,2048]{2,1,0:T(8,128)(2,1)}, bf16[4,32,2048]{2,1,0:T(8,128)(2,1)}) custom-call(bf16[4,32,2048]{2,1,0:T(8,128)(2,1)} %reduce_sum.42.refs_0_, bf16[4,32,2048]{2,1,0:T(8,128)(2,1)} %reduce_sum.43.refs_1_), custom_call_target="tpu_custom_call" | custom-call | tf_op jit(solution)/shard_map/pallas_call | solution.py:103
  210.9 1.1 reduce.3
  212.7 7.4 %shard_map.97 = bf16[8,32,512]{2,1,0:T(8,128)(2,1)} custom-call(bf16[8,32,512]{2,1,0:T(8,128)(2,1)} %maximum_bitcast_fusion.x_ref), custom_call_target="tpu_custom_call" | custom-call | tf_op jit(solution)/shard_map/pallas_call | solution.py:44
  222.8 13.4 %shard_map.98 = bf16[16,4,8,512]{3,2,1,0:T(8,128)(2,1)} custom-call(bf16[16,4,8,512]{3,2,1,0:T(8,128)(2,1)} %bitcast.88), custom_call_target="tpu_custom_call" | custom-call | tf_op jit(solution)/shard_map/pallas_call | solution.py:44
  236.2 1.9 copy.29
  (50 shorter events, 14.7 us)
Async XLA Ops:
  51.8 2.8 %copy-start.5 = (bf16[512,4096]{1,0:T(8,128)(2,1)S(1)}, bf16[512,4096]{1,0:T(8,128)(2,1)}, u32[]{:S(2)}) copy-start(bf16[512,4096]{1,0:T(8,128)(2,1)} %param.9) | copy-start | bytes 12582916
  54.6 1.6 copy-start.9
  56.2 1.3 copy-start.2
  57.9 12.3 %copy-start.3 = (s32[8,4]{0,1:T(4,128)S(1)}, s32[8,4]{0,1:T(4,128)}, u32[]{:S(2)}) copy-start(s32[8,4]{0,1:T(4,128)} %param.16) | copy-start | bytes 388
  132.9 2.8 %copy-start.6 = (bf16[1,4096,512]{2,1,0:T(8,128)(2,1)S(1)}, bf16[1,4096,512]{2,1,0:T(8,128)(2,1)}, u32[]{:S(2)}) copy-start(bf16[1,4096,512]{2,1,0:T(8,128)(2,1)} %param.12) | copy-start | bytes 12582916
  135.7 1.6 copy-start.8
  137.3 2.2 copy-start.7
  139.5 2.2 copy-start.10
  139.5 3.3 %copy-start.4 = (f32[1,512]{1,0:T(1,128)S(1)}, f32[1,512]{1,0:T(1,128)}, u32[]{:S(2)}) copy-start(f32[1,512]{1,0:T(1,128)} %param.15) | copy-start | bytes 6148
  194.7 3.1 %copy-start.1 = (bf16[4,4,32,2048]{3,2,1,0:T(8,128)(2,1)S(1)}, bf16[4,4,32,2048]{3,2,1,0:T(8,128)(2,1)}, u32[]{:S(2)}) copy-start(bf16[4,4,32,2048]{3,2,1,0:T(8,128)(2,1)} %get-tuple-element.18) | copy-start | bytes 6291460
  199.1 22.2 %copy-start = (bf16[16,4,8,512]{3,2,1,0:T(8,128)(2,1)S(1)}, bf16[16,4,8,512]{3,2,1,0:T(8,128)(2,1)}, u32[]{:S(2)}) copy-start(bf16[16,4,8,512]{3,2,1,0:T(8,128)(2,1)} %shard_map.92) | copy-start | bytes 1572868

commit v9 on v6

--- a/solution.py
+++ b/solution.py
@@ -142,6 +142,94 @@
     return got_a, got_b
 
 
+def _spread_kernel(n_dp, n_expert, chosen_ref, split_ref, pieces_ref, mine_ref,
+                   held, outgoing, local_sems, dp_send, dp_recv, ex_send, ex_recv):
+    me = lax.axis_index("dp")
+    mine_e = lax.axis_index("expert")
+    mesh_id = pl.DeviceIdType.MESH
+    group = split_ref.shape[1]
+    barrier = pltpu.get_barrier_semaphore()
+    for k in range(1, n_dp):
+        pl.semaphore_signal(barrier, 1, device_id={"dp": lax.rem(me + k, n_dp)}, device_id_type=mesh_id)
+    for k in range(1, n_expert):
+        pl.semaphore_signal(
+            barrier, 1, device_id={"expert": lax.rem(mine_e + k, n_expert)}, device_id_type=mesh_id
+        )
+    pl.semaphore_wait(barrier, n_dp + n_expert - 2)
+
+    def at_source(src):
+        return held.at[pl.ds(pl.multiple_of(src * group, group), group)]
+
+    local = pltpu.make_async_copy(split_ref.at[me], at_source(me), local_sems.at[0])
+    local.start()
+    copies = []
+    for k in range(1, n_dp):
+        target = lax.rem(me + k, n_dp)
+        copy = pltpu.make_async_remote_copy(
+            src_ref=split_ref.at[target],
+            dst_ref=at_source(me),
+            send_sem=dp_send.at[k - 1],
+            recv_sem=dp_recv.at[k - 1],
+            device_id={"dp": target},
+            device_id_type=mesh_id,
+        )
+        copy.start()
+        copies.append(copy)
+    local.wait()
+    for copy in copies:
+        copy.wait()
+    keep = pltpu.make_async_copy(held, pieces_ref, local_sems.at[1])
+    keep.start()
+    for e in range(n_expert):
+        for s in range(CAP):
+            outgoing[e, s] = held[chosen_ref[e * CAP + s]]
+    local = pltpu.make_async_copy(outgoing.at[mine_e], mine_ref.at[mine_e], local_sems.at[2])
+    local.start()
+    copies = []
+    for k in range(1, n_expert):
+        target = lax.rem(mine_e + k, n_expert)
+        copy = pltpu.make_async_remote_copy(
+            src_ref=outgoing.at[target],
+            dst_ref=mine_ref.at[mine_e],
+            send_sem=ex_send.at[k - 1],
+            recv_sem=ex_recv.at[k - 1],
+            device_id={"expert": target},
+            device_id_type=mesh_id,
+        )
+        copy.start()
+        copies.append(copy)
+    local.wait()
+    for copy in copies:
+        copy.wait()
+    keep.wait()
+
+
+def spread_select(chosen, split, cid):
+    n_dp = lax.axis_size("dp")
+    n_expert = lax.axis_size("expert")
+    _, group, rows, width = split.shape
+    n_blocks = n_dp * group
+    return pl.pallas_call(
+        functools.partial(_spread_kernel, n_dp, n_expert),
+        out_shape=[
+            jax.ShapeDtypeStruct((n_blocks, rows, width), split.dtype),
+            jax.ShapeDtypeStruct((n_expert, CAP, rows, width), split.dtype),
+        ],
+        in_specs=[pl.BlockSpec(memory_space=pltpu.SMEM), pl.BlockSpec(memory_space=pl.ANY)],
+        out_specs=[pl.BlockSpec(memory_space=pl.ANY)] * 2,
+        scratch_shapes=[
+            pltpu.VMEM((n_blocks, rows, width), split.dtype),
+            pltpu.VMEM((n_expert, CAP, rows, width), split.dtype),
+            pltpu.SemaphoreType.DMA((3,)),
+            pltpu.SemaphoreType.DMA((n_dp - 1,)),
+            pltpu.SemaphoreType.DMA((n_dp - 1,)),
+            pltpu.SemaphoreType.DMA((n_expert - 1,)),
+            pltpu.SemaphoreType.DMA((n_expert - 1,)),
+        ],
+        compiler_params=pltpu.CompilerParams(collective_id=cid, has_side_effects=True),
+    )(chosen, split)
+
+
 def body(
     context,
     out_weight,
@@ -176,12 +264,7 @@
     attended = (residual.astype(jnp.float32) + projected).astype(jnp.bfloat16)
 
     split = attended.reshape(local_blocks, n_dp, piece, local_width).transpose(1, 0, 2, 3)
-    pieces = dp_exchange(split, gather=False, cid=0)
-    pieces = pieces.reshape(n_blocks, piece, local_width)
-
-    slots = jnp.take(pieces, chosen_blocks.reshape(-1), axis=0)
-    slots = slots.reshape(n_expert, CAP, piece, local_width)
-    mine = dp_exchange(slots, gather=False, cid=4, axis="expert")
+    pieces, mine = spread_select(chosen_blocks.reshape(-1), split, cid=0)
     mine = mine.transpose(1, 2, 0, 3).reshape(CAP * piece, model_width)
     picked_a, picked_b = all_gather_2d(mine, cid=20)
     picked_a = picked_a.reshape(n_dp * CAP * piece, -1)

time: 233 us -> 229 us (0.983)
    pallas_call x4 -> x2, Pallas kernels: 42.7 us -> 20.9 us  [dp_exchange(): pl.pallas_call(functools.partial(_exchange_kernel, n, gather, axis), out_...]
    pallas_call x0 -> x1, Pallas kernels: none -> 19.9 us  [spread_select(): pl.pallas_call(functools.partial(_spread_kernel, n_dp, n_expert), out_sha...]
    unnamed x27 -> x29, local copies, waits for them, and re-layouts: 5.36 us -> 5.35 us
where the time goes in v9:
time: 229 us; the launch traced here: 228 us
  Pallas kernels  179 us (78%)
  local copies, waits for them, and re-layouts  23.7 us (10%)
  matrix products  16.3 us (7%)
  other arithmetic  8.92 us (4%)
    pallas_call x6, Pallas kernels, dp_route(): pl.pallas_call(functools.partial(_route_kernel, tuple(strides), side, gat...  138 us
    pallas_call x2, Pallas kernels, dp_exchange(): pl.pallas_call(functools.partial(_exchange_kernel, n, gather, axis), out_...  20.9 us
    pallas_call x1, Pallas kernels, spread_select(): pl.pallas_call(functools.partial(_spread_kernel, n_dp, n_expert), out_sha...  19.9 us
    dot_general x1, matrix products, body(): part = jnp.dot(hidden, w_down, preferred_element_type=jnp.float32)  8.69 us
    unnamed x29, local copies, waits for them, and re-layouts  5.35 us

profile of v9, /device:TPU:24, one launch (start us, length us, event | category | flops | bytes accessed | tf_op | source)
XLA Modules:
  0.0 228.2 jit_solution(3043039500449250349)
XLA Ops:
  0.0 1.7 fusion.38
  1.7 12.2 %shard_map.91 = (bf16[4,256,256]{2,1,0:T(8,128)(2,1)}, bf16[4,256,256]{2,1,0:T(8,128)(2,1)}) custom-call(bf16[256,256]{1,0:T(8,128)(2,1)} %get-tuple-element.38.refs_0_, bf16[256,256]{1,0:T(8,128)(2,1)} %get-tuple-element.37.refs_1_), custom_call_target="tpu_custom_call" | custom-call | tf_op jit(solution)/shard_map/pallas_call | solution.py:103
  13.9 34.4 %shard_map.92 = (bf16[4,4,256,256]{3,2,1,0:T(8,128)(2,1)}, bf16[4,4,256,256]{3,2,1,0:T(8,128)(2,1)}) custom-call(bf16[4,256,256]{2,1,0:T(8,128)(2,1)} %get-tuple-element.19.refs_0_, bf16[4,256,256]{2,1,0:T(8,128)(2,1)} %get-tuple-element.20.refs_1_), custom_call_target="tpu_custom_call" | custom-call | tf_op jit(solution)/shard_map/pallas_call | solution.py:103
  48.3 1.9 copy.16
  51.1 1.3 convolution_bitcast_fusion
  52.7 1.3 convolution_bitcast_fusion.1
  56.2 19.9 %shard_map.93 = (bf16[64,8,512]{2,1,0:T(8,128)(2,1)}, bf16[8,4,8,512]{3,2,1,0:T(8,128)(2,1)}) custom-call(s32[32]{0:T(128)} %reshape.41.chosen_ref, bf16[16,4,8,512]{3,2,1,0:T(8,128)(2,1)} %bitcast.79), custom_call_target="tpu_custom_call" | custom-call | tf_op jit(solution)/shard_map/pallas_call | solution.py:212
  77.8 11.3 %shard_map.94 = (bf16[4,32,2048]{2,1,0:T(8,128)(2,1)}, bf16[4,32,2048]{2,1,0:T(8,128)(2,1)}) custom-call(bf16[32,2048]{1,0:T(8,128)(2,1)} %get-tuple-element.36.refs_0_, bf16[32,2048]{1,0:T(8,128)(2,1)} %get-tuple-element.35.refs_1_), custom_call_target="tpu_custom_call" | custom-call | tf_op jit(solution)/shard_map/pallas_call | solution.py:103
  89.1 34.6 %shard_map.95 = (bf16[4,4,32,2048]{3,2,1,0:T(8,128)(2,1)}, bf16[4,4,32,2048]{3,2,1,0:T(8,128)(2,1)}) custom-call(bf16[4,32,2048]{2,1,0:T(8,128)(2,1)} %get-tuple-element.25.refs_0_, bf16[4,32,2048]{2,1,0:T(8,128)(2,1)} %get-tuple-element.26.refs_1_), custom_call_target="tpu_custom_call" | custom-call | tf_op jit(solution)/shard_map/pallas_call | solution.py:103
  123.7 1.9 copy.20
  126.5 1.2 fusion.6
  128.1 1.3 fusion.14
  130.3 2.2 fusion.2
  135.3 8.7 %multiply_convert_fusion = bf16[512,4096]{1,0:T(8,128)(2,1)} fusion(bf16[1,512,4096]{2,1,0:T(8,128)(2,1)} %param.14, f32[512]{0:T(512)S(1)} %mul.19, f32[512,512]{1,0:T(8,128)} %fusion.2, bf16[512,2048]{1,0:T(8,128)(2,1)S(1)} %bitcast.90, bf16[1,4096,512]{2,1,0:T(8,128)(2,1)} %param.13, f32[512,512]{1,0:T(8,128)S(1)} %fusion.14), kind=kOutput, calls=%fused_computation | convolution fusion | flops 3227254784 | bytes 14682112 | tf_op jit(solution)/shard_map/dot_general | solution.py:290
  144.0 4.1 %fusion.36 = (bf16[4,4,32,2048]{3,2,1,0:T(8,128)(2,1)}, bf16[4,4,32,2048]{3,2,0,1:T(8,128)(2,1)S(1)}) fusion(bf16[4,4,32,4096]{3,2,1,0:T(8,128)(2,1)} %bitcast.72), kind=kLoop, calls=%fused_computation.44 | loop fusion | bytes 8388608 | tf_op jit(solution)/shard_map/slice | solution.py:123
  148.1 1.6 copy.22.refs_0_
  149.6 35.1 %shard_map.96 = (bf16[4,4,32,2048]{3,2,1,0:T(8,128)(2,1)}, bf16[4,4,32,2048]{3,2,1,0:T(8,128)(2,1)}) custom-call(bf16[4,4,32,2048]{3,2,1,0:T(8,128)(2,1)} %copy.22.refs_0_, bf16[4,4,32,2048]{3,2,1,0:T(8,128)(2,1)} %get-tuple-element.33.refs_1_), custom_call_target="tpu_custom_call" | custom-call | tf_op jit(solution)/shard_map/pallas_call | solution.py:103
  184.8 3.1 %reduce_sum.42.refs_0_ = bf16[4,32,2048]{2,1,0:T(8,128)(2,1)} reduce(bf16[4,4,32,2048]{3,2,1,0:T(8,128)(2,1)} %get-tuple-element.29, bf16[]{:T(256)} %constant.48.clone.1), dimensions={0}, to_apply=%region_0.1 | reduce | flops 786432 | bytes 2621442 | tf_op jit(solution)/shard_map/reduce_sum | solution.py:125
  187.8 1.3 reduce_sum.43.refs_1_
  189.1 10.6 %shard_map.97 = (bf16[4,32,2048]{2,1,0:T(8,128)(2,1)}, bf16[4,32,2048]{2,1,0:T(8,128)(2,1)}) custom-call(bf16[4,32,2048]{2,1,0:T(8,128)(2,1)} %reduce_sum.42.refs_0_, bf16[4,32,2048]{2,1,0:T(8,128)(2,1)} %reduce_sum.43.refs_1_), custom_call_target="tpu_custom_call" | custom-call | tf_op jit(solution)/shard_map/pallas_call | solution.py:103
  199.8 1.1 reduce.2
  202.8 7.4 %shard_map.98 = bf16[8,32,512]{2,1,0:T(8,128)(2,1)} custom-call(bf16[8,32,512]{2,1,0:T(8,128)(2,1)} %maximum_bitcast_fusion.x_ref), custom_call_target="tpu_custom_call" | custom-call | tf_op jit(solution)/shard_map/pallas_call | solution.py:44
  212.8 13.5 %shard_map.99 = bf16[16,4,8,512]{3,2,1,0:T(8,128)(2,1)} custom-call(bf16[16,4,8,512]{3,2,1,0:T(8,128)(2,1)} %bitcast.81), custom_call_target="tpu_custom_call" | custom-call | tf_op jit(solution)/shard_map/pallas_call | solution.py:44
  226.3 1.9 copy.25
  (46 shorter events, 14.3 us)
Async XLA Ops:
  48.3 2.8 %copy-start.6 = (bf16[512,4096]{1,0:T(8,128)(2,1)S(1)}, bf16[512,4096]{1,0:T(8,128)(2,1)}, u32[]{:S(2)}) copy-start(bf16[512,4096]{1,0:T(8,128)(2,1)} %param.9) | copy-start | bytes 12582916
  51.1 1.6 copy-start.10
  52.7 1.3 copy-start.2
  54.2 1.3 copy-start.4
  123.7 2.8 %copy-start.7 = (bf16[1,4096,512]{2,1,0:T(8,128)(2,1)S(1)}, bf16[1,4096,512]{2,1,0:T(8,128)(2,1)}, u32[]{:S(2)}) copy-start(bf16[1,4096,512]{2,1,0:T(8,128)(2,1)} %param.12) | copy-start | bytes 12582916
  126.5 1.6 copy-start.9
  128.1 2.2 copy-start.8
  130.3 2.2 copy-start.11
  130.3 3.4 %copy-start.5 = (f32[1,512]{1,0:T(1,128)S(1)}, f32[1,512]{1,0:T(1,128)}, u32[]{:S(2)}) copy-start(f32[1,512]{1,0:T(1,128)} %param.15) | copy-start | bytes 6148
  184.7 3.1 %copy-start = (bf16[4,4,32,2048]{3,2,1,0:T(8,128)(2,1)S(1)}, bf16[4,4,32,2048]{3,2,1,0:T(8,128)(2,1)}, u32[]{:S(2)}) copy-start(bf16[4,4,32,2048]{3,2,1,0:T(8,128)(2,1)} %get-tuple-element.30) | copy-start | bytes 6291460
  189.1 22.2 %copy-start.1 = (bf16[64,8,512]{2,1,0:T(8,128)(2,1)S(1)}, bf16[64,8,512]{2,1,0:T(8,128)(2,1)}, u32[]{:S(2)}) copy-start(bf16[64,8,512]{2,1,0:T(8,128)(2,1)} %get-tuple-element.23) | copy-start | bytes 1572868
  200.9 10.6 %copy-start.3 = (s32[32]{0:T(128)S(1)}, s32[32]{0:T(128)}, u32[]{:S(2)}) copy-start(s32[32]{0:T(128)} %reshape.41.chosen_ref) | copy-start | bytes 388

commit v10 on v9

--- a/solution.py
+++ b/solution.py
@@ -114,20 +114,105 @@
     )(*xs)
 
 
+def _finish_kernel(side, n_expert, a_ref, b_ref, out_ref, got_a, got_b, outgoing,
+                   local_sems, send_sems, recv_sems, ex_send, ex_recv):
+    me = lax.axis_index("dp")
+    mine_e = lax.axis_index("expert")
+    mesh_id = pl.DeviceIdType.MESH
+    routes = ((a_ref, got_a, side), (b_ref, got_b, 1))
+    barrier = pltpu.get_barrier_semaphore()
+    for _, _, stride in routes:
+        coord = lax.rem(me // stride, side)
+        base = me - coord * stride
+        for k in range(1, side):
+            peer = base + lax.rem(coord + k, side) * stride
+            pl.semaphore_signal(barrier, 1, device_id={"dp": peer}, device_id_type=mesh_id)
+    for k in range(1, n_expert):
+        pl.semaphore_signal(
+            barrier, 1, device_id={"expert": lax.rem(mine_e + k, n_expert)}, device_id_type=mesh_id
+        )
+    pl.semaphore_wait(barrier, 2 * (side - 1) + n_expert - 1)
+    locals_, copies = [], []
+    for r, (src, dst, stride) in enumerate(routes):
+        coord = lax.rem(me // stride, side)
+        base = me - coord * stride
+        local = pltpu.make_async_copy(src.at[coord], dst.at[coord], local_sems.at[r])
+        local.start()
+        locals_.append(local)
+        for k in range(1, side):
+            to = lax.rem(coord + k, side)
+            copy = pltpu.make_async_remote_copy(
+                src_ref=src.at[to],
+                dst_ref=dst.at[coord],
+                send_sem=send_sems.at[r, k - 1],
+                recv_sem=recv_sems.at[r, k - 1],
+                device_id={"dp": base + to * stride},
+                device_id_type=mesh_id,
+            )
+            copy.start()
+            copies.append(copy)
+    for local in locals_:
+        local.wait()
+    for copy in copies:
+        copy.wait()
+    width = outgoing.shape[-1]
+    per_half = got_a.shape[-1] // width
+    for h, got in enumerate((got_a, got_b)):
+        total = got[0].astype(jnp.float32)
+        for j in range(1, side):
+            total = total + got[j].astype(jnp.float32)
+        total = total.astype(outgoing.dtype)
+        for j in range(per_half):
+            outgoing[h * per_half + j] = total[:, j * width:(j + 1) * width]
+    local = pltpu.make_async_copy(outgoing.at[mine_e], out_ref.at[mine_e], local_sems.at[2])
+    local.start()
+    copies = []
+    for k in range(1, n_expert):
+        target = lax.rem(mine_e + k, n_expert)
+        copy = pltpu.make_async_remote_copy(
+            src_ref=outgoing.at[target],
+            dst_ref=out_ref.at[mine_e],
+            send_sem=ex_send.at[k - 1],
+            recv_sem=ex_recv.at[k - 1],
+            device_id={"expert": target},
+            device_id_type=mesh_id,
+        )
+        copy.start()
+        copies.append(copy)
+    local.wait()
+    for copy in copies:
+        copy.wait()
+
+
 def reduce_scatter_2d(part, cid):
     side = 4
+    n_expert = lax.axis_size("expert")
     n_dp, rows, cols = part.shape
     half = cols // 2
+    width = cols // n_expert
     grid = part.reshape(side, side, rows, cols)
     first_a = grid[..., :half].transpose(1, 0, 2, 3)
     first_b = grid[..., half:]
     got_a, got_b = dp_route([first_a, first_b], (1, side), cid)
     second_a = got_a.astype(jnp.float32).sum(axis=0).astype(jnp.bfloat16)
     second_b = got_b.astype(jnp.float32).sum(axis=0).astype(jnp.bfloat16)
-    got_a, got_b = dp_route([second_a, second_b], (side, 1), cid + 1)
-    total_a = got_a.astype(jnp.float32).sum(axis=0)
-    total_b = got_b.astype(jnp.float32).sum(axis=0)
-    return jnp.concatenate([total_a, total_b], axis=-1)
+    return pl.pallas_call(
+        functools.partial(_finish_kernel, side, n_expert),
+        out_shape=jax.ShapeDtypeStruct((n_expert, rows, width), part.dtype),
+        in_specs=[pl.BlockSpec(memory_space=pl.ANY)] * 2,
+        out_specs=pl.BlockSpec(memory_space=pl.ANY),
+        scratch_shapes=[
+            pltpu.VMEM(second_a.shape, second_a.dtype),
+            pltpu.VMEM(second_b.shape, second_b.dtype),
+            pltpu.VMEM((n_expert, rows, width), part.dtype),
+            pltpu.SemaphoreType.DMA((3,)),
+            pltpu.SemaphoreType.DMA((2, side - 1)),
+            pltpu.SemaphoreType.DMA((2, side - 1)),
+            pltpu.SemaphoreType.DMA((n_expert - 1,)),
+            pltpu.SemaphoreType.DMA((n_expert - 1,)),
+        ],
+        compiler_params=pltpu.CompilerParams(collective_id=cid + 1, has_side_effects=True),
+    )(second_a, second_b)
 
 
 def all_gather_2d(x, cid):
@@ -290,10 +375,7 @@
     part = jnp.dot(hidden, w_down, preferred_element_type=jnp.float32)
     part = (part * scale[:, None]).astype(jnp.bfloat16)
 
-    summed = reduce_scatter_2d(part.reshape(n_dp, CAP * piece, model_width), cid=1)
-    summed = summed.astype(jnp.bfloat16)
-    summed = summed.reshape(CAP * piece, n_expert, local_width).transpose(1, 0, 2)
-    outs = dp_exchange(summed, gather=False, cid=5, axis="expert")
+    outs = reduce_scatter_2d(part.reshape(n_dp, CAP * piece, model_width), cid=1)
     outs = outs.reshape(n_expert * CAP, piece * local_width)
 
     selector = chosen_blocks.reshape(-1)[None, :] == jnp.arange(n_blocks)[:, None]

time: 229 us -> 223 us (0.974)
  other arithmetic: 8.92 us -> 5.88 us
  Pallas kernels: 179 us -> 176 us
    pallas_call x0 -> x1, Pallas kernels: none -> 15 us  [reduce_scatter_2d(): pl.pallas_call(functools.partial(_finish_kernel, side, n_expert), out_sha...]
    pallas_call x6 -> x5, Pallas kernels: 138 us -> 128 us  [dp_route(): pl.pallas_call(functools.partial(_route_kernel, tuple(strides), side, gat...]
    pallas_call x2 -> x1, Pallas kernels: 20.9 us -> 13.8 us  [dp_exchange(): pl.pallas_call(functools.partial(_exchange_kernel, n, gather, axis), out_...]
where the time goes in v10:
time: 223 us; the launch traced here: 222 us
  Pallas kernels  176 us (79%)
  local copies, waits for them, and re-layouts  23.6 us (11%)
  matrix products  16.3 us (7%)
  other arithmetic  5.88 us (3%)
    pallas_call x5, Pallas kernels, dp_route(): pl.pallas_call(functools.partial(_route_kernel, tuple(strides), side, gat...  128 us
    pallas_call x1, Pallas kernels, spread_select(): pl.pallas_call(functools.partial(_spread_kernel, n_dp, n_expert), out_sha...  19.9 us
    pallas_call x1, Pallas kernels, reduce_scatter_2d(): pl.pallas_call(functools.partial(_finish_kernel, side, n_expert), out_sha...  15 us
    pallas_call x1, Pallas kernels, dp_exchange(): pl.pallas_call(functools.partial(_exchange_kernel, n, gather, axis), out_...  13.8 us
    dot_general x1, matrix products, body(): part = jnp.dot(hidden, w_down, preferred_element_type=jnp.float32)  8.72 us
    unnamed x29, local copies, waits for them, and re-layouts  5.36 us

profile of v10, /device:TPU:24, one launch (start us, length us, event | category | flops | bytes accessed | tf_op | source)
XLA Modules:
  0.0 222.3 jit_solution(5905900696325112993)
XLA Ops:
  0.0 1.7 fusion.38
  1.7 12.2 %shard_map.91 = (bf16[4,256,256]{2,1,0:T(8,128)(2,1)}, bf16[4,256,256]{2,1,0:T(8,128)(2,1)}) custom-call(bf16[256,256]{1,0:T(8,128)(2,1)} %get-tuple-element.34.refs_0_, bf16[256,256]{1,0:T(8,128)(2,1)} %get-tuple-element.33.refs_1_), custom_call_target="tpu_custom_call" | custom-call | tf_op jit(solution)/shard_map/pallas_call | solution.py:103
  13.9 34.4 %shard_map.92 = (bf16[4,4,256,256]{3,2,1,0:T(8,128)(2,1)}, bf16[4,4,256,256]{3,2,1,0:T(8,128)(2,1)}) custom-call(bf16[4,256,256]{2,1,0:T(8,128)(2,1)} %get-tuple-element.17.refs_0_, bf16[4,256,256]{2,1,0:T(8,128)(2,1)} %get-tuple-element.18.refs_1_), custom_call_target="tpu_custom_call" | custom-call | tf_op jit(solution)/shard_map/pallas_call | solution.py:103
  48.3 1.9 copy.16
  51.1 1.3 convolution_bitcast_fusion
  52.7 1.3 convolution_bitcast_fusion.1
  56.2 19.9 %shard_map.93 = (bf16[64,8,512]{2,1,0:T(8,128)(2,1)}, bf16[8,4,8,512]{3,2,1,0:T(8,128)(2,1)}) custom-call(s32[32]{0:T(128)} %reshape.36.chosen_ref, bf16[16,4,8,512]{3,2,1,0:T(8,128)(2,1)} %bitcast.71), custom_call_target="tpu_custom_call" | custom-call | tf_op jit(solution)/shard_map/pallas_call | solution.py:297
  76.1 1.0 copy.19
  77.8 11.3 %shard_map.94 = (bf16[4,32,2048]{2,1,0:T(8,128)(2,1)}, bf16[4,32,2048]{2,1,0:T(8,128)(2,1)}) custom-call(bf16[32,2048]{1,0:T(8,128)(2,1)} %get-tuple-element.32.refs_0_, bf16[32,2048]{1,0:T(8,128)(2,1)} %get-tuple-element.31.refs_1_), custom_call_target="tpu_custom_call" | custom-call | tf_op jit(solution)/shard_map/pallas_call | solution.py:103
  89.1 34.6 %shard_map.95 = (bf16[4,4,32,2048]{3,2,1,0:T(8,128)(2,1)}, bf16[4,4,32,2048]{3,2,1,0:T(8,128)(2,1)}) custom-call(bf16[4,32,2048]{2,1,0:T(8,128)(2,1)} %get-tuple-element.23.refs_0_, bf16[4,32,2048]{2,1,0:T(8,128)(2,1)} %get-tuple-element.24.refs_1_), custom_call_target="tpu_custom_call" | custom-call | tf_op jit(solution)/shard_map/pallas_call | solution.py:103
  123.7 1.9 copy.20
  126.5 1.2 fusion.6
  128.1 1.3 fusion.14
  130.3 2.2 fusion.2
  135.2 8.7 %multiply_convert_fusion = bf16[512,4096]{1,0:T(8,128)(2,1)} fusion(bf16[1,512,4096]{2,1,0:T(8,128)(2,1)} %param.14, f32[512]{0:T(512)S(1)} %mul.19, f32[512,512]{1,0:T(8,128)} %fusion.2, bf16[512,2048]{1,0:T(8,128)(2,1)S(1)} %bitcast.80, bf16[1,4096,512]{2,1,0:T(8,128)(2,1)} %param.13, f32[512,512]{1,0:T(8,128)S(1)} %fusion.14), kind=kOutput, calls=%fused_computation | convolution fusion | flops 3227254784 | bytes 14682112 | tf_op jit(solution)/shard_map/dot_general | solution.py:375
  143.9 4.1 %fusion.36 = (bf16[4,4,32,2048]{3,2,1,0:T(8,128)(2,1)}, bf16[4,4,32,2048]{3,2,0,1:T(8,128)(2,1)S(1)}) fusion(bf16[4,4,32,4096]{3,2,1,0:T(8,128)(2,1)} %bitcast.64), kind=kLoop, calls=%fused_computation.41 | loop fusion | bytes 8388608 | tf_op jit(solution)/shard_map/slice | solution.py:195
  148.0 1.6 copy.22.refs_0_
  149.5 35.1 %shard_map.96 = (bf16[4,4,32,2048]{3,2,1,0:T(8,128)(2,1)}, bf16[4,4,32,2048]{3,2,1,0:T(8,128)(2,1)}) custom-call(bf16[4,4,32,2048]{3,2,1,0:T(8,128)(2,1)} %copy.22.refs_0_, bf16[4,4,32,2048]{3,2,1,0:T(8,128)(2,1)} %get-tuple-element.29.refs_1_), custom_call_target="tpu_custom_call" | custom-call | tf_op jit(solution)/shard_map/pallas_call | solution.py:103
  184.7 3.1 %reduce_sum.24.a_ref = bf16[4,32,2048]{2,1,0:T(8,128)(2,1)} reduce(bf16[4,4,32,2048]{3,2,1,0:T(8,128)(2,1)} %get-tuple-element.27, bf16[]{:T(256)} %constant.48.clone.1), dimensions={0}, to_apply=%region_0.1 | reduce | flops 786432 | bytes 2621442 | tf_op jit(solution)/shard_map/reduce_sum | solution.py:197
  187.7 1.3 reduce_sum.25.b_ref
  189.0 15.0 %shard_map.97 = bf16[8,32,512]{2,1,0:T(8,128)(2,1)} custom-call(bf16[4,32,2048]{2,1,0:T(8,128)(2,1)} %reduce_sum.24.a_ref, bf16[4,32,2048]{2,1,0:T(8,128)(2,1)} %reduce_sum.25.b_ref), custom_call_target="tpu_custom_call" | custom-call | tf_op jit(solution)/shard_map/pallas_call | solution.py:199
  204.1 1.1 reshape.39
  206.6 13.8 %shard_map.98 = bf16[16,4,8,512]{3,2,1,0:T(8,128)(2,1)} custom-call(bf16[16,4,8,512]{3,2,1,0:T(8,128)(2,1)} %bitcast.73), custom_call_target="tpu_custom_call" | custom-call | tf_op jit(solution)/shard_map/pallas_call | solution.py:44
  220.4 1.9 copy.23
  (41 shorter events, 10.3 us)
Async XLA Ops:
  48.3 2.8 %copy-start.6 = (bf16[512,4096]{1,0:T(8,128)(2,1)S(1)}, bf16[512,4096]{1,0:T(8,128)(2,1)}, u32[]{:S(2)}) copy-start(bf16[512,4096]{1,0:T(8,128)(2,1)} %param.9) | copy-start | bytes 12582916
  51.1 1.6 copy-start.10
  52.7 1.3 copy-start.2
  54.2 1.3 copy-start.4
  123.7 2.8 %copy-start.7 = (bf16[1,4096,512]{2,1,0:T(8,128)(2,1)S(1)}, bf16[1,4096,512]{2,1,0:T(8,128)(2,1)}, u32[]{:S(2)}) copy-start(bf16[1,4096,512]{2,1,0:T(8,128)(2,1)} %param.12) | copy-start | bytes 12582916
  126.5 1.6 copy-start.9
  128.1 2.2 copy-start.8
  130.3 2.2 copy-start.11
  130.3 3.3 %copy-start.5 = (f32[1,512]{1,0:T(1,128)S(1)}, f32[1,512]{1,0:T(1,128)}, u32[]{:S(2)}) copy-start(f32[1,512]{1,0:T(1,128)} %param.15) | copy-start | bytes 6148
  184.6 3.1 %copy-start = (bf16[4,4,32,2048]{3,2,1,0:T(8,128)(2,1)S(1)}, bf16[4,4,32,2048]{3,2,1,0:T(8,128)(2,1)}, u32[]{:S(2)}) copy-start(bf16[4,4,32,2048]{3,2,1,0:T(8,128)(2,1)} %get-tuple-element.28) | copy-start | bytes 6291460
  187.7 17.4 %copy-start.1 = (bf16[64,8,512]{2,1,0:T(8,128)(2,1)S(1)}, bf16[64,8,512]{2,1,0:T(8,128)(2,1)}, u32[]{:S(2)}) copy-start(bf16[64,8,512]{2,1,0:T(8,128)(2,1)} %get-tuple-element.21) | copy-start | bytes 1572868
  189.0 16.3 %copy-start.3 = (s32[32]{0:T(128)S(1)}, s32[32]{0:T(128)}, u32[]{:S(2)}) copy-start(s32[32]{0:T(128)} %reshape.36.chosen_ref) | copy-start | bytes 388

commit v11 on v10

--- a/solution.py
+++ b/solution.py
@@ -227,6 +227,104 @@
     return got_a, got_b
 
 
+def _gather_gate_kernel(side, a_ref, b_ref, wg_ref, wu_ref, hidden_ref,
+                        got_a, got_b, acc_g, acc_u, local_sems, send_sems, recv_sems):
+    me = lax.axis_index("dp")
+    mesh_id = pl.DeviceIdType.MESH
+    half = a_ref.shape[-1]
+    group = got_a.shape[1] * got_a.shape[2]
+    rows = got_a.shape[2]
+    routes = ((a_ref, got_a, side), (b_ref, got_b, 1))
+    geo = []
+    for _, _, stride in routes:
+        coord = lax.rem(me // stride, side)
+        geo.append((coord, me - coord * stride))
+    barrier = pltpu.get_barrier_semaphore()
+    for (coord, base), (_, _, stride) in zip(geo, routes):
+        for k in range(1, side):
+            peer = base + lax.rem(coord + k, side) * stride
+            pl.semaphore_signal(barrier, 1, device_id={"dp": peer}, device_id_type=mesh_id)
+    pl.semaphore_wait(barrier, 2 * (side - 1))
+
+    def remote(r, k, source, to):
+        src, dst, stride = routes[r]
+        coord, base = geo[r]
+        return pltpu.make_async_remote_copy(
+            src_ref=src,
+            dst_ref=dst.at[source],
+            send_sem=send_sems.at[r, k - 1],
+            recv_sem=recv_sems.at[r, k - 1],
+            device_id={"dp": base + to * stride},
+            device_id_type=mesh_id,
+        )
+
+    locals_, sends = [], []
+    for r, (src, dst, stride) in enumerate(routes):
+        coord, base = geo[r]
+        local = pltpu.make_async_copy(src, dst.at[coord], local_sems.at[r])
+        local.start()
+        locals_.append(local)
+        for k in range(1, side):
+            copy = remote(r, k, coord, lax.rem(coord + k, side))
+            copy.start()
+            sends.append(copy)
+    acc_g[...] = jnp.zeros_like(acc_g)
+    acc_u[...] = jnp.zeros_like(acc_u)
+
+    def add_a(source):
+        block = got_a[source].reshape(group, half)
+        at = pl.ds(pl.multiple_of(source * group, group), group)
+        acc_g[at] += jnp.dot(block, wg_ref[:half], preferred_element_type=jnp.float32)
+        acc_u[at] += jnp.dot(block, wu_ref[:half], preferred_element_type=jnp.float32)
+
+    def add_b(source):
+        block = got_b[source].reshape(group, half)
+        g = jnp.dot(block, wg_ref[half:], preferred_element_type=jnp.float32)
+        u = jnp.dot(block, wu_ref[half:], preferred_element_type=jnp.float32)
+        for x in range(side):
+            at = pl.ds(pl.multiple_of((x * side + source) * rows, rows), rows)
+            acc_g[at] += g[x * rows:(x + 1) * rows]
+            acc_u[at] += u[x * rows:(x + 1) * rows]
+
+    for local in locals_:
+        local.wait()
+    add_a(geo[0][0])
+    add_b(geo[1][0])
+    for k in range(1, side):
+        for r, add in ((0, add_a), (1, add_b)):
+            coord, _ = geo[r]
+            source = lax.rem(coord + side - k, side)
+            remote(r, k, source, source).wait_recv()
+            add(source)
+    g = acc_g[...]
+    hidden_ref[...] = (g / (1.0 + jnp.exp(-g)) * acc_u[...]).astype(hidden_ref.dtype)
+    for copy in sends:
+        copy.wait_send()
+
+
+def gather_gate(x, w_gate, w_up, cid):
+    side = 4
+    n = side * side
+    half = x.shape[-1] // 2
+    first_a, first_b = dp_route([x[..., :half], x[..., half:]], (1, side), cid, gather=True)
+    return pl.pallas_call(
+        functools.partial(_gather_gate_kernel, side),
+        out_shape=jax.ShapeDtypeStruct((n * x.shape[0], w_gate.shape[1]), jnp.bfloat16),
+        in_specs=[pl.BlockSpec(memory_space=pl.ANY)] * 2 + [pl.BlockSpec(memory_space=pltpu.VMEM)] * 2,
+        out_specs=pl.BlockSpec(memory_space=pltpu.VMEM),
+        scratch_shapes=[
+            pltpu.VMEM((side,) + first_a.shape, first_a.dtype),
+            pltpu.VMEM((side,) + first_b.shape, first_b.dtype),
+            pltpu.VMEM((n * x.shape[0], w_gate.shape[1]), jnp.float32),
+            pltpu.VMEM((n * x.shape[0], w_gate.shape[1]), jnp.float32),
+            pltpu.SemaphoreType.DMA((2,)),
+            pltpu.SemaphoreType.DMA((2, side - 1)),
+            pltpu.SemaphoreType.DMA((2, side - 1)),
+        ],
+        compiler_params=pltpu.CompilerParams(collective_id=cid + 1, has_side_effects=True),
+    )(first_a, first_b, w_gate, w_up)
+
+
 def _spread_kernel(n_dp, n_expert, chosen_ref, split_ref, pieces_ref, mine_ref,
                    held, outgoing, local_sems, dp_send, dp_recv, ex_send, ex_recv):
     me = lax.axis_index("dp")
@@ -351,11 +449,6 @@
     split = attended.reshape(local_blocks, n_dp, piece, local_width).transpose(1, 0, 2, 3)
     pieces, mine = spread_select(chosen_blocks.reshape(-1), split, cid=0)
     mine = mine.transpose(1, 2, 0, 3).reshape(CAP * piece, model_width)
-    picked_a, picked_b = all_gather_2d(mine, cid=20)
-    picked_a = picked_a.reshape(n_dp * CAP * piece, -1)
-    picked_b = picked_b.reshape(n_dp * CAP * piece, -1)
-    half = picked_a.shape[1]
-
     w_gate = gate_weight[0]
     w_up = up_weight[0]
     w_down = down_weight[0]
@@ -365,13 +458,7 @@
     scale = jnp.where(live, gate_row, jnp.zeros_like(gate_row))
     scale = scale.reshape(CAP, n_dp, piece).transpose(1, 0, 2).reshape(-1)
 
-    gate = jnp.dot(picked_a, w_gate[:half], preferred_element_type=jnp.float32) + jnp.dot(
-        picked_b, w_gate[half:], preferred_element_type=jnp.float32
-    )
-    upper = jnp.dot(picked_a, w_up[:half], preferred_element_type=jnp.float32) + jnp.dot(
-        picked_b, w_up[half:], preferred_element_type=jnp.float32
-    )
-    hidden = (jax.nn.silu(gate) * upper).astype(jnp.bfloat16)
+    hidden = gather_gate(mine, w_gate, w_up, cid=20)
     part = jnp.dot(hidden, w_down, preferred_element_type=jnp.float32)
     part = (part * scale[:, None]).astype(jnp.bfloat16)
 

time: 223 us -> 209 us (0.937)
  matrix products: 16.3 us -> 7.58 us
  local copies, waits for them, and re-layouts: 23.6 us -> 17.2 us
    pallas_call x5 -> x4, Pallas kernels: 128 us -> 92.3 us  [dp_route(): pl.pallas_call(functools.partial(_route_kernel, tuple(strides), side, gat...]
    pallas_call x0 -> x1, Pallas kernels: none -> 34.3 us  [gather_gate(): pl.pallas_call(functools.partial(_gather_gate_kernel, side), out_shape=ja...]
    dot_general x3 -> x0, matrix products: 4.71 us -> none  [the longest x1 2.21 us: body(): jnp.dot(picked_b, w_up[half:], preferred_element_type=jnp.float32)]
    dot_general x1, matrix products: 8.72 us -> 4.71 us  [body(): part = jnp.dot(hidden, w_down, preferred_element_type=jnp.float32)]
    unnamed x29 -> x21, local copies, waits for them, and re-layouts: 5.36 us -> 2.87 us
where the time goes in v11:
time: 209 us; the launch traced here: 208 us
  Pallas kernels  176 us (84%)
  local copies, waits for them, and re-layouts  17.2 us (8%)
  matrix products  7.58 us (4%)
  other arithmetic  7.37 us (4%)
    pallas_call x4, Pallas kernels, dp_route(): pl.pallas_call(functools.partial(_route_kernel, tuple(strides), side, gat...  92.3 us
    pallas_call x1, Pallas kernels, gather_gate(): pl.pallas_call(functools.partial(_gather_gate_kernel, side), out_shape=ja...  34.3 us
    pallas_call x1, Pallas kernels, spread_select(): pl.pallas_call(functools.partial(_spread_kernel, n_dp, n_expert), out_sha...  19.9 us
    pallas_call x1, Pallas kernels, reduce_scatter_2d(): pl.pallas_call(functools.partial(_finish_kernel, side, n_expert), out_sha...  15.7 us
    pallas_call x1, Pallas kernels, dp_exchange(): pl.pallas_call(functools.partial(_exchange_kernel, n, gather, axis), out_...  13.4 us
    dot_general x1, matrix products, body(): part = jnp.dot(hidden, w_down, preferred_element_type=jnp.float32)  4.71 us

profile of v11, /device:TPU:24, one launch (start us, length us, event | category | flops | bytes accessed | tf_op | source)
XLA Modules:
  0.0 208.1 jit_solution(17166098208294285270)
XLA Ops:
  0.0 1.7 fusion.10
  1.7 12.2 %shard_map.91 = (bf16[4,256,256]{2,1,0:T(8,128)(2,1)}, bf16[4,256,256]{2,1,0:T(8,128)(2,1)}) custom-call(bf16[256,256]{1,0:T(8,128)(2,1)} %get-tuple-element.30.refs_0_, bf16[256,256]{1,0:T(8,128)(2,1)} %get-tuple-element.29.refs_1_), custom_call_target="tpu_custom_call" | custom-call | tf_op jit(solution)/shard_map/pallas_call | solution.py:103
  13.9 34.4 %shard_map.92 = (bf16[4,4,256,256]{3,2,1,0:T(8,128)(2,1)}, bf16[4,4,256,256]{3,2,1,0:T(8,128)(2,1)}) custom-call(bf16[4,256,256]{2,1,0:T(8,128)(2,1)} %get-tuple-element.15.refs_0_, bf16[4,256,256]{2,1,0:T(8,128)(2,1)} %get-tuple-element.16.refs_1_), custom_call_target="tpu_custom_call" | custom-call | tf_op jit(solution)/shard_map/pallas_call | solution.py:103
  48.3 1.9 copy.16
  50.2 0.9 copy-done.5
  51.1 1.3 convolution_bitcast_fusion
  52.4 1.3 convolution_bitcast_fusion.1
  54.4 0.8 copy.26
  56.0 19.9 %shard_map.93 = (bf16[64,8,512]{2,1,0:T(8,128)(2,1)}, bf16[8,4,8,512]{3,2,1,0:T(8,128)(2,1)}) custom-call(s32[32]{0:T(128)} %reshape.32.chosen_ref, bf16[16,4,8,512]{3,2,1,0:T(8,128)(2,1)} %bitcast.44), custom_call_target="tpu_custom_call" | custom-call | tf_op jit(solution)/shard_map/pallas_call | solution.py:395
  75.9 1.0 copy.19
  76.9 0.7 fusion.9
  77.6 11.3 %shard_map.94 = (bf16[4,32,2048]{2,1,0:T(8,128)(2,1)}, bf16[4,32,2048]{2,1,0:T(8,128)(2,1)}) custom-call(bf16[32,2048]{1,0:T(8,128)(2,1)} %get-tuple-element.28.refs_0_, bf16[32,2048]{1,0:T(8,128)(2,1)} %get-tuple-element.27.refs_1_), custom_call_target="tpu_custom_call" | custom-call | tf_op jit(solution)/shard_map/pallas_call | solution.py:103
  88.9 34.3 %shard_map.95 = bf16[512,512]{1,0:T(8,128)(2,1)} custom-call(bf16[4,32,2048]{2,1,0:T(8,128)(2,1)} %get-tuple-element.21.a_ref, bf16[4,32,2048]{2,1,0:T(8,128)(2,1)} %get-tuple-element.22.b_ref, bf16[4096,512]{1,0:T(8,128)(2,1)} %bitcast.38, bf16[4096,512]{1,0:T(8,128)(2,1)} %bitcast.39), custom_call_target="tpu_custom_call" | custom-call | tf_op jit(solution)/shard_map/pallas_call | solution.py:310
  125.9 4.7 %multiply_convert_fusion = bf16[512,4096]{1,0:T(8,128)(2,1)S(1)} fusion(bf16[512,512]{1,0:T(8,128)(2,1)} %shard_map.95, bf16[1,512,4096]{2,1,0:T(8,128)(2,1)} %param.14, f32[512]{0:T(512)S(1)} %mul.10), kind=kOutput, calls=%fused_computation | convolution fusion | flops 2151677952 | bytes 8914944 | tf_op jit(solution)/shard_map/dot_general | solution.py:462
  130.6 2.0 fusion.8
  132.6 1.6 copy.21.refs_0_
  134.2 34.4 %shard_map.96 = (bf16[4,4,32,2048]{3,2,1,0:T(8,128)(2,1)}, bf16[4,4,32,2048]{3,2,1,0:T(8,128)(2,1)}) custom-call(bf16[4,4,32,2048]{3,2,1,0:T(8,128)(2,1)} %copy.21.refs_0_, bf16[4,4,32,2048]{3,2,1,0:T(8,128)(2,1)} %get-tuple-element.25.refs_1_), custom_call_target="tpu_custom_call" | custom-call | tf_op jit(solution)/shard_map/pallas_call | solution.py:103
  168.7 3.0 %reduce_sum.24.a_ref = bf16[4,32,2048]{2,1,0:T(8,128)(2,1)} reduce(bf16[4,4,32,2048]{3,2,1,0:T(8,128)(2,1)} %get-tuple-element.23, bf16[]{:T(256)} %constant.45.clone.1), dimensions={0}, to_apply=%region_0.1 | reduce | flops 786432 | bytes 2621442 | tf_op jit(solution)/shard_map/reduce_sum | solution.py:197
  171.6 2.9 %reduce_sum.25.b_ref = bf16[4,32,2048]{2,1,0:T(8,128)(2,1)} reduce(bf16[4,4,32,2048]{3,2,1,0:T(8,128)(2,1)} %get-tuple-element.24, bf16[]{:T(256)} %constant.45.clone.1), dimensions={0}, to_apply=%region_1.2 | reduce | flops 786432 | bytes 2621442 | tf_op jit(solution)/shard_map/reduce_sum | solution.py:198
  174.6 15.7 %shard_map.97 = bf16[8,32,512]{2,1,0:T(8,128)(2,1)} custom-call(bf16[4,32,2048]{2,1,0:T(8,128)(2,1)} %reduce_sum.24.a_ref, bf16[4,32,2048]{2,1,0:T(8,128)(2,1)} %reduce_sum.25.b_ref), custom_call_target="tpu_custom_call" | custom-call | tf_op jit(solution)/shard_map/pallas_call | solution.py:199
  190.3 1.1 reshape.35
  191.9 1.0 copy.24
  192.9 13.4 %shard_map.98 = bf16[16,4,8,512]{3,2,1,0:T(8,128)(2,1)} custom-call(bf16[16,4,8,512]{3,2,1,0:T(8,128)(2,1)} %bitcast.46), custom_call_target="tpu_custom_call" | custom-call | tf_op jit(solution)/shard_map/pallas_call | solution.py:44
  206.2 1.9 copy.22
  (29 shorter events, 4.5 us)
Async XLA Ops:
  48.3 2.8 %copy-start.5 = (bf16[512,4096]{1,0:T(8,128)(2,1)S(1)}, bf16[512,4096]{1,0:T(8,128)(2,1)}, u32[]{:S(2)}) copy-start(bf16[512,4096]{1,0:T(8,128)(2,1)} %param.9) | copy-start | bytes 12582916
  50.2 2.2 %copy-start.6 = (bf16[4,4,256,256]{3,2,1,0:T(8,128)(2,1)S(1)}, bf16[4,4,256,256]{3,2,1,0:T(8,128)(2,1)}, u32[]{:S(2)}) copy-start(bf16[4,4,256,256]{3,2,1,0:T(8,128)(2,1)} %get-tuple-element.17) | copy-start | bytes 6291460
  52.4 1.3 copy-start.1
  53.7 1.5 copy-start.3
  88.9 34.4 %copy-start.7 = (s32[8]{0:T(128)S(1)}, s32[8]{0:T(128)}, u32[]{:S(2)}) copy-start(s32[8]{0:T(128)} %param.17) | copy-start | bytes 100
  88.9 35.5 %copy-start.4 = (f32[1,512]{1,0:T(1,128)S(1)}, f32[1,512]{1,0:T(1,128)}, u32[]{:S(2)}) copy-start(f32[1,512]{1,0:T(1,128)} %param.15) | copy-start | bytes 6148
  168.7 22.7 %copy-start = (bf16[64,8,512]{2,1,0:T(8,128)(2,1)S(1)}, bf16[64,8,512]{2,1,0:T(8,128)(2,1)}, u32[]{:S(2)}) copy-start(bf16[64,8,512]{2,1,0:T(8,128)(2,1)} %get-tuple-element.19) | copy-start | bytes 1572868
  168.7 22.9 %copy-start.2 = (s32[32]{0:T(128)S(1)}, s32[32]{0:T(128)}, u32[]{:S(2)}) copy-start(s32[32]{0:T(128)} %reshape.32.chosen_ref) | copy-start | bytes 388

commit v12 on v11

--- a/solution.py
+++ b/solution.py
@@ -184,34 +184,117 @@
         copy.wait()
 
 
+def _down_scatter_kernel(side, hidden_ref, wd_ref, scale_ref, sum_a, sum_b,
+                         send_a, send_b, got_a, got_b, send_sems, recv_sems):
+    me = lax.axis_index("dp")
+    mesh_id = pl.DeviceIdType.MESH
+    half = send_a.shape[-1]
+    rows = send_a.shape[2]
+    chunk = side * rows
+    my_y = lax.rem(me, side)
+    my_x = lax.rem(me // side, side)
+    base_y = me - my_y
+    base_x = me - my_x * side
+    barrier = pltpu.get_barrier_semaphore()
+    for k in range(1, side):
+        pl.semaphore_signal(barrier, 1, device_id={"dp": base_y + lax.rem(my_y + k, side)}, device_id_type=mesh_id)
+        pl.semaphore_signal(
+            barrier, 1, device_id={"dp": base_x + lax.rem(my_x + k, side) * side}, device_id_type=mesh_id
+        )
+    pl.semaphore_wait(barrier, 2 * (side - 1))
+
+    def to_a(k, y):
+        return pltpu.make_async_remote_copy(
+            src_ref=send_a.at[y], dst_ref=got_a.at[my_y], send_sem=send_sems.at[0, k - 1],
+            recv_sem=recv_sems.at[0, k - 1], device_id={"dp": base_y + y}, device_id_type=mesh_id,
+        )
+
+    def to_b(k, x):
+        return pltpu.make_async_remote_copy(
+            src_ref=send_b.at[x], dst_ref=got_b.at[my_x], send_sem=send_sems.at[1, k - 1],
+            recv_sem=recv_sems.at[1, k - 1], device_id={"dp": base_x + x * side}, device_id_type=mesh_id,
+        )
+
+    sends = []
+    for k in list(range(1, side)) + [0]:
+        x = lax.rem(my_x + k, side)
+        at = pl.ds(pl.multiple_of(x * chunk, chunk), chunk)
+        part = jnp.dot(hidden_ref[at], wd_ref[...], preferred_element_type=jnp.float32)
+        part = (part * scale_ref[at]).astype(send_a.dtype)
+        for y in range(side):
+            send_a[y, x] = part[y * rows:(y + 1) * rows, :half]
+            send_b[x, y] = part[y * rows:(y + 1) * rows, half:]
+        if k:
+            copy = to_b(k, x)
+            copy.start()
+            sends.append(copy)
+    for k in range(1, side):
+        copy = to_a(k, lax.rem(my_y + k, side))
+        copy.start()
+        sends.append(copy)
+    for k in range(1, side):
+        to_a(k, lax.rem(my_y + side - k, side)).wait_recv()
+        to_b(k, lax.rem(my_x + side - k, side)).wait_recv()
+    for x in range(side):
+        total = send_a[my_y, x].astype(jnp.float32)
+        for k in range(1, side):
+            total = total + got_a[lax.rem(my_y + side - k, side), x].astype(jnp.float32)
+        sum_a[x] = total.astype(sum_a.dtype)
+    for y in range(side):
+        total = send_b[my_x, y].astype(jnp.float32)
+        for k in range(1, side):
+            total = total + got_b[lax.rem(my_x + side - k, side), y].astype(jnp.float32)
+        sum_b[y] = total.astype(sum_b.dtype)
+    for copy in sends:
+        copy.wait_send()
+
+
+def down_scatter(hidden, w_down, scale, cid):
+    side = 4
+    rows = hidden.shape[0] // (side * side)
+    half = w_down.shape[1] // 2
+    slab = (side, side, rows, half)
+    vmem = pl.BlockSpec(memory_space=pltpu.VMEM)
+    return pl.pallas_call(
+        functools.partial(_down_scatter_kernel, side),
+        out_shape=[jax.ShapeDtypeStruct((side, rows, half), jnp.bfloat16)] * 2,
+        in_specs=[vmem] * 3,
+        out_specs=[vmem] * 2,
+        scratch_shapes=[
+            pltpu.VMEM(slab, jnp.bfloat16),
+            pltpu.VMEM(slab, jnp.bfloat16),
+            pltpu.VMEM(slab, jnp.bfloat16),
+            pltpu.VMEM(slab, jnp.bfloat16),
+            pltpu.SemaphoreType.DMA((2, side - 1)),
+            pltpu.SemaphoreType.DMA((2, side - 1)),
+        ],
+        compiler_params=pltpu.CompilerParams(collective_id=cid, has_side_effects=True),
+    )(hidden, w_down, scale)
+
+
 def reduce_scatter_2d(part, cid):
     side = 4
     n_expert = lax.axis_size("expert")
-    n_dp, rows, cols = part.shape
-    half = cols // 2
+    second_a, second_b = part
+    rows = second_a.shape[1]
+    cols = 2 * second_a.shape[2]
     width = cols // n_expert
-    grid = part.reshape(side, side, rows, cols)
-    first_a = grid[..., :half].transpose(1, 0, 2, 3)
-    first_b = grid[..., half:]
-    got_a, got_b = dp_route([first_a, first_b], (1, side), cid)
-    second_a = got_a.astype(jnp.float32).sum(axis=0).astype(jnp.bfloat16)
-    second_b = got_b.astype(jnp.float32).sum(axis=0).astype(jnp.bfloat16)
     return pl.pallas_call(
         functools.partial(_finish_kernel, side, n_expert),
-        out_shape=jax.ShapeDtypeStruct((n_expert, rows, width), part.dtype),
+        out_shape=jax.ShapeDtypeStruct((n_expert, rows, width), second_a.dtype),
         in_specs=[pl.BlockSpec(memory_space=pl.ANY)] * 2,
         out_specs=pl.BlockSpec(memory_space=pl.ANY),
         scratch_shapes=[
             pltpu.VMEM(second_a.shape, second_a.dtype),
             pltpu.VMEM(second_b.shape, second_b.dtype),
-            pltpu.VMEM((n_expert, rows, width), part.dtype),
+            pltpu.VMEM((n_expert, rows, width), second_a.dtype),
             pltpu.SemaphoreType.DMA((3,)),
             pltpu.SemaphoreType.DMA((2, side - 1)),
             pltpu.SemaphoreType.DMA((2, side - 1)),
             pltpu.SemaphoreType.DMA((n_expert - 1,)),
             pltpu.SemaphoreType.DMA((n_expert - 1,)),
         ],
-        compiler_params=pltpu.CompilerParams(collective_id=cid + 1, has_side_effects=True),
+        compiler_params=pltpu.CompilerParams(collective_id=cid, has_side_effects=True),
     )(second_a, second_b)
 
 
@@ -459,10 +542,9 @@
     scale = scale.reshape(CAP, n_dp, piece).transpose(1, 0, 2).reshape(-1)
 
     hidden = gather_gate(mine, w_gate, w_up, cid=20)
-    part = jnp.dot(hidden, w_down, preferred_element_type=jnp.float32)
-    part = (part * scale[:, None]).astype(jnp.bfloat16)
-
-    outs = reduce_scatter_2d(part.reshape(n_dp, CAP * piece, model_width), cid=1)
+    halves = down_scatter(hidden, w_down, scale[:, None], cid=1)
+
+    outs = reduce_scatter_2d(halves, cid=2)
     outs = outs.reshape(n_expert * CAP, piece * local_width)
 
     selector = chosen_blocks.reshape(-1)[None, :] == jnp.arange(n_blocks)[:, None]

time: 209 us -> 198 us (0.947)
  other arithmetic: 7.37 us -> 2.13 us
    pallas_call x4 -> x3, Pallas kernels: 92.3 us -> 58.1 us  [dp_route(): pl.pallas_call(functools.partial(_route_kernel, tuple(strides), side, gat...]
    pallas_call x0 -> x1, Pallas kernels: none -> 32.5 us  [down_scatter(): pl.pallas_call(functools.partial(_down_scatter_kernel, side), out_shape=[...]
    reduce_sum x2 -> x0, other arithmetic: 5.89 us -> none  [the longest x1 2.96 us: reduce_scatter_2d(): second_a = got_a.astype(jnp.float32).sum(axis=0).astype(jnp.bfloat16)]
    dot_general x1 -> x0, matrix products: 4.71 us -> none  [body(): part = jnp.dot(hidden, w_down, preferred_element_type=jnp.float32)]
    dot_general x1, matrix products: 1.3 us -> 4.26 us  [body(): jnp.dot(context, w_a, preferred_element_type=jnp.float32)]
    unnamed x21 -> x11, local copies, waits for them, and re-layouts: 2.87 us -> 4.89 us
where the time goes in v12:
time: 198 us
  Pallas kernels  174 us (88%)
  local copies, waits for them, and re-layouts  15.3 us (8%)
  matrix products  5.83 us (3%)
  other arithmetic  2.13 us (1%)
    pallas_call x3, Pallas kernels, dp_route(): pl.pallas_call(functools.partial(_route_kernel, tuple(strides), side, gat...  58.1 us
    pallas_call x1, Pallas kernels, gather_gate(): pl.pallas_call(functools.partial(_gather_gate_kernel, side), out_shape=ja...  34.3 us
    pallas_call x1, Pallas kernels, down_scatter(): pl.pallas_call(functools.partial(_down_scatter_kernel, side), out_shape=[...  32.5 us
    pallas_call x1, Pallas kernels, spread_select(): pl.pallas_call(functools.partial(_spread_kernel, n_dp, n_expert), out_sha...  19.9 us
    pallas_call x1, Pallas kernels, reduce_scatter_2d(): pl.pallas_call(functools.partial(_finish_kernel, side, n_expert), out_sha...  15.8 us
    pallas_call x1, Pallas kernels, dp_exchange(): pl.pallas_call(functools.partial(_exchange_kernel, n, gather, axis), out_...  13.4 us
    unnamed x11, local copies, waits for them, and re-layouts  4.89 us
    dot_general x1, matrix products, body(): jnp.dot(context, w_a, preferred_element_type=jnp.float32)  4.26 us

profile of v12, /device:TPU:24, one launch (start us, length us, event | category | flops | bytes accessed | tf_op | source)
XLA Modules:
  0.0 197.6 jit_solution(3720565638452074380)
XLA Ops:
  0.0 1.2 dynamic_slice.4
  1.7 1.3 reduce.3
  3.1 0.8 copy.14
  3.8 0.7 reshape.31.chosen_ref
  5.2 0.8 broadcast_in_dim_reshape.5.scale_ref
  6.1 1.7 fusion.8
  7.7 1.3 copy.15
  9.0 12.3 %shard_map.91 = (bf16[4,256,256]{2,1,0:T(8,128)(2,1)}, bf16[4,256,256]{2,1,0:T(8,128)(2,1)}) custom-call(bf16[256,256]{1,0:T(8,128)(2,1)} %get-tuple-element.28.refs_0_, bf16[256,256]{1,0:T(8,128)(2,1)} %get-tuple-element.27.refs_1_), custom_call_target="tpu_custom_call" | custom-call | tf_op jit(solution)/shard_map/pallas_call | solution.py:103
  21.3 34.4 %shard_map.92 = (bf16[4,4,256,256]{3,2,1,0:T(8,128)(2,1)}, bf16[4,4,256,256]{3,2,1,0:T(8,128)(2,1)}) custom-call(bf16[4,256,256]{2,1,0:T(8,128)(2,1)} %get-tuple-element.15.refs_0_, bf16[4,256,256]{2,1,0:T(8,128)(2,1)} %get-tuple-element.16.refs_1_), custom_call_target="tpu_custom_call" | custom-call | tf_op jit(solution)/shard_map/pallas_call | solution.py:103
  55.7 4.3 %convolution_bitcast_fusion.1 = f32[512,256]{0,1:T(8,128)S(1)} fusion(bf16[4096,256]{1,0:T(8,128)(2,1)} %bitcast.46, bf16[512,4096]{1,0:T(8,128)(2,1)} %param.9), kind=kOutput, calls=%fused_computation.3 | convolution fusion | flops 1073741824 | bytes 6815744 | tf_op jit(solution)/shard_map/dot_general | solution.py:525
  60.4 1.3 convolution_bitcast_fusion
  62.1 0.9 copy.26
  63.0 19.9 %shard_map.93 = (bf16[64,8,512]{2,1,0:T(8,128)(2,1)}, bf16[8,4,8,512]{3,2,1,0:T(8,128)(2,1)}) custom-call(s32[32]{0:T(128)} %reshape.31.chosen_ref, bf16[16,4,8,512]{3,2,1,0:T(8,128)(2,1)} %bitcast.38), custom_call_target="tpu_custom_call" | custom-call | tf_op jit(solution)/shard_map/pallas_call | solution.py:478
  82.9 1.0 copy.19
  83.9 0.7 fusion.7
  84.6 1.2 copy.23
  85.8 11.4 %shard_map.94 = (bf16[4,32,2048]{2,1,0:T(8,128)(2,1)}, bf16[4,32,2048]{2,1,0:T(8,128)(2,1)}) custom-call(bf16[32,2048]{1,0:T(8,128)(2,1)} %get-tuple-element.26.refs_0_, bf16[32,2048]{1,0:T(8,128)(2,1)} %get-tuple-element.25.refs_1_), custom_call_target="tpu_custom_call" | custom-call | tf_op jit(solution)/shard_map/pallas_call | solution.py:103
  97.2 34.3 %shard_map.95.hidden_ref = bf16[512,512]{1,0:T(8,128)(2,1)} custom-call(bf16[4,32,2048]{2,1,0:T(8,128)(2,1)} %get-tuple-element.21.a_ref, bf16[4,32,2048]{2,1,0:T(8,128)(2,1)} %get-tuple-element.22.b_ref, bf16[4096,512]{1,0:T(8,128)(2,1)} %bitcast.33, bf16[4096,512]{1,0:T(8,128)(2,1)} %bitcast.34), custom_call_target="tpu_custom_call" | custom-call | tf_op jit(solution)/shard_map/pallas_call | solution.py:393
  131.6 32.5 %shard_map.96 = (bf16[4,32,2048]{2,1,0:T(8,128)(2,1)}, bf16[4,32,2048]{2,1,0:T(8,128)(2,1)}) custom-call(bf16[512,512]{1,0:T(8,128)(2,1)} %shard_map.95.hidden_ref, bf16[512,4096]{1,0:T(8,128)(2,1)} %bitcast.32, f32[512,1]{1,0:T(8,128)} %broadcast_in_dim_reshape.5.scale_ref), custom_call_target="tpu_custom_call" | custom-call | tf_op jit(solution)/shard_map/pallas_call | solution.py:258
  164.1 15.8 %shard_map.97 = bf16[8,32,512]{2,1,0:T(8,128)(2,1)} custom-call(bf16[4,32,2048]{2,1,0:T(8,128)(2,1)} %get-tuple-element.23.a_ref, bf16[4,32,2048]{2,1,0:T(8,128)(2,1)} %get-tuple-element.24.b_ref), custom_call_target="tpu_custom_call" | custom-call | tf_op jit(solution)/shard_map/pallas_call | solution.py:282
  179.9 1.1 reshape.34
  181.3 1.0 copy.24
  182.3 13.4 %shard_map.98 = bf16[16,4,8,512]{3,2,1,0:T(8,128)(2,1)} custom-call(bf16[16,4,8,512]{3,2,1,0:T(8,128)(2,1)} %bitcast.40), custom_call_target="tpu_custom_call" | custom-call | tf_op jit(solution)/shard_map/pallas_call | solution.py:44
  195.7 1.9 copy.22
  (14 shorter events, 2.3 us)
Async XLA Ops:
  55.7 4.3 %copy-start = (bf16[4,4,256,256]{3,2,1,0:T(8,128)(2,1)S(1)}, bf16[4,4,256,256]{3,2,1,0:T(8,128)(2,1)}, u32[]{:S(2)}) copy-start(bf16[4,4,256,256]{3,2,1,0:T(8,128)(2,1)} %get-tuple-element.18) | copy-start | bytes 6291460
  55.7 4.7 %copy-start.2 = (bf16[512,4096]{1,0:T(8,128)(2,1)S(1)}, bf16[512,4096]{1,0:T(8,128)(2,1)}, u32[]{:S(2)}) copy-start(bf16[512,4096]{1,0:T(8,128)(2,1)} %param.9) | copy-start | bytes 12582916
  131.5 49.5 %copy-start.1 = (s32[32]{0:T(128)S(1)}, s32[32]{0:T(128)}, u32[]{:S(2)}) copy-start(s32[32]{0:T(128)} %reshape.31.chosen_ref) | copy-start | bytes 388

commit v13 on v12

--- a/solution.py
+++ b/solution.py
@@ -408,6 +408,99 @@
     )(first_a, first_b, w_gate, w_up)
 
 
+def _gather_attend_kernel(side, a_ref, b_ref, ctx_ref, res_ref, out_ref,
+                          got_a, got_b, acc_a, acc_b, local_sems, send_sems, recv_sems):
+    me = lax.axis_index("dp")
+    mesh_id = pl.DeviceIdType.MESH
+    rows = got_a.shape[2]
+    bundle = side * rows
+    routes = ((a_ref, got_a, side), (b_ref, got_b, 1))
+    geo = []
+    for _, _, stride in routes:
+        coord = lax.rem(me // stride, side)
+        geo.append((coord, me - coord * stride))
+    barrier = pltpu.get_barrier_semaphore()
+    for (coord, base), (_, _, stride) in zip(geo, routes):
+        for k in range(1, side):
+            peer = base + lax.rem(coord + k, side) * stride
+            pl.semaphore_signal(barrier, 1, device_id={"dp": peer}, device_id_type=mesh_id)
+    pl.semaphore_wait(barrier, 2 * (side - 1))
+
+    def remote(r, k, source, to):
+        src, dst, stride = routes[r]
+        coord, base = geo[r]
+        return pltpu.make_async_remote_copy(
+            src_ref=src,
+            dst_ref=dst.at[source],
+            send_sem=send_sems.at[r, k - 1],
+            recv_sem=recv_sems.at[r, k - 1],
+            device_id={"dp": base + to * stride},
+            device_id_type=mesh_id,
+        )
+
+    locals_, sends = [], []
+    for r, (src, dst, stride) in enumerate(routes):
+        coord, base = geo[r]
+        local = pltpu.make_async_copy(src, dst.at[coord], local_sems.at[r])
+        local.start()
+        locals_.append(local)
+        for k in range(1, side):
+            copy = remote(r, k, coord, lax.rem(coord + k, side))
+            copy.start()
+            sends.append(copy)
+    acc_a[...] = jnp.zeros_like(acc_a)
+    acc_b[...] = jnp.zeros_like(acc_b)
+
+    def add_a(source):
+        block = got_a[source].reshape(bundle, got_a.shape[-1])
+        at = pl.ds(pl.multiple_of(source * bundle, bundle), bundle)
+        acc_a[...] += jnp.dot(ctx_ref[:, at], block, preferred_element_type=jnp.float32)
+
+    def add_b(source):
+        for x in range(side):
+            at = pl.ds(pl.multiple_of((x * side + source) * rows, rows), rows)
+            acc_b[...] += jnp.dot(ctx_ref[:, at], got_b[source, x], preferred_element_type=jnp.float32)
+
+    for local in locals_:
+        local.wait()
+    add_a(geo[0][0])
+    add_b(geo[1][0])
+    for k in range(1, side):
+        for r, add in ((0, add_a), (1, add_b)):
+            coord, _ = geo[r]
+            source = lax.rem(coord + side - k, side)
+            remote(r, k, source, source).wait_recv()
+            add(source)
+    half = acc_a.shape[1]
+    out_ref[:, :half] = (res_ref[:, :half].astype(jnp.float32) + acc_a[...]).astype(out_ref.dtype)
+    out_ref[:, half:] = (res_ref[:, half:].astype(jnp.float32) + acc_b[...]).astype(out_ref.dtype)
+    for copy in sends:
+        copy.wait_send()
+
+
+def gather_attend(w, context, residual, cid):
+    side = 4
+    half = w.shape[-1] // 2
+    first_a, first_b = dp_route([w[..., :half], w[..., half:]], (1, side), cid, gather=True)
+    vmem = pl.BlockSpec(memory_space=pltpu.VMEM)
+    return pl.pallas_call(
+        functools.partial(_gather_attend_kernel, side),
+        out_shape=jax.ShapeDtypeStruct(residual.shape, jnp.bfloat16),
+        in_specs=[pl.BlockSpec(memory_space=pl.ANY)] * 2 + [vmem] * 2,
+        out_specs=vmem,
+        scratch_shapes=[
+            pltpu.VMEM((side,) + first_a.shape, first_a.dtype),
+            pltpu.VMEM((side,) + first_b.shape, first_b.dtype),
+            pltpu.VMEM((context.shape[0], half), jnp.float32),
+            pltpu.VMEM((context.shape[0], half), jnp.float32),
+            pltpu.SemaphoreType.DMA((2,)),
+            pltpu.SemaphoreType.DMA((2, side - 1)),
+            pltpu.SemaphoreType.DMA((2, side - 1)),
+        ],
+        compiler_params=pltpu.CompilerParams(collective_id=cid + 1, has_side_effects=True),
+    )(first_a, first_b, context, residual)
+
+
 def _spread_kernel(n_dp, n_expert, chosen_ref, split_ref, pieces_ref, mine_ref,
                    held, outgoing, local_sems, dp_send, dp_recv, ex_send, ex_recv):
     me = lax.axis_index("dp")
@@ -517,17 +610,7 @@
     piece = BLK // n_dp
     my_expert = lax.axis_index("expert")
 
-    w_a, w_b = all_gather_2d(out_weight, cid=10)
-    w_a = w_a.reshape(model_width, -1)
-    w_b = w_b.reshape(model_width, -1)
-    projected = jnp.concatenate(
-        [
-            jnp.dot(context, w_a, preferred_element_type=jnp.float32),
-            jnp.dot(context, w_b, preferred_element_type=jnp.float32),
-        ],
-        axis=1,
-    )
-    attended = (residual.astype(jnp.float32) + projected).astype(jnp.bfloat16)
+    attended = gather_attend(out_weight, context, residual, cid=10)
 
     split = attended.reshape(local_blocks, n_dp, piece, local_width).transpose(1, 0, 2, 3)
     pieces, mine = spread_select(chosen_blocks.reshape(-1), split, cid=0)

time: 198 us -> 185 us (0.934)
  matrix products: 5.83 us -> 0.28 us
  local copies, waits for them, and re-layouts: 15.3 us -> 12.2 us
  Pallas kernels: 174 us -> 171 us
    pallas_call x3 -> x2, Pallas kernels: 58.1 us -> 22.9 us  [dp_route(): pl.pallas_call(functools.partial(_route_kernel, tuple(strides), side, gat...]
    pallas_call x0 -> x1, Pallas kernels: none -> 32.3 us  [gather_attend(): pl.pallas_call(functools.partial(_gather_attend_kernel, side), out_shape=...]
    dot_general x2 -> x0, matrix products: 5.55 us -> none  [the longest x1 4.26 us: body(): jnp.dot(context, w_a, preferred_element_type=jnp.float32)]
    unnamed x11 -> x14, local copies, waits for them, and re-layouts: 4.89 us -> 1.77 us
where the time goes in v13:
time: 185 us
  Pallas kernels  171 us (92%)
  local copies, waits for them, and re-layouts  12.2 us (7%)
    pallas_call x1, Pallas kernels, gather_gate(): pl.pallas_call(functools.partial(_gather_gate_kernel, side), out_shape=ja...  34.3 us
    pallas_call x1, Pallas kernels, down_scatter(): pl.pallas_call(functools.partial(_down_scatter_kernel, side), out_shape=[...  32.3 us
    pallas_call x1, Pallas kernels, gather_attend(): pl.pallas_call(functools.partial(_gather_attend_kernel, side), out_shape=...  32.3 us
    pallas_call x2, Pallas kernels, dp_route(): pl.pallas_call(functools.partial(_route_kernel, tuple(strides), side, gat...  22.9 us
    pallas_call x1, Pallas kernels, spread_select(): pl.pallas_call(functools.partial(_spread_kernel, n_dp, n_expert), out_sha...  19.6 us
    pallas_call x1, Pallas kernels, reduce_scatter_2d(): pl.pallas_call(functools.partial(_finish_kernel, side, n_expert), out_sha...  15.8 us
    pallas_call x1, Pallas kernels, dp_exchange(): pl.pallas_call(functools.partial(_exchange_kernel, n, gather, axis), out_...  13.5 us

profile of v13, /device:TPU:24, one launch (start us, length us, event | category | flops | bytes accessed | tf_op | source)
XLA Modules:
  0.0 184.6 jit_solution(413545068744892470)
XLA Ops:
  0.0 1.7 fusion.7
  1.7 12.2 %shard_map.91 = (bf16[4,256,256]{2,1,0:T(8,128)(2,1)}, bf16[4,256,256]{2,1,0:T(8,128)(2,1)}) custom-call(bf16[256,256]{1,0:T(8,128)(2,1)} %get-tuple-element.24.refs_0_, bf16[256,256]{1,0:T(8,128)(2,1)} %get-tuple-element.23.refs_1_), custom_call_target="tpu_custom_call" | custom-call | tf_op jit(solution)/shard_map/pallas_call | solution.py:103
  13.9 32.3 %shard_map.92 = bf16[512,512]{1,0:T(8,128)(2,1)} custom-call(bf16[4,256,256]{2,1,0:T(8,128)(2,1)} %get-tuple-element.13.a_ref, bf16[4,256,256]{2,1,0:T(8,128)(2,1)} %get-tuple-element.14.b_ref, bf16[512,4096]{1,0:T(8,128)(2,1)} %ctx_ref.1, bf16[512,512]{1,0:T(8,128)(2,1)} %res_ref.1), custom_call_target="tpu_custom_call" | custom-call | tf_op jit(solution)/shard_map/pallas_call | solution.py:486
  46.2 1.9 %copy.22 = bf16[4,16,8,512]{3,2,0,1:T(8,128)(2,1)} copy(bf16[4,16,8,512]{3,2,1,0:T(8,128)(2,1)} %bitcast.25) | data formatting | bytes 1048576 | tf_op jit(solution)/shard_map/reshape | solution.py:615
  48.2 0.7 reshape.31.chosen_ref
  48.8 19.6 %shard_map.93 = (bf16[64,8,512]{2,1,0:T(8,128)(2,1)}, bf16[8,4,8,512]{3,2,1,0:T(8,128)(2,1)}) custom-call(s32[32]{0:T(128)} %reshape.31.chosen_ref, bf16[16,4,8,512]{3,2,1,0:T(8,128)(2,1)} %bitcast.26), custom_call_target="tpu_custom_call" | custom-call | tf_op jit(solution)/shard_map/pallas_call | solution.py:571
  68.4 1.0 copy.15
  69.4 0.7 fusion.6
  70.1 10.7 %shard_map.94 = (bf16[4,32,2048]{2,1,0:T(8,128)(2,1)}, bf16[4,32,2048]{2,1,0:T(8,128)(2,1)}) custom-call(bf16[32,2048]{1,0:T(8,128)(2,1)} %get-tuple-element.22.refs_0_, bf16[32,2048]{1,0:T(8,128)(2,1)} %get-tuple-element.21.refs_1_), custom_call_target="tpu_custom_call" | custom-call | tf_op jit(solution)/shard_map/pallas_call | solution.py:103
  80.8 34.3 %shard_map.95.hidden_ref = bf16[512,512]{1,0:T(8,128)(2,1)} custom-call(bf16[4,32,2048]{2,1,0:T(8,128)(2,1)} %get-tuple-element.17.a_ref, bf16[4,32,2048]{2,1,0:T(8,128)(2,1)} %get-tuple-element.18.b_ref, bf16[4096,512]{1,0:T(8,128)(2,1)} %bitcast.22, bf16[4096,512]{1,0:T(8,128)(2,1)} %bitcast.23), custom_call_target="tpu_custom_call" | custom-call | tf_op jit(solution)/shard_map/pallas_call | solution.py:393
  115.2 0.6 dynamic_slice.4
  115.8 0.5 broadcast.42
  116.3 0.7 reduce.3
  116.9 0.1 squeeze.20
  117.0 0.6 select_bitcast_fusion
  117.7 0.8 broadcast_in_dim_reshape.5.scale_ref
  118.6 32.3 %shard_map.96 = (bf16[4,32,2048]{2,1,0:T(8,128)(2,1)}, bf16[4,32,2048]{2,1,0:T(8,128)(2,1)}) custom-call(bf16[512,512]{1,0:T(8,128)(2,1)} %shard_map.95.hidden_ref, bf16[512,4096]{1,0:T(8,128)(2,1)} %bitcast.21, f32[512,1]{1,0:T(8,128)} %broadcast_in_dim_reshape.5.scale_ref), custom_call_target="tpu_custom_call" | custom-call | tf_op jit(solution)/shard_map/pallas_call | solution.py:258
  150.9 15.8 %shard_map.97 = bf16[8,32,512]{2,1,0:T(8,128)(2,1)} custom-call(bf16[4,32,2048]{2,1,0:T(8,128)(2,1)} %get-tuple-element.19.a_ref, bf16[4,32,2048]{2,1,0:T(8,128)(2,1)} %get-tuple-element.20.b_ref), custom_call_target="tpu_custom_call" | custom-call | tf_op jit(solution)/shard_map/pallas_call | solution.py:282
  166.7 1.1 reshape.34
  167.8 0.2 copy.19
  168.0 0.3 fusion
  168.3 1.0 copy.20
  169.2 13.5 %shard_map.98 = bf16[16,4,8,512]{3,2,1,0:T(8,128)(2,1)} custom-call(bf16[16,4,8,512]{3,2,1,0:T(8,128)(2,1)} %bitcast.27), custom_call_target="tpu_custom_call" | custom-call | tf_op jit(solution)/shard_map/pallas_call | solution.py:44
  182.8 1.9 %copy.18 = bf16[4,16,8,512]{3,2,1,0:T(8,128)(2,1)} copy(bf16[4,16,8,512]{3,2,0,1:T(8,128)(2,1)} %bitcast.28) | data formatting | bytes 1048576 | tf_op jit(solution)/shard_map/transpose | solution.py:638
  (12 shorter events, 0.1 us)
Async XLA Ops:
  0.0 48.1 %copy-start.2 = (s32[8,4]{0,1:T(4,128)S(1)}, s32[8,4]{0,1:T(4,128)}, u32[]{:S(2)}) copy-start(s32[8,4]{0,1:T(4,128)} %param.16) | copy-start | bytes 388
  80.8 34.4 %copy-start.4 = (s32[8]{0:T(128)S(1)}, s32[8]{0:T(128)}, u32[]{:S(2)}) copy-start(s32[8]{0:T(128)} %param.17) | copy-start | bytes 100
  80.8 35.5 %copy-start.3 = (f32[1,512]{1,0:T(1,128)S(1)}, f32[1,512]{1,0:T(1,128)}, u32[]{:S(2)}) copy-start(f32[1,512]{1,0:T(1,128)} %param.15) | copy-start | bytes 6148
  115.1 52.6 %copy-start = (bf16[64,8,512]{2,1,0:T(8,128)(2,1)S(1)}, bf16[64,8,512]{2,1,0:T(8,128)(2,1)}, u32[]{:S(2)}) copy-start(bf16[64,8,512]{2,1,0:T(8,128)(2,1)} %get-tuple-element.15) | copy-start | bytes 1572868
  118.6 49.4 %copy-start.1 = (s32[32]{0:T(128)S(1)}, s32[32]{0:T(128)}, u32[]{:S(2)}) copy-start(s32[32]{0:T(128)} %reshape.31.chosen_ref) | copy-start | bytes 388

commit v14 on v13

--- a/solution.py
+++ b/solution.py
@@ -55,12 +55,19 @@
     )(x)
 
 
-def _route_kernel(strides, side, gather, *refs):
+def _route_kernel(strides, side, gather, windows, *refs):
     n_in = len(strides)
     ins, outs = refs[:n_in], refs[n_in:2 * n_in]
     local_sems, send_sems, recv_sems = refs[2 * n_in:]
     me = lax.axis_index("dp")
     mesh_id = pl.DeviceIdType.MESH
+
+    def window(r):
+        if windows is None:
+            return ins[r]
+        start, size = windows[r]
+        return ins[r].at[:, pl.ds(start, size)]
+
     routes = []
     for r, stride in enumerate(strides):
         coord = lax.rem(me // stride, side)
@@ -75,14 +82,14 @@
     locals_ = []
     for r in range(n_in):
         coord = lax.rem(me // strides[r], side)
-        source = ins[r] if gather else ins[r].at[coord]
+        source = window(r) if gather else ins[r].at[coord]
         local = pltpu.make_async_copy(source, outs[r].at[coord], local_sems.at[r])
         local.start()
         locals_.append(local)
     copies = []
     for i, (r, coord, to, target) in enumerate(routes):
         copy = pltpu.make_async_remote_copy(
-            src_ref=ins[r] if gather else ins[r].at[to],
+            src_ref=window(r) if gather else ins[r].at[to],
             dst_ref=outs[r].at[coord],
             send_sem=send_sems.at[i],
             recv_sem=recv_sems.at[i],
@@ -97,11 +104,14 @@
         copy.wait()
 
 
-def dp_route(xs, strides, cid, side=4, gather=False):
+def dp_route(xs, strides, cid, side=4, gather=False, windows=None):
     n_routes = len(strides) * (side - 1)
-    shapes = [((side,) + x.shape) if gather else x.shape for x in xs]
+    if windows is not None:
+        shapes = [(side, x.shape[0], size) for x, (_, size) in zip(xs, windows)]
+    else:
+        shapes = [((side,) + x.shape) if gather else x.shape for x in xs]
     return pl.pallas_call(
-        functools.partial(_route_kernel, tuple(strides), side, gather),
+        functools.partial(_route_kernel, tuple(strides), side, gather, windows),
         out_shape=[jax.ShapeDtypeStruct(s, x.dtype) for s, x in zip(shapes, xs)],
         in_specs=[pl.BlockSpec(memory_space=pl.ANY)] * len(xs),
         out_specs=[pl.BlockSpec(memory_space=pl.ANY)] * len(xs),
@@ -301,7 +311,7 @@
 def all_gather_2d(x, cid):
     side = 4
     half = x.shape[-1] // 2
-    got_a, got_b = dp_route([x[..., :half], x[..., half:]], (1, side), cid, gather=True)
+    got_a, got_b = dp_route([x, x], (1, side), cid, gather=True, windows=((0, half), (half, half)))
     got_a, got_b = dp_route([got_a, got_b], (side, 1), cid + 1, gather=True)
     n = side * side
     got_a = got_a.reshape((n,) + got_a.shape[2:])
@@ -389,7 +399,7 @@
     side = 4
     n = side * side
     half = x.shape[-1] // 2
-    first_a, first_b = dp_route([x[..., :half], x[..., half:]], (1, side), cid, gather=True)
+    first_a, first_b = dp_route([x, x], (1, side), cid, gather=True, windows=((0, half), (half, half)))
     return pl.pallas_call(
         functools.partial(_gather_gate_kernel, side),
         out_shape=jax.ShapeDtypeStruct((n * x.shape[0], w_gate.shape[1]), jnp.bfloat16),
@@ -481,7 +491,7 @@
 def gather_attend(w, context, residual, cid):
     side = 4
     half = w.shape[-1] // 2
-    first_a, first_b = dp_route([w[..., :half], w[..., half:]], (1, side), cid, gather=True)
+    first_a, first_b = dp_route([w, w], (1, side), cid, gather=True, windows=((0, half), (half, half)))
     vmem = pl.BlockSpec(memory_space=pltpu.VMEM)
     return pl.pallas_call(
         functools.partial(_gather_attend_kernel, side),

time: 185 us -> 183 us (0.989)
    slice x2 -> x0, local copies, waits for them, and re-layouts: 2.41 us -> none  [the longest x1 1.7 us: gather_attend(): w[..., half:]]
where the time goes in v14:
time: 183 us
  Pallas kernels  171 us (93%)
  local copies, waits for them, and re-layouts  10.5 us (6%)
    pallas_call x1, Pallas kernels, gather_gate(): pl.pallas_call(functools.partial(_gather_gate_kernel, side), out_shape=ja...  34.3 us
    pallas_call x1, Pallas kernels, down_scatter(): pl.pallas_call(functools.partial(_down_scatter_kernel, side), out_shape=[...  32.3 us
    pallas_call x1, Pallas kernels, gather_attend(): pl.pallas_call(functools.partial(_gather_attend_kernel, side), out_shape=...  32.3 us
    pallas_call x2, Pallas kernels, dp_route(): pl.pallas_call(functools.partial(_route_kernel, tuple(strides), side, gat...  22.9 us
    pallas_call x1, Pallas kernels, spread_select(): pl.pallas_call(functools.partial(_spread_kernel, n_dp, n_expert), out_sha...  19.6 us
    pallas_call x1, Pallas kernels, reduce_scatter_2d(): pl.pallas_call(functools.partial(_finish_kernel, side, n_expert), out_sha...  15.8 us
    pallas_call x1, Pallas kernels, dp_exchange(): pl.pallas_call(functools.partial(_exchange_kernel, n, gather, axis), out_...  13.5 us

profile of v14, /device:TPU:24, one launch (start us, length us, event | category | flops | bytes accessed | tf_op | source)
XLA Modules:
  0.0 182.9 jit_solution(7857047695344855073)
XLA Ops:
  0.0 12.2 %shard_map.91 = (bf16[4,256,256]{2,1,0:T(8,128)(2,1)}, bf16[4,256,256]{2,1,0:T(8,128)(2,1)}) custom-call(bf16[256,512]{1,0:T(8,128)(2,1)} %refs_1_.1, bf16[256,512]{1,0:T(8,128)(2,1)} %refs_1_.1), custom_call_target="tpu_custom_call" | custom-call | tf_op jit(solution)/shard_map/pallas_call | solution.py:113
  12.2 32.3 %shard_map.92 = bf16[512,512]{1,0:T(8,128)(2,1)} custom-call(bf16[4,256,256]{2,1,0:T(8,128)(2,1)} %get-tuple-element.13.a_ref, bf16[4,256,256]{2,1,0:T(8,128)(2,1)} %get-tuple-element.14.b_ref, bf16[512,4096]{1,0:T(8,128)(2,1)} %ctx_ref.1, bf16[512,512]{1,0:T(8,128)(2,1)} %res_ref.1), custom_call_target="tpu_custom_call" | custom-call | tf_op jit(solution)/shard_map/pallas_call | solution.py:496
  44.5 1.9 %copy.22 = bf16[4,16,8,512]{3,2,0,1:T(8,128)(2,1)} copy(bf16[4,16,8,512]{3,2,1,0:T(8,128)(2,1)} %bitcast.27) | data formatting | bytes 1048576 | tf_op jit(solution)/shard_map/reshape | solution.py:625
  46.4 0.1 copy.13
  46.5 0.7 reshape.31.chosen_ref
  47.1 19.6 %shard_map.93 = (bf16[64,8,512]{2,1,0:T(8,128)(2,1)}, bf16[8,4,8,512]{3,2,1,0:T(8,128)(2,1)}) custom-call(s32[32]{0:T(128)} %reshape.31.chosen_ref, bf16[16,4,8,512]{3,2,1,0:T(8,128)(2,1)} %bitcast.28), custom_call_target="tpu_custom_call" | custom-call | tf_op jit(solution)/shard_map/pallas_call | solution.py:581
  66.7 1.7 copy.15
  68.4 10.7 %shard_map.94 = (bf16[4,32,2048]{2,1,0:T(8,128)(2,1)}, bf16[4,32,2048]{2,1,0:T(8,128)(2,1)}) custom-call(bf16[32,4096]{1,0:T(8,128)(2,1)} %bitcast.25, bf16[32,4096]{1,0:T(8,128)(2,1)} %bitcast.26), custom_call_target="tpu_custom_call" | custom-call | tf_op jit(solution)/shard_map/pallas_call | solution.py:113
  79.1 0.0 copy-start.4
  79.1 34.3 %shard_map.95.hidden_ref = bf16[512,512]{1,0:T(8,128)(2,1)} custom-call(bf16[4,32,2048]{2,1,0:T(8,128)(2,1)} %get-tuple-element.17.a_ref, bf16[4,32,2048]{2,1,0:T(8,128)(2,1)} %get-tuple-element.18.b_ref, bf16[4096,512]{1,0:T(8,128)(2,1)} %bitcast.22, bf16[4096,512]{1,0:T(8,128)(2,1)} %bitcast.23), custom_call_target="tpu_custom_call" | custom-call | tf_op jit(solution)/shard_map/pallas_call | solution.py:403
  113.4 0.6 dynamic_slice.4
  114.1 0.5 broadcast.42
  114.6 0.7 reduce.3
  115.2 0.1 squeeze.20
  115.3 0.7 select_bitcast_fusion
  116.0 0.8 broadcast_in_dim_reshape.5.scale_ref
  116.9 32.3 %shard_map.96 = (bf16[4,32,2048]{2,1,0:T(8,128)(2,1)}, bf16[4,32,2048]{2,1,0:T(8,128)(2,1)}) custom-call(bf16[512,512]{1,0:T(8,128)(2,1)} %shard_map.95.hidden_ref, bf16[512,4096]{1,0:T(8,128)(2,1)} %bitcast.21, f32[512,1]{1,0:T(8,128)} %broadcast_in_dim_reshape.5.scale_ref), custom_call_target="tpu_custom_call" | custom-call | tf_op jit(solution)/shard_map/pallas_call | solution.py:268
  149.2 15.8 %shard_map.97 = bf16[8,32,512]{2,1,0:T(8,128)(2,1)} custom-call(bf16[4,32,2048]{2,1,0:T(8,128)(2,1)} %get-tuple-element.19.a_ref, bf16[4,32,2048]{2,1,0:T(8,128)(2,1)} %get-tuple-element.20.b_ref), custom_call_target="tpu_custom_call" | custom-call | tf_op jit(solution)/shard_map/pallas_call | solution.py:292
  165.0 1.1 reshape.34
  166.1 0.2 copy.19
  166.3 0.3 fusion
  166.6 1.0 copy.20
  167.5 13.5 %shard_map.98 = bf16[16,4,8,512]{3,2,1,0:T(8,128)(2,1)} custom-call(bf16[16,4,8,512]{3,2,1,0:T(8,128)(2,1)} %bitcast.29), custom_call_target="tpu_custom_call" | custom-call | tf_op jit(solution)/shard_map/pallas_call | solution.py:44
  181.0 1.9 %copy.18 = bf16[4,16,8,512]{3,2,1,0:T(8,128)(2,1)} copy(bf16[4,16,8,512]{3,2,0,1:T(8,128)(2,1)} %bitcast.30) | data formatting | bytes 1048576 | tf_op jit(solution)/shard_map/transpose | solution.py:648
  (10 shorter events, 0.0 us)
Async XLA Ops:
  0.0 46.4 %copy-start.2 = (s32[8,4]{0,1:T(4,128)S(1)}, s32[8,4]{0,1:T(4,128)}, u32[]{:S(2)}) copy-start(s32[8,4]{0,1:T(4,128)} %param.16) | copy-start | bytes 388
  79.1 34.4 %copy-start.4 = (s32[8]{0:T(128)S(1)}, s32[8]{0:T(128)}, u32[]{:S(2)}) copy-start(s32[8]{0:T(128)} %param.17) | copy-start | bytes 100
  79.1 35.5 %copy-start.3 = (f32[1,512]{1,0:T(1,128)S(1)}, f32[1,512]{1,0:T(1,128)}, u32[]{:S(2)}) copy-start(f32[1,512]{1,0:T(1,128)} %param.15) | copy-start | bytes 6148
  113.4 52.7 %copy-start = (bf16[64,8,512]{2,1,0:T(8,128)(2,1)S(1)}, bf16[64,8,512]{2,1,0:T(8,128)(2,1)}, u32[]{:S(2)}) copy-start(bf16[64,8,512]{2,1,0:T(8,128)(2,1)} %get-tuple-element.15) | copy-start | bytes 1572868
  116.9 49.4 %copy-start.1 = (s32[32]{0:T(128)S(1)}, s32[32]{0:T(128)}, u32[]{:S(2)}) copy-start(s32[32]{0:T(128)} %reshape.31.chosen_ref) | copy-start | bytes 388

commit v15 on v14

--- a/solution.py
+++ b/solution.py
@@ -549,17 +549,20 @@
         copy.wait()
     keep = pltpu.make_async_copy(held, pieces_ref, local_sems.at[1])
     keep.start()
+    rows = held.shape[1]
+    width = held.shape[2]
     for e in range(n_expert):
         for s in range(CAP):
-            outgoing[e, s] = held[chosen_ref[e * CAP + s]]
-    local = pltpu.make_async_copy(outgoing.at[mine_e], mine_ref.at[mine_e], local_sems.at[2])
+            outgoing[e, s * rows:(s + 1) * rows] = held[chosen_ref[e * CAP + s]]
+    columns = pl.ds(pl.multiple_of(mine_e * width, width), width)
+    local = pltpu.make_async_copy(outgoing.at[mine_e], mine_ref.at[:, columns], local_sems.at[2])
     local.start()
     copies = []
     for k in range(1, n_expert):
         target = lax.rem(mine_e + k, n_expert)
         copy = pltpu.make_async_remote_copy(
             src_ref=outgoing.at[target],
-            dst_ref=mine_ref.at[mine_e],
+            dst_ref=mine_ref.at[:, columns],
             send_sem=ex_send.at[k - 1],
             recv_sem=ex_recv.at[k - 1],
             device_id={"expert": target},
@@ -582,13 +585,13 @@
         functools.partial(_spread_kernel, n_dp, n_expert),
         out_shape=[
             jax.ShapeDtypeStruct((n_blocks, rows, width), split.dtype),
-            jax.ShapeDtypeStruct((n_expert, CAP, rows, width), split.dtype),
+            jax.ShapeDtypeStruct((CAP * rows, n_expert * width), split.dtype),
         ],
         in_specs=[pl.BlockSpec(memory_space=pltpu.SMEM), pl.BlockSpec(memory_space=pl.ANY)],
         out_specs=[pl.BlockSpec(memory_space=pl.ANY)] * 2,
         scratch_shapes=[
             pltpu.VMEM((n_blocks, rows, width), split.dtype),
-            pltpu.VMEM((n_expert, CAP, rows, width), split.dtype),
+            pltpu.VMEM((n_expert, CAP * rows, width), split.dtype),
             pltpu.SemaphoreType.DMA((3,)),
             pltpu.SemaphoreType.DMA((n_dp - 1,)),
             pltpu.SemaphoreType.DMA((n_dp - 1,)),
@@ -624,7 +627,6 @@
 
     split = attended.reshape(local_blocks, n_dp, piece, local_width).transpose(1, 0, 2, 3)
     pieces, mine = spread_select(chosen_blocks.reshape(-1), split, cid=0)
-    mine = mine.transpose(1, 2, 0, 3).reshape(CAP * piece, model_width)
     w_gate = gate_weight[0]
     w_up = up_weight[0]
     w_down = down_weight[0]

time: 183 us -> 182 us (level)
  no operation moved by 1% of the time
where the time goes in v15:
time: 182 us; the launch traced here: 181 us
  Pallas kernels  171 us (94%)
  local copies, waits for them, and re-layouts  8.82 us (5%)
    pallas_call x1, Pallas kernels, gather_gate(): pl.pallas_call(functools.partial(_gather_gate_kernel, side), out_shape=ja...  34.3 us
    pallas_call x1, Pallas kernels, down_scatter(): pl.pallas_call(functools.partial(_down_scatter_kernel, side), out_shape=[...  32.3 us
    pallas_call x1, Pallas kernels, gather_attend(): pl.pallas_call(functools.partial(_gather_attend_kernel, side), out_shape=...  32.3 us
    pallas_call x2, Pallas kernels, dp_route(): pl.pallas_call(functools.partial(_route_kernel, tuple(strides), side, gat...  23 us
    pallas_call x1, Pallas kernels, spread_select(): pl.pallas_call(functools.partial(_spread_kernel, n_dp, n_expert), out_sha...  19.6 us
    pallas_call x1, Pallas kernels, reduce_scatter_2d(): pl.pallas_call(functools.partial(_finish_kernel, side, n_expert), out_sha...  15.8 us
    pallas_call x1, Pallas kernels, dp_exchange(): pl.pallas_call(functools.partial(_exchange_kernel, n, gather, axis), out_...  13.4 us

profile of v15, /device:TPU:24, one launch (start us, length us, event | category | flops | bytes accessed | tf_op | source)
XLA Modules:
  0.0 181.3 jit_solution(5954041845599753127)
XLA Ops:
  0.0 12.2 %shard_map.91 = (bf16[4,256,256]{2,1,0:T(8,128)(2,1)}, bf16[4,256,256]{2,1,0:T(8,128)(2,1)}) custom-call(bf16[256,512]{1,0:T(8,128)(2,1)} %refs_1_.1, bf16[256,512]{1,0:T(8,128)(2,1)} %refs_1_.1), custom_call_target="tpu_custom_call" | custom-call | tf_op jit(solution)/shard_map/pallas_call | solution.py:113
  12.2 32.3 %shard_map.92 = bf16[512,512]{1,0:T(8,128)(2,1)} custom-call(bf16[4,256,256]{2,1,0:T(8,128)(2,1)} %get-tuple-element.13.a_ref, bf16[4,256,256]{2,1,0:T(8,128)(2,1)} %get-tuple-element.14.b_ref, bf16[512,4096]{1,0:T(8,128)(2,1)} %ctx_ref.1, bf16[512,512]{1,0:T(8,128)(2,1)} %res_ref.1), custom_call_target="tpu_custom_call" | custom-call | tf_op jit(solution)/shard_map/pallas_call | solution.py:496
  44.5 1.9 %copy.20 = bf16[4,16,8,512]{3,2,0,1:T(8,128)(2,1)} copy(bf16[4,16,8,512]{3,2,1,0:T(8,128)(2,1)} %bitcast.23) | data formatting | bytes 1048576 | tf_op jit(solution)/shard_map/reshape | solution.py:628
  46.4 0.1 copy.12
  46.5 0.7 reshape.28.chosen_ref
  47.1 19.6 %shard_map.93 = (bf16[64,8,512]{2,1,0:T(8,128)(2,1)}, bf16[32,4096]{1,0:T(8,128)(2,1)}) custom-call(s32[32]{0:T(128)} %reshape.28.chosen_ref, bf16[16,4,8,512]{3,2,1,0:T(8,128)(2,1)} %bitcast.24), custom_call_target="tpu_custom_call" | custom-call | tf_op jit(solution)/shard_map/pallas_call | solution.py:584
  66.7 10.8 %shard_map.94 = (bf16[4,32,2048]{2,1,0:T(8,128)(2,1)}, bf16[4,32,2048]{2,1,0:T(8,128)(2,1)}) custom-call(bf16[32,4096]{1,0:T(8,128)(2,1)} %get-tuple-element.16.refs_0_.refs_1_, bf16[32,4096]{1,0:T(8,128)(2,1)} %get-tuple-element.16.refs_0_.refs_1_), custom_call_target="tpu_custom_call" | custom-call | tf_op jit(solution)/shard_map/pallas_call | solution.py:113
  77.5 0.0 copy-start.4
  77.5 0.0 copy-start.3
  77.6 34.3 %shard_map.95.hidden_ref = bf16[512,512]{1,0:T(8,128)(2,1)} custom-call(bf16[4,32,2048]{2,1,0:T(8,128)(2,1)} %get-tuple-element.17.a_ref, bf16[4,32,2048]{2,1,0:T(8,128)(2,1)} %get-tuple-element.18.b_ref, bf16[4096,512]{1,0:T(8,128)(2,1)} %bitcast.20, bf16[4096,512]{1,0:T(8,128)(2,1)} %bitcast.21), custom_call_target="tpu_custom_call" | custom-call | tf_op jit(solution)/shard_map/pallas_call | solution.py:403
  111.9 0.6 dynamic_slice.4
  112.5 0.5 broadcast.42
  113.0 0.7 reduce.3
  113.7 0.1 squeeze.20
  113.8 0.7 select_bitcast_fusion
  114.5 0.8 broadcast_in_dim_reshape.5.scale_ref
  115.3 32.3 %shard_map.96 = (bf16[4,32,2048]{2,1,0:T(8,128)(2,1)}, bf16[4,32,2048]{2,1,0:T(8,128)(2,1)}) custom-call(bf16[512,512]{1,0:T(8,128)(2,1)} %shard_map.95.hidden_ref, bf16[512,4096]{1,0:T(8,128)(2,1)} %bitcast.19, f32[512,1]{1,0:T(8,128)} %broadcast_in_dim_reshape.5.scale_ref), custom_call_target="tpu_custom_call" | custom-call | tf_op jit(solution)/shard_map/pallas_call | solution.py:268
  147.7 15.8 %shard_map.97 = bf16[8,32,512]{2,1,0:T(8,128)(2,1)} custom-call(bf16[4,32,2048]{2,1,0:T(8,128)(2,1)} %get-tuple-element.19.a_ref, bf16[4,32,2048]{2,1,0:T(8,128)(2,1)} %get-tuple-element.20.b_ref), custom_call_target="tpu_custom_call" | custom-call | tf_op jit(solution)/shard_map/pallas_call | solution.py:292
  163.5 1.1 reshape.30
  164.6 0.2 copy.17
  164.8 0.3 fusion
  165.0 1.0 copy.18
  166.0 13.4 %shard_map.98 = bf16[16,4,8,512]{3,2,1,0:T(8,128)(2,1)} custom-call(bf16[16,4,8,512]{3,2,1,0:T(8,128)(2,1)} %bitcast.25), custom_call_target="tpu_custom_call" | custom-call | tf_op jit(solution)/shard_map/pallas_call | solution.py:44
  179.5 1.9 %copy.16 = bf16[4,16,8,512]{3,2,1,0:T(8,128)(2,1)} copy(bf16[4,16,8,512]{3,2,0,1:T(8,128)(2,1)} %bitcast.26) | data formatting | bytes 1048576 | tf_op jit(solution)/shard_map/transpose | solution.py:650
  (9 shorter events, 0.0 us)
Async XLA Ops:
  0.0 46.4 %copy-start.2 = (s32[8,4]{0,1:T(4,128)S(1)}, s32[8,4]{0,1:T(4,128)}, u32[]{:S(2)}) copy-start(s32[8,4]{0,1:T(4,128)} %param.16) | copy-start | bytes 388
  77.5 34.4 %copy-start.4 = (s32[8]{0:T(128)S(1)}, s32[8]{0:T(128)}, u32[]{:S(2)}) copy-start(s32[8]{0:T(128)} %param.17) | copy-start | bytes 100
  77.5 35.5 %copy-start.3 = (f32[1,512]{1,0:T(1,128)S(1)}, f32[1,512]{1,0:T(1,128)}, u32[]{:S(2)}) copy-start(f32[1,512]{1,0:T(1,128)} %param.15) | copy-start | bytes 6148
  111.9 52.7 %copy-start = (bf16[64,8,512]{2,1,0:T(8,128)(2,1)S(1)}, bf16[64,8,512]{2,1,0:T(8,128)(2,1)}, u32[]{:S(2)}) copy-start(bf16[64,8,512]{2,1,0:T(8,128)(2,1)} %get-tuple-element.15) | copy-start | bytes 1572868
  115.3 49.4 %copy-start.1 = (s32[32]{0:T(128)S(1)}, s32[32]{0:T(128)}, u32[]{:S(2)}) copy-start(s32[32]{0:T(128)} %reshape.28.chosen_ref) | copy-start | bytes 388

commit v16 on v15

--- a/solution.py
+++ b/solution.py
@@ -631,10 +631,10 @@
     w_up = up_weight[0]
     w_down = down_weight[0]
     gate_row = gate_values[0]
-    my_count = lax.dynamic_index_in_dim(block_counts, my_expert, 0, keepdims=False)
-    live = jnp.arange(CAP * BLK) // BLK < my_count
-    scale = jnp.where(live, gate_row, jnp.zeros_like(gate_row))
-    scale = scale.reshape(CAP, n_dp, piece).transpose(1, 0, 2).reshape(-1)
+    my_count = jnp.sum(jnp.where(jnp.arange(n_expert) == my_expert, block_counts, 0))
+    row_slot = (jnp.arange(CAP * BLK) // piece) % CAP
+    gate_perm = gate_row.reshape(CAP, n_dp, piece).transpose(1, 0, 2).reshape(-1)
+    scale = jnp.where(row_slot < my_count, gate_perm, jnp.zeros_like(gate_perm))
 
     hidden = gather_gate(mine, w_gate, w_up, cid=20)
     halves = down_scatter(hidden, w_down, scale[:, None], cid=1)

time: 182 us -> 182 us (level)
  no operation moved by 1% of the time
where the time goes in v16:
time: 182 us; the launch traced here: 181 us
  Pallas kernels  171 us (94%)
  local copies, waits for them, and re-layouts  7.5 us (4%)
  other arithmetic  2.59 us (1%)
    pallas_call x1, Pallas kernels, gather_gate(): pl.pallas_call(functools.partial(_gather_gate_kernel, side), out_shape=ja...  34.3 us
    pallas_call x1, Pallas kernels, down_scatter(): pl.pallas_call(functools.partial(_down_scatter_kernel, side), out_shape=[...  32.3 us
    pallas_call x1, Pallas kernels, gather_attend(): pl.pallas_call(functools.partial(_gather_attend_kernel, side), out_shape=...  32.3 us
    pallas_call x2, Pallas kernels, dp_route(): pl.pallas_call(functools.partial(_route_kernel, tuple(strides), side, gat...  23 us
    pallas_call x1, Pallas kernels, spread_select(): pl.pallas_call(functools.partial(_spread_kernel, n_dp, n_expert), out_sha...  19.6 us
    pallas_call x1, Pallas kernels, reduce_scatter_2d(): pl.pallas_call(functools.partial(_finish_kernel, side, n_expert), out_sha...  15.8 us
    pallas_call x1, Pallas kernels, dp_exchange(): pl.pallas_call(functools.partial(_exchange_kernel, n, gather, axis), out_...  13.5 us

profile of v16, /device:TPU:24, one launch (start us, length us, event | category | flops | bytes accessed | tf_op | source)
XLA Modules:
  0.0 181.2 jit_solution(18234848798736527782)
XLA Ops:
  0.0 12.2 %shard_map.91 = (bf16[4,256,256]{2,1,0:T(8,128)(2,1)}, bf16[4,256,256]{2,1,0:T(8,128)(2,1)}) custom-call(bf16[256,512]{1,0:T(8,128)(2,1)} %refs_1_.1, bf16[256,512]{1,0:T(8,128)(2,1)} %refs_1_.1), custom_call_target="tpu_custom_call" | custom-call | tf_op jit(solution)/shard_map/pallas_call | solution.py:113
  12.2 32.3 %shard_map.92 = bf16[512,512]{1,0:T(8,128)(2,1)} custom-call(bf16[4,256,256]{2,1,0:T(8,128)(2,1)} %get-tuple-element.13.a_ref, bf16[4,256,256]{2,1,0:T(8,128)(2,1)} %get-tuple-element.14.b_ref, bf16[512,4096]{1,0:T(8,128)(2,1)} %ctx_ref.1, bf16[512,512]{1,0:T(8,128)(2,1)} %res_ref.1), custom_call_target="tpu_custom_call" | custom-call | tf_op jit(solution)/shard_map/pallas_call | solution.py:496
  44.5 1.9 %copy.20 = bf16[4,16,8,512]{3,2,0,1:T(8,128)(2,1)} copy(bf16[4,16,8,512]{3,2,1,0:T(8,128)(2,1)} %bitcast.21) | data formatting | bytes 1048576 | tf_op jit(solution)/shard_map/reshape | solution.py:628
  46.4 0.1 copy.12
  46.5 0.6 reshape.102.chosen_ref
  47.1 19.6 %shard_map.93 = (bf16[64,8,512]{2,1,0:T(8,128)(2,1)}, bf16[32,4096]{1,0:T(8,128)(2,1)}) custom-call(s32[32]{0:T(128)} %reshape.102.chosen_ref, bf16[16,4,8,512]{3,2,1,0:T(8,128)(2,1)} %bitcast.22), custom_call_target="tpu_custom_call" | custom-call | tf_op jit(solution)/shard_map/pallas_call | solution.py:584
  66.7 10.8 %shard_map.94 = (bf16[4,32,2048]{2,1,0:T(8,128)(2,1)}, bf16[4,32,2048]{2,1,0:T(8,128)(2,1)}) custom-call(bf16[32,4096]{1,0:T(8,128)(2,1)} %get-tuple-element.16.refs_0_.refs_1_, bf16[32,4096]{1,0:T(8,128)(2,1)} %get-tuple-element.16.refs_0_.refs_1_), custom_call_target="tpu_custom_call" | custom-call | tf_op jit(solution)/shard_map/pallas_call | solution.py:113
  77.5 0.0 copy-start.3
  77.5 0.0 copy-start.4
  77.6 34.3 %shard_map.95.hidden_ref = bf16[512,512]{1,0:T(8,128)(2,1)} custom-call(bf16[4,32,2048]{2,1,0:T(8,128)(2,1)} %get-tuple-element.17.a_ref, bf16[4,32,2048]{2,1,0:T(8,128)(2,1)} %get-tuple-element.18.b_ref, bf16[4096,512]{1,0:T(8,128)(2,1)} %bitcast.18, bf16[4096,512]{1,0:T(8,128)(2,1)} %bitcast.19), custom_call_target="tpu_custom_call" | custom-call | tf_op jit(solution)/shard_map/pallas_call | solution.py:403
  111.9 0.5 broadcast.99
  112.4 0.7 reduce.3
  113.0 0.1 reshape_squeeze.3
  113.2 0.1 reshape.109
  113.3 0.6 fusion.8
  113.9 1.3 fusion.6.scale_ref
  115.2 32.3 %shard_map.96 = (bf16[4,32,2048]{2,1,0:T(8,128)(2,1)}, bf16[4,32,2048]{2,1,0:T(8,128)(2,1)}) custom-call(bf16[512,512]{1,0:T(8,128)(2,1)} %shard_map.95.hidden_ref, bf16[512,4096]{1,0:T(8,128)(2,1)} %bitcast.17, f32[512,1]{1,0:T(8,128)} %fusion.6.scale_ref), custom_call_target="tpu_custom_call" | custom-call | tf_op jit(solution)/shard_map/pallas_call | solution.py:268
  147.6 15.8 %shard_map.97 = bf16[8,32,512]{2,1,0:T(8,128)(2,1)} custom-call(bf16[4,32,2048]{2,1,0:T(8,128)(2,1)} %get-tuple-element.19.a_ref, bf16[4,32,2048]{2,1,0:T(8,128)(2,1)} %get-tuple-element.20.b_ref), custom_call_target="tpu_custom_call" | custom-call | tf_op jit(solution)/shard_map/pallas_call | solution.py:292
  163.3 1.1 reshape.105
  164.4 0.2 copy.17
  164.6 0.3 fusion
  164.9 1.0 copy.18
  165.9 13.5 %shard_map.98 = bf16[16,4,8,512]{3,2,1,0:T(8,128)(2,1)} custom-call(bf16[16,4,8,512]{3,2,1,0:T(8,128)(2,1)} %bitcast.23), custom_call_target="tpu_custom_call" | custom-call | tf_op jit(solution)/shard_map/pallas_call | solution.py:44
  179.4 1.9 %copy.16 = bf16[4,16,8,512]{3,2,1,0:T(8,128)(2,1)} copy(bf16[4,16,8,512]{3,2,0,1:T(8,128)(2,1)} %bitcast.24) | data formatting | bytes 1048576 | tf_op jit(solution)/shard_map/transpose | solution.py:650
  (9 shorter events, 0.0 us)
Async XLA Ops:
  0.0 46.4 %copy-start.2 = (s32[8,4]{0,1:T(4,128)S(1)}, s32[8,4]{0,1:T(4,128)}, u32[]{:S(2)}) copy-start(s32[8,4]{0,1:T(4,128)} %param.16) | copy-start | bytes 388
  77.5 34.9 %copy-start.3 = (f32[1,512]{1,0:T(1,128)S(1)}, f32[1,512]{1,0:T(1,128)}, u32[]{:S(2)}) copy-start(f32[1,512]{1,0:T(1,128)} %param.15) | copy-start | bytes 6148
  77.5 35.8 %copy-start.4 = (s32[8]{0:T(128)S(1)}, s32[8]{0:T(128)}, u32[]{:S(2)}) copy-start(s32[8]{0:T(128)} %param.17) | copy-start | bytes 100
  111.9 52.6 %copy-start = (bf16[64,8,512]{2,1,0:T(8,128)(2,1)S(1)}, bf16[64,8,512]{2,1,0:T(8,128)(2,1)}, u32[]{:S(2)}) copy-start(bf16[64,8,512]{2,1,0:T(8,128)(2,1)} %get-tuple-element.15) | copy-start | bytes 1572868
  115.2 49.4 %copy-start.1 = (s32[32]{0:T(128)S(1)}, s32[32]{0:T(128)}, u32[]{:S(2)}) copy-start(s32[32]{0:T(128)} %reshape.102.chosen_ref) | copy-start | bytes 388

commit v17 on v16

--- a/solution.py
+++ b/solution.py
@@ -482,20 +482,28 @@
             remote(r, k, source, source).wait_recv()
             add(source)
     half = acc_a.shape[1]
-    out_ref[:, :half] = (res_ref[:, :half].astype(jnp.float32) + acc_a[...]).astype(out_ref.dtype)
-    out_ref[:, half:] = (res_ref[:, half:].astype(jnp.float32) + acc_b[...]).astype(out_ref.dtype)
+    n_pieces, n_local, piece = out_ref.shape[:3]
+    for b in range(n_local):
+        for k in range(n_pieces):
+            at = b * n_pieces * piece + k * piece
+            out_ref[k, b, :, :half] = (
+                res_ref[at:at + piece, :half].astype(jnp.float32) + acc_a[at:at + piece]
+            ).astype(out_ref.dtype)
+            out_ref[k, b, :, half:] = (
+                res_ref[at:at + piece, half:].astype(jnp.float32) + acc_b[at:at + piece]
+            ).astype(out_ref.dtype)
     for copy in sends:
         copy.wait_send()
 
 
-def gather_attend(w, context, residual, cid):
+def gather_attend(w, context, residual, cid, layout):
     side = 4
     half = w.shape[-1] // 2
     first_a, first_b = dp_route([w, w], (1, side), cid, gather=True, windows=((0, half), (half, half)))
     vmem = pl.BlockSpec(memory_space=pltpu.VMEM)
     return pl.pallas_call(
         functools.partial(_gather_attend_kernel, side),
-        out_shape=jax.ShapeDtypeStruct(residual.shape, jnp.bfloat16),
+        out_shape=jax.ShapeDtypeStruct(layout, jnp.bfloat16),
         in_specs=[pl.BlockSpec(memory_space=pl.ANY)] * 2 + [vmem] * 2,
         out_specs=vmem,
         scratch_shapes=[
@@ -623,9 +631,10 @@
     piece = BLK // n_dp
     my_expert = lax.axis_index("expert")
 
-    attended = gather_attend(out_weight, context, residual, cid=10)
-
-    split = attended.reshape(local_blocks, n_dp, piece, local_width).transpose(1, 0, 2, 3)
+    split = gather_attend(
+        out_weight, context, residual, cid=10, layout=(n_dp, local_blocks, BLK // n_dp, local_width)
+    )
+
     pieces, mine = spread_select(chosen_blocks.reshape(-1), split, cid=0)
     w_gate = gate_weight[0]
     w_up = up_weight[0]

time: 182 us -> 180 us (0.989)
  local copies, waits for them, and re-layouts: 7.5 us -> 5.63 us
    reshape x1 -> x0, local copies, waits for them, and re-layouts: 1.89 us -> none  [body(): attended.reshape(local_blocks, n_dp, piece, local_width)]
where the time goes in v17:
time: 180 us; the launch traced here: 179 us
  Pallas kernels  171 us (95%)
  local copies, waits for them, and re-layouts  5.63 us (3%)
  other arithmetic  2.59 us (1%)
    pallas_call x1, Pallas kernels, gather_gate(): pl.pallas_call(functools.partial(_gather_gate_kernel, side), out_shape=ja...  34.3 us
    pallas_call x1, Pallas kernels, down_scatter(): pl.pallas_call(functools.partial(_down_scatter_kernel, side), out_shape=[...  32.3 us
    pallas_call x1, Pallas kernels, gather_attend(): pl.pallas_call(functools.partial(_gather_attend_kernel, side), out_shape=...  32.2 us
    pallas_call x2, Pallas kernels, dp_route(): pl.pallas_call(functools.partial(_route_kernel, tuple(strides), side, gat...  23 us
    pallas_call x1, Pallas kernels, spread_select(): pl.pallas_call(functools.partial(_spread_kernel, n_dp, n_expert), out_sha...  19.6 us
    pallas_call x1, Pallas kernels, reduce_scatter_2d(): pl.pallas_call(functools.partial(_finish_kernel, side, n_expert), out_sha...  15.8 us
    pallas_call x1, Pallas kernels, dp_exchange(): pl.pallas_call(functools.partial(_exchange_kernel, n, gather, axis), out_...  13.5 us

profile of v17, /device:TPU:24, one launch (start us, length us, event | category | flops | bytes accessed | tf_op | source)
XLA Modules:
  0.0 179.3 jit_solution(1108727958036487577)
XLA Ops:
  0.0 12.2 %shard_map.91 = (bf16[4,256,256]{2,1,0:T(8,128)(2,1)}, bf16[4,256,256]{2,1,0:T(8,128)(2,1)}) custom-call(bf16[256,512]{1,0:T(8,128)(2,1)} %refs_1_.1, bf16[256,512]{1,0:T(8,128)(2,1)} %refs_1_.1), custom_call_target="tpu_custom_call" | custom-call | tf_op jit(solution)/shard_map/pallas_call | solution.py:113
  12.2 32.2 %shard_map.92.split_ref = bf16[16,4,8,512]{3,2,1,0:T(8,128)(2,1)} custom-call(bf16[4,256,256]{2,1,0:T(8,128)(2,1)} %get-tuple-element.13.a_ref, bf16[4,256,256]{2,1,0:T(8,128)(2,1)} %get-tuple-element.14.b_ref, bf16[512,4096]{1,0:T(8,128)(2,1)} %ctx_ref.1, bf16[512,512]{1,0:T(8,128)(2,1)} %res_ref.1), custom_call_target="tpu_custom_call" | custom-call | tf_op jit(solution)/shard_map/pallas_call | solution.py:504
  44.4 0.0 copy-done.2
  44.4 0.1 copy.12
  44.5 0.7 reshape.99.chosen_ref
  45.2 19.6 %shard_map.93 = (bf16[64,8,512]{2,1,0:T(8,128)(2,1)}, bf16[32,4096]{1,0:T(8,128)(2,1)}) custom-call(s32[32]{0:T(128)} %reshape.99.chosen_ref, bf16[16,4,8,512]{3,2,1,0:T(8,128)(2,1)} %shard_map.92.split_ref), custom_call_target="tpu_custom_call" | custom-call | tf_op jit(solution)/shard_map/pallas_call | solution.py:592
  64.8 10.8 %shard_map.94 = (bf16[4,32,2048]{2,1,0:T(8,128)(2,1)}, bf16[4,32,2048]{2,1,0:T(8,128)(2,1)}) custom-call(bf16[32,4096]{1,0:T(8,128)(2,1)} %get-tuple-element.16.refs_0_.refs_1_, bf16[32,4096]{1,0:T(8,128)(2,1)} %get-tuple-element.16.refs_0_.refs_1_), custom_call_target="tpu_custom_call" | custom-call | tf_op jit(solution)/shard_map/pallas_call | solution.py:113
  75.6 0.0 copy-start.3
  75.6 0.0 copy-start.4
  75.6 34.3 %shard_map.95.hidden_ref = bf16[512,512]{1,0:T(8,128)(2,1)} custom-call(bf16[4,32,2048]{2,1,0:T(8,128)(2,1)} %get-tuple-element.17.a_ref, bf16[4,32,2048]{2,1,0:T(8,128)(2,1)} %get-tuple-element.18.b_ref, bf16[4096,512]{1,0:T(8,128)(2,1)} %bitcast.14, bf16[4096,512]{1,0:T(8,128)(2,1)} %bitcast.15), custom_call_target="tpu_custom_call" | custom-call | tf_op jit(solution)/shard_map/pallas_call | solution.py:403
  109.9 0.5 broadcast.99
  110.5 0.7 reduce.3
  111.1 0.1 reshape_squeeze.3
  111.2 0.1 reshape.105
  111.4 0.6 fusion.8
  112.0 1.3 fusion.6.scale_ref
  113.3 32.3 %shard_map.96 = (bf16[4,32,2048]{2,1,0:T(8,128)(2,1)}, bf16[4,32,2048]{2,1,0:T(8,128)(2,1)}) custom-call(bf16[512,512]{1,0:T(8,128)(2,1)} %shard_map.95.hidden_ref, bf16[512,4096]{1,0:T(8,128)(2,1)} %bitcast.13, f32[512,1]{1,0:T(8,128)} %fusion.6.scale_ref), custom_call_target="tpu_custom_call" | custom-call | tf_op jit(solution)/shard_map/pallas_call | solution.py:268
  145.6 15.8 %shard_map.97 = bf16[8,32,512]{2,1,0:T(8,128)(2,1)} custom-call(bf16[4,32,2048]{2,1,0:T(8,128)(2,1)} %get-tuple-element.19.a_ref, bf16[4,32,2048]{2,1,0:T(8,128)(2,1)} %get-tuple-element.20.b_ref), custom_call_target="tpu_custom_call" | custom-call | tf_op jit(solution)/shard_map/pallas_call | solution.py:292
  161.4 1.1 reshape.101
  162.5 0.2 copy.16
  162.7 0.3 fusion
  163.0 1.0 copy.17
  164.0 13.5 %shard_map.98 = bf16[16,4,8,512]{3,2,1,0:T(8,128)(2,1)} custom-call(bf16[16,4,8,512]{3,2,1,0:T(8,128)(2,1)} %bitcast.17), custom_call_target="tpu_custom_call" | custom-call | tf_op jit(solution)/shard_map/pallas_call | solution.py:44
  177.5 1.9 %copy.15 = bf16[4,16,8,512]{3,2,1,0:T(8,128)(2,1)} copy(bf16[4,16,8,512]{3,2,0,1:T(8,128)(2,1)} %bitcast.18) | data formatting | bytes 1048576 | tf_op jit(solution)/shard_map/transpose | solution.py:659
  (8 shorter events, 0.0 us)
Async XLA Ops:
  0.0 44.4 %copy-start.2 = (s32[8,4]{0,1:T(4,128)S(1)}, s32[8,4]{0,1:T(4,128)}, u32[]{:S(2)}) copy-start(s32[8,4]{0,1:T(4,128)} %param.16) | copy-start | bytes 388
  75.6 34.9 %copy-start.3 = (f32[1,512]{1,0:T(1,128)S(1)}, f32[1,512]{1,0:T(1,128)}, u32[]{:S(2)}) copy-start(f32[1,512]{1,0:T(1,128)} %param.15) | copy-start | bytes 6148
  75.6 35.8 %copy-start.4 = (s32[8]{0:T(128)S(1)}, s32[8]{0:T(128)}, u32[]{:S(2)}) copy-start(s32[8]{0:T(128)} %param.17) | copy-start | bytes 100
  109.9 52.6 %copy-start = (bf16[64,8,512]{2,1,0:T(8,128)(2,1)S(1)}, bf16[64,8,512]{2,1,0:T(8,128)(2,1)}, u32[]{:S(2)}) copy-start(bf16[64,8,512]{2,1,0:T(8,128)(2,1)} %get-tuple-element.15) | copy-start | bytes 1572868
  113.3 49.4 %copy-start.1 = (s32[32]{0:T(128)S(1)}, s32[32]{0:T(128)}, u32[]{:S(2)}) copy-start(s32[32]{0:T(128)} %reshape.99.chosen_ref) | copy-start | bytes 388

commit v18 on v17

--- a/solution.py
+++ b/solution.py
@@ -649,11 +649,13 @@
     halves = down_scatter(hidden, w_down, scale[:, None], cid=1)
 
     outs = reduce_scatter_2d(halves, cid=2)
-    outs = outs.reshape(n_expert * CAP, piece * local_width)
-
-    selector = chosen_blocks.reshape(-1)[None, :] == jnp.arange(n_blocks)[:, None]
-    added = jnp.dot(selector.astype(jnp.bfloat16), outs, preferred_element_type=jnp.float32)
-    mixed = pieces.reshape(n_blocks, piece * local_width).astype(jnp.float32) + added
+    outs = outs.reshape(n_expert, CAP, piece, local_width)
+
+    selector = chosen_blocks[None, :, :] == jnp.arange(n_blocks)[:, None, None]
+    added = jnp.einsum(
+        "bes,esrf->brf", selector.astype(jnp.bfloat16), outs, preferred_element_type=jnp.float32
+    )
+    mixed = pieces.astype(jnp.float32) + added
     mixed = mixed.astype(jnp.bfloat16).reshape(n_dp, local_blocks, piece, local_width)
     back = dp_exchange(mixed, gather=False, cid=3)
     return back.transpose(1, 0, 2, 3).reshape(local_tokens, local_width)

time: 180 us -> 182 us (1.011)
  other arithmetic: 2.59 us -> 5.32 us
where the time goes in v18:
time: 182 us
  Pallas kernels  171 us (94%)
  other arithmetic  5.32 us (3%)
  local copies, waits for them, and re-layouts  4.05 us (2%)
    pallas_call x1, Pallas kernels, gather_gate(): pl.pallas_call(functools.partial(_gather_gate_kernel, side), out_shape=ja...  34.3 us
    pallas_call x1, Pallas kernels, down_scatter(): pl.pallas_call(functools.partial(_down_scatter_kernel, side), out_shape=[...  32.4 us
    pallas_call x1, Pallas kernels, gather_attend(): pl.pallas_call(functools.partial(_gather_attend_kernel, side), out_shape=...  32.2 us
    pallas_call x2, Pallas kernels, dp_route(): pl.pallas_call(functools.partial(_route_kernel, tuple(strides), side, gat...  23 us
    pallas_call x1, Pallas kernels, spread_select(): pl.pallas_call(functools.partial(_spread_kernel, n_dp, n_expert), out_sha...  19.7 us
    pallas_call x1, Pallas kernels, reduce_scatter_2d(): pl.pallas_call(functools.partial(_finish_kernel, side, n_expert), out_sha...  15.8 us
    pallas_call x1, Pallas kernels, dp_exchange(): pl.pallas_call(functools.partial(_exchange_kernel, n, gather, axis), out_...  13.5 us

profile of v18, /device:TPU:24, one launch (start us, length us, event | category | flops | bytes accessed | tf_op | source)
XLA Modules:
  0.0 181.8 jit_solution(13952256329575318969)
XLA Ops:
  0.0 1.3 fusion.11
  1.3 0.5 broadcast.100
  1.8 1.3 reduce.3
  3.1 0.8 copy.14
  3.9 0.7 reshape.96.chosen_ref
  4.6 0.1 reshape_squeeze.3
  4.7 0.1 reshape.103
  4.8 1.3 fusion.7.scale_ref
  6.1 12.2 %shard_map.91 = (bf16[4,256,256]{2,1,0:T(8,128)(2,1)}, bf16[4,256,256]{2,1,0:T(8,128)(2,1)}) custom-call(bf16[256,512]{1,0:T(8,128)(2,1)} %refs_1_.1, bf16[256,512]{1,0:T(8,128)(2,1)} %refs_1_.1), custom_call_target="tpu_custom_call" | custom-call | tf_op jit(solution)/shard_map/pallas_call | solution.py:113
  18.3 32.2 %shard_map.92.split_ref = bf16[16,4,8,512]{3,2,1,0:T(8,128)(2,1)} custom-call(bf16[4,256,256]{2,1,0:T(8,128)(2,1)} %get-tuple-element.13.a_ref, bf16[4,256,256]{2,1,0:T(8,128)(2,1)} %get-tuple-element.14.b_ref, bf16[512,4096]{1,0:T(8,128)(2,1)} %ctx_ref.1, bf16[512,512]{1,0:T(8,128)(2,1)} %res_ref.1), custom_call_target="tpu_custom_call" | custom-call | tf_op jit(solution)/shard_map/pallas_call | solution.py:504
  50.6 19.7 %shard_map.93 = (bf16[64,8,512]{2,1,0:T(8,128)(2,1)}, bf16[32,4096]{1,0:T(8,128)(2,1)}) custom-call(s32[32]{0:T(128)} %reshape.96.chosen_ref, bf16[16,4,8,512]{3,2,1,0:T(8,128)(2,1)} %shard_map.92.split_ref), custom_call_target="tpu_custom_call" | custom-call | tf_op jit(solution)/shard_map/pallas_call | solution.py:592
  70.3 10.8 %shard_map.94 = (bf16[4,32,2048]{2,1,0:T(8,128)(2,1)}, bf16[4,32,2048]{2,1,0:T(8,128)(2,1)}) custom-call(bf16[32,4096]{1,0:T(8,128)(2,1)} %get-tuple-element.16.refs_0_.refs_1_, bf16[32,4096]{1,0:T(8,128)(2,1)} %get-tuple-element.16.refs_0_.refs_1_), custom_call_target="tpu_custom_call" | custom-call | tf_op jit(solution)/shard_map/pallas_call | solution.py:113
  81.1 34.3 %shard_map.95.hidden_ref = bf16[512,512]{1,0:T(8,128)(2,1)} custom-call(bf16[4,32,2048]{2,1,0:T(8,128)(2,1)} %get-tuple-element.17.a_ref, bf16[4,32,2048]{2,1,0:T(8,128)(2,1)} %get-tuple-element.18.b_ref, bf16[4096,512]{1,0:T(8,128)(2,1)} %bitcast.15, bf16[4096,512]{1,0:T(8,128)(2,1)} %bitcast.16), custom_call_target="tpu_custom_call" | custom-call | tf_op jit(solution)/shard_map/pallas_call | solution.py:403
  115.4 0.0 copy-start.1
  115.4 0.0 copy-start
  115.4 32.4 %shard_map.96 = (bf16[4,32,2048]{2,1,0:T(8,128)(2,1)}, bf16[4,32,2048]{2,1,0:T(8,128)(2,1)}) custom-call(bf16[512,512]{1,0:T(8,128)(2,1)} %shard_map.95.hidden_ref, bf16[512,4096]{1,0:T(8,128)(2,1)} %bitcast.14, f32[512,1]{1,0:T(8,128)} %fusion.7.scale_ref), custom_call_target="tpu_custom_call" | custom-call | tf_op jit(solution)/shard_map/pallas_call | solution.py:268
  147.9 15.8 %shard_map.97 = bf16[8,32,512]{2,1,0:T(8,128)(2,1)} custom-call(bf16[4,32,2048]{2,1,0:T(8,128)(2,1)} %get-tuple-element.19.a_ref, bf16[4,32,2048]{2,1,0:T(8,128)(2,1)} %get-tuple-element.20.b_ref), custom_call_target="tpu_custom_call" | custom-call | tf_op jit(solution)/shard_map/pallas_call | solution.py:292
  163.7 0.0 copy-done.1
  163.7 1.4 convolution_bitcast_fusion
  165.0 0.0 copy-done
  165.0 1.4 fusion
  166.4 13.5 %shard_map.98 = bf16[16,4,8,512]{3,2,1,0:T(8,128)(2,1)} custom-call(bf16[16,4,8,512]{3,2,1,0:T(8,128)(2,1)} %bitcast.18), custom_call_target="tpu_custom_call" | custom-call | tf_op jit(solution)/shard_map/pallas_call | solution.py:44
  179.9 1.9 %copy.19 = bf16[4,16,8,512]{3,2,1,0:T(8,128)(2,1)} copy(bf16[4,16,8,512]{3,2,0,1:T(8,128)(2,1)} %bitcast.17) | data formatting | bytes 1048576 | tf_op jit(solution)/shard_map/transpose | solution.py:661
  (1 shorter events, 0.0 us)
Async XLA Ops:
  115.4 48.3 %copy-start.1 = (s32[8,4]{0,1:T(4,128)S(1)}, s32[8,4]{0,1:T(4,128)}, u32[]{:S(2)}) copy-start(s32[8,4]{0,1:T(4,128)} %param.16) | copy-start | bytes 388
  115.4 49.6 %copy-start = (bf16[64,8,512]{2,1,0:T(8,128)(2,1)S(1)}, bf16[64,8,512]{2,1,0:T(8,128)(2,1)}, u32[]{:S(2)}) copy-start(bf16[64,8,512]{2,1,0:T(8,128)(2,1)} %get-tuple-element.15) | copy-start | bytes 1572868

commit v19 on v17

--- a/solution.py
+++ b/solution.py
@@ -561,7 +561,7 @@
     width = held.shape[2]
     for e in range(n_expert):
         for s in range(CAP):
-            outgoing[e, s * rows:(s + 1) * rows] = held[chosen_ref[e * CAP + s]]
+            outgoing[e, s * rows:(s + 1) * rows] = held[chosen_ref[e, s]]
     columns = pl.ds(pl.multiple_of(mine_e * width, width), width)
     local = pltpu.make_async_copy(outgoing.at[mine_e], mine_ref.at[:, columns], local_sems.at[2])
     local.start()
@@ -635,7 +635,7 @@
         out_weight, context, residual, cid=10, layout=(n_dp, local_blocks, BLK // n_dp, local_width)
     )
 
-    pieces, mine = spread_select(chosen_blocks.reshape(-1), split, cid=0)
+    pieces, mine = spread_select(chosen_blocks, split, cid=0)
     w_gate = gate_weight[0]
     w_up = up_weight[0]
     w_down = down_weight[0]

time: 180 us -> 180 us (level)
  no operation moved by 1% of the time
where the time goes in v19:
time: 180 us; the launch traced here: 179 us
  Pallas kernels  171 us (95%)
  local copies, waits for them, and re-layouts  5.62 us (3%)
  other arithmetic  2.59 us (1%)
    pallas_call x1, Pallas kernels, gather_gate(): pl.pallas_call(functools.partial(_gather_gate_kernel, side), out_shape=ja...  34.3 us
    pallas_call x1, Pallas kernels, down_scatter(): pl.pallas_call(functools.partial(_down_scatter_kernel, side), out_shape=[...  32.3 us
    pallas_call x1, Pallas kernels, gather_attend(): pl.pallas_call(functools.partial(_gather_attend_kernel, side), out_shape=...  32.2 us
    pallas_call x2, Pallas kernels, dp_route(): pl.pallas_call(functools.partial(_route_kernel, tuple(strides), side, gat...  23 us
    pallas_call x1, Pallas kernels, spread_select(): pl.pallas_call(functools.partial(_spread_kernel, n_dp, n_expert), out_sha...  19.7 us
    pallas_call x1, Pallas kernels, reduce_scatter_2d(): pl.pallas_call(functools.partial(_finish_kernel, side, n_expert), out_sha...  15.8 us
    pallas_call x1, Pallas kernels, dp_exchange(): pl.pallas_call(functools.partial(_exchange_kernel, n, gather, axis), out_...  13.5 us

profile of v19, /device:TPU:24, one launch (start us, length us, event | category | flops | bytes accessed | tf_op | source)
XLA Modules:
  0.0 179.4 jit_solution(5674983087549517408)
XLA Ops:
  0.0 12.2 %shard_map.91 = (bf16[4,256,256]{2,1,0:T(8,128)(2,1)}, bf16[4,256,256]{2,1,0:T(8,128)(2,1)}) custom-call(bf16[256,512]{1,0:T(8,128)(2,1)} %refs_1_.1, bf16[256,512]{1,0:T(8,128)(2,1)} %refs_1_.1), custom_call_target="tpu_custom_call" | custom-call | tf_op jit(solution)/shard_map/pallas_call | solution.py:113
  12.2 32.2 %shard_map.92.split_ref = bf16[16,4,8,512]{3,2,1,0:T(8,128)(2,1)} custom-call(bf16[4,256,256]{2,1,0:T(8,128)(2,1)} %get-tuple-element.13.a_ref, bf16[4,256,256]{2,1,0:T(8,128)(2,1)} %get-tuple-element.14.b_ref, bf16[512,4096]{1,0:T(8,128)(2,1)} %ctx_ref.1, bf16[512,512]{1,0:T(8,128)(2,1)} %res_ref.1), custom_call_target="tpu_custom_call" | custom-call | tf_op jit(solution)/shard_map/pallas_call | solution.py:504
  44.4 0.0 copy-done.2
  44.4 0.7 copy.13.chosen_ref
  45.1 19.7 %shard_map.93 = (bf16[64,8,512]{2,1,0:T(8,128)(2,1)}, bf16[32,4096]{1,0:T(8,128)(2,1)}) custom-call(s32[8,4]{1,0:T(8,128)} %copy.13.chosen_ref, bf16[16,4,8,512]{3,2,1,0:T(8,128)(2,1)} %shard_map.92.split_ref), custom_call_target="tpu_custom_call" | custom-call | tf_op jit(solution)/shard_map/pallas_call | solution.py:592
  64.8 10.8 %shard_map.94 = (bf16[4,32,2048]{2,1,0:T(8,128)(2,1)}, bf16[4,32,2048]{2,1,0:T(8,128)(2,1)}) custom-call(bf16[32,4096]{1,0:T(8,128)(2,1)} %get-tuple-element.16.refs_0_.refs_1_, bf16[32,4096]{1,0:T(8,128)(2,1)} %get-tuple-element.16.refs_0_.refs_1_), custom_call_target="tpu_custom_call" | custom-call | tf_op jit(solution)/shard_map/pallas_call | solution.py:113
  75.6 0.0 copy-start.3
  75.6 0.0 copy-start.4
  75.6 34.3 %shard_map.95.hidden_ref = bf16[512,512]{1,0:T(8,128)(2,1)} custom-call(bf16[4,32,2048]{2,1,0:T(8,128)(2,1)} %get-tuple-element.17.a_ref, bf16[4,32,2048]{2,1,0:T(8,128)(2,1)} %get-tuple-element.18.b_ref, bf16[4096,512]{1,0:T(8,128)(2,1)} %bitcast.14, bf16[4096,512]{1,0:T(8,128)(2,1)} %bitcast.15), custom_call_target="tpu_custom_call" | custom-call | tf_op jit(solution)/shard_map/pallas_call | solution.py:403
  109.9 0.5 broadcast.99
  110.4 0.7 reduce.3
  111.1 0.1 reshape_squeeze.3
  111.2 0.1 reshape.101
  111.4 0.6 fusion.8
  112.0 1.3 fusion.6.scale_ref
  113.3 32.3 %shard_map.96 = (bf16[4,32,2048]{2,1,0:T(8,128)(2,1)}, bf16[4,32,2048]{2,1,0:T(8,128)(2,1)}) custom-call(bf16[512,512]{1,0:T(8,128)(2,1)} %shard_map.95.hidden_ref, bf16[512,4096]{1,0:T(8,128)(2,1)} %bitcast.13, f32[512,1]{1,0:T(8,128)} %fusion.6.scale_ref), custom_call_target="tpu_custom_call" | custom-call | tf_op jit(solution)/shard_map/pallas_call | solution.py:268
  145.6 15.8 %shard_map.97 = bf16[8,32,512]{2,1,0:T(8,128)(2,1)} custom-call(bf16[4,32,2048]{2,1,0:T(8,128)(2,1)} %get-tuple-element.19.a_ref, bf16[4,32,2048]{2,1,0:T(8,128)(2,1)} %get-tuple-element.20.b_ref), custom_call_target="tpu_custom_call" | custom-call | tf_op jit(solution)/shard_map/pallas_call | solution.py:292
  161.4 1.1 reshape.97
  162.5 0.2 copy.18
  162.7 0.1 eq.23
  162.8 0.3 fusion
  163.1 1.0 copy.19
  164.0 13.5 %shard_map.98 = bf16[16,4,8,512]{3,2,1,0:T(8,128)(2,1)} custom-call(bf16[16,4,8,512]{3,2,1,0:T(8,128)(2,1)} %bitcast.17), custom_call_target="tpu_custom_call" | custom-call | tf_op jit(solution)/shard_map/pallas_call | solution.py:44
  177.5 1.9 %copy.17 = bf16[4,16,8,512]{3,2,1,0:T(8,128)(2,1)} copy(bf16[4,16,8,512]{3,2,0,1:T(8,128)(2,1)} %bitcast.18) | data formatting | bytes 1048576 | tf_op jit(solution)/shard_map/transpose | solution.py:659
  (8 shorter events, 0.0 us)
Async XLA Ops:
  0.0 44.4 %copy-start.2 = (s32[8,4]{0,1:T(4,128)S(1)}, s32[8,4]{0,1:T(4,128)}, u32[]{:S(2)}) copy-start(s32[8,4]{0,1:T(4,128)} %param.16) | copy-start | bytes 388
  75.6 34.9 %copy-start.3 = (f32[1,512]{1,0:T(1,128)S(1)}, f32[1,512]{1,0:T(1,128)}, u32[]{:S(2)}) copy-start(f32[1,512]{1,0:T(1,128)} %param.15) | copy-start | bytes 6148
  75.6 35.8 %copy-start.4 = (s32[8]{0:T(128)S(1)}, s32[8]{0:T(128)}, u32[]{:S(2)}) copy-start(s32[8]{0:T(128)} %param.17) | copy-start | bytes 100
  109.9 52.6 %copy-start = (bf16[64,8,512]{2,1,0:T(8,128)(2,1)S(1)}, bf16[64,8,512]{2,1,0:T(8,128)(2,1)}, u32[]{:S(2)}) copy-start(bf16[64,8,512]{2,1,0:T(8,128)(2,1)} %get-tuple-element.15) | copy-start | bytes 1572868
  113.3 49.4 %copy-start.1 = (s32[8,4]{1,0:T(8,128)S(1)}, s32[8,4]{1,0:T(8,128)}, u32[]{:S(2)}) copy-start(s32[8,4]{1,0:T(8,128)} %copy.13.chosen_ref) | copy-start | bytes 388

commit v20 on v17

--- a/solution.py
+++ b/solution.py
@@ -194,7 +194,7 @@
         copy.wait()
 
 
-def _down_scatter_kernel(side, hidden_ref, wd_ref, scale_ref, sum_a, sum_b,
+def _down_scatter_kernel(side, counts_ref, hidden_ref, wd_ref, scale_ref, sum_a, sum_b,
                          send_a, send_b, got_a, got_b, send_sems, recv_sems):
     me = lax.axis_index("dp")
     mesh_id = pl.DeviceIdType.MESH
@@ -225,12 +225,16 @@
             recv_sem=recv_sems.at[1, k - 1], device_id={"dp": base_x + x * side}, device_id_type=mesh_id,
         )
 
+    count = counts_ref[lax.axis_index("expert")]
+    rows_per_slot = rows // CAP
     sends = []
     for k in list(range(1, side)) + [0]:
         x = lax.rem(my_x + k, side)
         at = pl.ds(pl.multiple_of(x * chunk, chunk), chunk)
         part = jnp.dot(hidden_ref[at], wd_ref[...], preferred_element_type=jnp.float32)
-        part = (part * scale_ref[at]).astype(send_a.dtype)
+        slot = lax.rem(lax.broadcasted_iota(jnp.int32, (chunk, 1), 0) // rows_per_slot, CAP)
+        live = jnp.where(slot < count, scale_ref[at], 0.0)
+        part = (part * live).astype(send_a.dtype)
         for y in range(side):
             send_a[y, x] = part[y * rows:(y + 1) * rows, :half]
             send_b[x, y] = part[y * rows:(y + 1) * rows, half:]
@@ -259,7 +263,7 @@
         copy.wait_send()
 
 
-def down_scatter(hidden, w_down, scale, cid):
+def down_scatter(counts, hidden, w_down, scale, cid):
     side = 4
     rows = hidden.shape[0] // (side * side)
     half = w_down.shape[1] // 2
@@ -268,7 +272,7 @@
     return pl.pallas_call(
         functools.partial(_down_scatter_kernel, side),
         out_shape=[jax.ShapeDtypeStruct((side, rows, half), jnp.bfloat16)] * 2,
-        in_specs=[vmem] * 3,
+        in_specs=[pl.BlockSpec(memory_space=pltpu.SMEM)] + [vmem] * 3,
         out_specs=[vmem] * 2,
         scratch_shapes=[
             pltpu.VMEM(slab, jnp.bfloat16),
@@ -279,7 +283,7 @@
             pltpu.SemaphoreType.DMA((2, side - 1)),
         ],
         compiler_params=pltpu.CompilerParams(collective_id=cid, has_side_effects=True),
-    )(hidden, w_down, scale)
+    )(counts, hidden, w_down, scale)
 
 
 def reduce_scatter_2d(part, cid):
@@ -640,13 +644,10 @@
     w_up = up_weight[0]
     w_down = down_weight[0]
     gate_row = gate_values[0]
-    my_count = jnp.sum(jnp.where(jnp.arange(n_expert) == my_expert, block_counts, 0))
-    row_slot = (jnp.arange(CAP * BLK) // piece) % CAP
-    gate_perm = gate_row.reshape(CAP, n_dp, piece).transpose(1, 0, 2).reshape(-1)
-    scale = jnp.where(row_slot < my_count, gate_perm, jnp.zeros_like(gate_perm))
+    scale = gate_row.reshape(CAP, n_dp, piece).transpose(1, 0, 2).reshape(-1)
 
     hidden = gather_gate(mine, w_gate, w_up, cid=20)
-    halves = down_scatter(hidden, w_down, scale[:, None], cid=1)
+    halves = down_scatter(block_counts, hidden, w_down, scale[:, None], cid=1)
 
     outs = reduce_scatter_2d(halves, cid=2)
     outs = outs.reshape(n_expert * CAP, piece * local_width)

time: 180 us -> 179 us (level)
  other arithmetic: 2.59 us -> 0.66 us
where the time goes in v20:
time: 179 us; the launch traced here: 178 us
  Pallas kernels  171 us (96%)
  local copies, waits for them, and re-layouts  6.32 us (4%)
    pallas_call x1, Pallas kernels, gather_gate(): pl.pallas_call(functools.partial(_gather_gate_kernel, side), out_shape=ja...  34.3 us
    pallas_call x1, Pallas kernels, down_scatter(): pl.pallas_call(functools.partial(_down_scatter_kernel, side), out_shape=[...  32.4 us
    pallas_call x1, Pallas kernels, gather_attend(): pl.pallas_call(functools.partial(_gather_attend_kernel, side), out_shape=...  32.2 us
    pallas_call x2, Pallas kernels, dp_route(): pl.pallas_call(functools.partial(_route_kernel, tuple(strides), side, gat...  23 us
    pallas_call x1, Pallas kernels, spread_select(): pl.pallas_call(functools.partial(_spread_kernel, n_dp, n_expert), out_sha...  19.6 us
    pallas_call x1, Pallas kernels, reduce_scatter_2d(): pl.pallas_call(functools.partial(_finish_kernel, side, n_expert), out_sha...  15.8 us
    pallas_call x1, Pallas kernels, dp_exchange(): pl.pallas_call(functools.partial(_exchange_kernel, n, gather, axis), out_...  13.5 us

profile of v20, /device:TPU:24, one launch (start us, length us, event | category | flops | bytes accessed | tf_op | source)
XLA Modules:
  0.0 178.2 jit_solution(3256758632329878300)
XLA Ops:
  0.0 12.2 %shard_map.91 = (bf16[4,256,256]{2,1,0:T(8,128)(2,1)}, bf16[4,256,256]{2,1,0:T(8,128)(2,1)}) custom-call(bf16[256,512]{1,0:T(8,128)(2,1)} %refs_1_.1, bf16[256,512]{1,0:T(8,128)(2,1)} %refs_1_.1), custom_call_target="tpu_custom_call" | custom-call | tf_op jit(solution)/shard_map/pallas_call | solution.py:113
  12.2 32.2 %shard_map.92.split_ref = bf16[16,4,8,512]{3,2,1,0:T(8,128)(2,1)} custom-call(bf16[4,256,256]{2,1,0:T(8,128)(2,1)} %get-tuple-element.13.a_ref, bf16[4,256,256]{2,1,0:T(8,128)(2,1)} %get-tuple-element.14.b_ref, bf16[512,4096]{1,0:T(8,128)(2,1)} %ctx_ref.1, bf16[512,512]{1,0:T(8,128)(2,1)} %res_ref.1), custom_call_target="tpu_custom_call" | custom-call | tf_op jit(solution)/shard_map/pallas_call | solution.py:508
  44.4 0.0 copy-done.2
  44.4 0.1 copy.12
  44.5 0.7 reshape.16.chosen_ref
  45.2 19.6 %shard_map.93 = (bf16[64,8,512]{2,1,0:T(8,128)(2,1)}, bf16[32,4096]{1,0:T(8,128)(2,1)}) custom-call(s32[32]{0:T(128)} %reshape.16.chosen_ref, bf16[16,4,8,512]{3,2,1,0:T(8,128)(2,1)} %shard_map.92.split_ref), custom_call_target="tpu_custom_call" | custom-call | tf_op jit(solution)/shard_map/pallas_call | solution.py:596
  64.8 10.8 %shard_map.94 = (bf16[4,32,2048]{2,1,0:T(8,128)(2,1)}, bf16[4,32,2048]{2,1,0:T(8,128)(2,1)}) custom-call(bf16[32,4096]{1,0:T(8,128)(2,1)} %get-tuple-element.16.refs_0_.refs_1_, bf16[32,4096]{1,0:T(8,128)(2,1)} %get-tuple-element.16.refs_0_.refs_1_), custom_call_target="tpu_custom_call" | custom-call | tf_op jit(solution)/shard_map/pallas_call | solution.py:113
  75.6 0.0 copy-start.3
  75.6 34.3 %shard_map.95.hidden_ref = bf16[512,512]{1,0:T(8,128)(2,1)} custom-call(bf16[4,32,2048]{2,1,0:T(8,128)(2,1)} %get-tuple-element.17.a_ref, bf16[4,32,2048]{2,1,0:T(8,128)(2,1)} %get-tuple-element.18.b_ref, bf16[4096,512]{1,0:T(8,128)(2,1)} %bitcast.14, bf16[4096,512]{1,0:T(8,128)(2,1)} %bitcast.15), custom_call_target="tpu_custom_call" | custom-call | tf_op jit(solution)/shard_map/pallas_call | solution.py:407
  109.9 0.0 copy-start
  109.9 0.5 broadcast.3
  110.5 0.0 copy-done.3
  110.5 0.7 reduce.3
  111.1 0.1 reshape_squeeze.3
  111.2 0.8 broadcast_in_dim_reshape.5.scale_ref
  112.1 32.4 %shard_map.96 = (bf16[4,32,2048]{2,1,0:T(8,128)(2,1)}, bf16[4,32,2048]{2,1,0:T(8,128)(2,1)}) custom-call(s32[8]{0:T(128)} %counts_ref.1, bf16[512,512]{1,0:T(8,128)(2,1)} %shard_map.95.hidden_ref, bf16[512,4096]{1,0:T(8,128)(2,1)} %bitcast.13, f32[512,1]{1,0:T(8,128)} %broadcast_in_dim_reshape.5.scale_ref), custom_call_target="tpu_custom_call" | custom-call | tf_op jit(solution)/shard_map/pallas_call | solution.py:272
  144.5 15.8 %shard_map.97 = bf16[8,32,512]{2,1,0:T(8,128)(2,1)} custom-call(bf16[4,32,2048]{2,1,0:T(8,128)(2,1)} %get-tuple-element.19.a_ref, bf16[4,32,2048]{2,1,0:T(8,128)(2,1)} %get-tuple-element.20.b_ref), custom_call_target="tpu_custom_call" | custom-call | tf_op jit(solution)/shard_map/pallas_call | solution.py:296
  160.3 1.1 reshape.17
  161.4 0.2 copy.16
  161.6 0.0 copy-done.1
  161.6 0.3 fusion
  161.8 1.0 copy.17
  162.8 13.5 %shard_map.98 = bf16[16,4,8,512]{3,2,1,0:T(8,128)(2,1)} custom-call(bf16[16,4,8,512]{3,2,1,0:T(8,128)(2,1)} %bitcast.17), custom_call_target="tpu_custom_call" | custom-call | tf_op jit(solution)/shard_map/pallas_call | solution.py:44
  176.3 1.9 %copy.15 = bf16[4,16,8,512]{3,2,1,0:T(8,128)(2,1)} copy(bf16[4,16,8,512]{3,2,0,1:T(8,128)(2,1)} %bitcast.18) | data formatting | bytes 1048576 | tf_op jit(solution)/shard_map/transpose | solution.py:660
  (4 shorter events, 0.0 us)
Async XLA Ops:
  0.0 44.4 %copy-start.2 = (s32[8,4]{0,1:T(4,128)S(1)}, s32[8,4]{0,1:T(4,128)}, u32[]{:S(2)}) copy-start(s32[8,4]{0,1:T(4,128)} %param.16) | copy-start | bytes 388
  75.6 34.9 %copy-start.3 = (f32[1,512]{1,0:T(1,128)S(1)}, f32[1,512]{1,0:T(1,128)}, u32[]{:S(2)}) copy-start(f32[1,512]{1,0:T(1,128)} %param.15) | copy-start | bytes 6148
  109.9 51.4 %copy-start = (bf16[64,8,512]{2,1,0:T(8,128)(2,1)S(1)}, bf16[64,8,512]{2,1,0:T(8,128)(2,1)}, u32[]{:S(2)}) copy-start(bf16[64,8,512]{2,1,0:T(8,128)(2,1)} %get-tuple-element.15) | copy-start | bytes 1572868
  112.1 49.5 %copy-start.1 = (s32[32]{0:T(128)S(1)}, s32[32]{0:T(128)}, u32[]{:S(2)}) copy-start(s32[32]{0:T(128)} %reshape.16.chosen_ref) | copy-start | bytes 388
